TPU v7x, 128 devices: a whole 4x4x4 slice. The times are simulated.
128 devices in a mesh: shard: 4 (over z_hi, core), rep: 32 (over y, x, z_lo).
Axes of the slice: x: 4, y: 4, z: 4 (z_hi: 2, z_lo: 2; z = z_hi * 2 + z_lo), core: 2. Of those that a mesh axis runs over, the one named last changes fastest.
Arguments:
- tokens: bfloat16 [49152, 4608], P(('shard', 'rep')), may hold values from -6 to 6
- norm_gain: float32 [4608], replicated, may hold values from 0.25 to 1.75
- key_grad: bfloat16 [49152, 1024], P(('shard', 'rep')), may hold values from -6 to 6
- key_weight: bfloat16 [4608, 1024], P('shard'), may hold values from -0.09375 to 0.09375
- m_code: bfloat16 [4608, 1024], P('shard'), may hold values from -127 to 127, as said below
- m_exp: int32 [4608, 4], P('shard'), may hold values from 3 to 7
- v_code: bfloat16 [4608, 1024], P('shard'), may hold values from 1 to 255, as said below
- v_exp: int32 [4608, 4], P('shard'), may hold values from 4 to 9
Outputs:
- keys: bfloat16 [49152, 1024], P(('shard', 'rep'))
- token_grad: bfloat16 [49152, 4608], P(('shard', 'rep'))
- adam_step: float32 [4608, 1024], P('shard')
- m_rel: bfloat16 [4608, 1024], P('shard')
- m_scale: float32 [4608, 4], P('shard')
- v_rel: bfloat16 [4608, 1024], P('shard')
- v_scale: float32 [4608, 4], P('shard')
Inputs may be any that keep to these rules, and one draw needn't show every extreme that they name: `m_code`: whole numbers. `v_code`: whole numbers.
All inputs are finite; a program needn't handle non-finite values. Where the computation divides by a largest or mean magnitude, that divisor is 1e-20 or more.
Results may differ from a plain program's by a relative error of at most 0.0099.
Values may be sent and summed in bfloat16 or wider, within the bound.
No kernel may reach another device: no remote copies, remote signals or barrier semaphores. Data moves between devices by JAX's collectives and lax.ppermute only.
A program may use at most 192 MiB of HBM per device.

v0:
```python
import jax
import jax.numpy as jnp
from jax import lax
from jax.experimental import pallas as pl
from jax.experimental.pallas import tpu as pltpu
from jax.sharding import Mesh, PartitionSpec as P


bias_first = 0.9999734386011124
bias_second = 0.0952078528862904

AXES = ("zh", "c", "y", "x", "zl")

D = 4608
KH = 1024
ROWS = 1152
T = 384
RING = (0, 1, 3, 2)
RB, CB = 144, 256


def index_of(zh, c, y, x, zl):
    return (((zh * 2 + c) * 4 + y) * 4 + x) * 2 + zl


def pairs(move):
    out = []
    for zh in range(2):
        for c in range(2):
            for y in range(4):
                for x in range(4):
                    for zl in range(2):
                        to = move(zh, c, y, x, zl)
                        out.append((index_of(zh, c, y, x, zl), index_of(*to)))
    return out


def partner(zh, c, y, x, zl):
    return zh, 1 - c, y, x, zl


def across(zh, c, y, x, zl):
    return 1 - zh, c, y, x, 1 - zl


def zl_partner(zh, c, y, x, zl):
    return zh, c, y, x, 1 - zl


def opposite(zh, c, y, x, zl):
    return 1 - zh, c, y, x, zl


def around(step, second=False):
    def move(zh, c, y, x, zl):
        if (c == 0) != second:
            return zh, c, y, (x + step) % 4, zl
        return zh, c, (y + step) % 4, x, zl

    return move


def send(value, move):
    return lax.ppermute(value, AXES, pairs(move))


def send_ring(value, second):
    return [send(value, around(k, second)) for k in RING[1:]]


def unpack(where):
    w = where[0]
    return w % 2, (w // 2) % 2, (w // 4) % 4, w // 16


def vmem(n):
    return [pl.BlockSpec(memory_space=pltpu.VMEM)] * n


def norm_kernel(where, x_ref, gain_ref, mine_ref, theirs_ref, inv_ref):
    x = x_ref[...].astype(jnp.float32)
    inv = lax.rsqrt(jnp.mean(x * x, axis=1, keepdims=True) + 1e-06)
    inv_ref[...] = inv
    c = unpack(where)[0]
    for half in range(2):
        for out, which in ((mine_ref, c), (theirs_ref, 1 - c)):
            for part in range(ROWS // 128):
                at = (half * 2 + which) * (ROWS // 128) + part
                cols = pl.ds(pl.multiple_of(at * 128, 128), 128)
                value = x_ref[:, cols].astype(jnp.float32) * inv * gain_ref[pl.ds(at, 1), :]
                out[:, half * ROWS + part * 128:half * ROWS + (part + 1) * 128] = value.astype(jnp.bfloat16)


def norm_call(where, tokens, gain):
    tm = 64
    return pl.pallas_call(
        norm_kernel,
        grid_spec=pltpu.PrefetchScalarGridSpec(
            num_scalar_prefetch=1,
            grid=(T // tm,),
            in_specs=[
                pl.BlockSpec((tm, D), lambda i, where: (i, 0)),
                pl.BlockSpec((D // 128, 128), lambda i, where: (0, 0)),
            ],
            out_specs=[
                pl.BlockSpec((tm, D // 2), lambda i, where: (i, 0)),
                pl.BlockSpec((tm, D // 2), lambda i, where: (i, 0)),
                pl.BlockSpec((tm, 1), lambda i, where: (i, 0)),
            ],
        ),
        out_shape=[
            jax.ShapeDtypeStruct((T, D // 2), jnp.bfloat16),
            jax.ShapeDtypeStruct((T, D // 2), jnp.bfloat16),
            jax.ShapeDtypeStruct((T, 1), jnp.float32),
        ],
        cost_estimate=pl.CostEstimate(flops=6 * T * D, bytes_accessed=4 * T * D, transcendentals=T),
        compiler_params=pltpu.CompilerParams(vmem_limit_bytes=16 << 20),
        name="norm",
    )(where, tokens, gain)


def grad_kernel(where, a_ref, b_ref, ka_ref, kb_ref, *rest):
    outs, hold = rest[:4], rest[4]
    dims = (((0,), (0,)), ((), ()))
    acc = lax.dot_general(a_ref[...], ka_ref[...], dims, preferred_element_type=jnp.float32)
    acc += lax.dot_general(b_ref[...], kb_ref[...], dims, preferred_element_type=jnp.float32)
    hold[...] = acc.astype(jnp.bfloat16)
    _, _, pos, other = unpack(where)
    for k in range(4):
        first = lax.rem(pos + k, 4) * (2 * RB)
        for j in range(4):
            o = lax.rem(other + j, 4)
            rows = pl.ds(pl.multiple_of(first + (o // 2) * RB, 16), RB)
            for zl in range(2):
                cols = pl.ds(pl.multiple_of((o % 2) * (2 * CB) + zl * CB, 128), CB)
                outs[k][j, 0, zl] = hold[rows, cols]


def grad_call(where, a, b, ka, kb):
    return pl.pallas_call(
        grad_kernel,
        grid_spec=pltpu.PrefetchScalarGridSpec(
            num_scalar_prefetch=1,
            grid=(2,),
            in_specs=[
                pl.BlockSpec((T, ROWS), lambda i, where: (0, i)),
                pl.BlockSpec((T, ROWS), lambda i, where: (0, i)),
                pl.BlockSpec((T, KH), lambda i, where: (0, 0)),
                pl.BlockSpec((T, KH), lambda i, where: (0, 0)),
            ],
            out_specs=[pl.BlockSpec((4, 1, 2, RB, CB), lambda i, where: (0, i, 0, 0, 0))] * 4,
            scratch_shapes=[pltpu.VMEM((ROWS, KH), jnp.bfloat16)],
        ),
        out_shape=[jax.ShapeDtypeStruct((4, 2, 2, RB, CB), jnp.bfloat16)] * 4,
        cost_estimate=pl.CostEstimate(flops=4 * T * ROWS * 2 * KH, bytes_accessed=10 << 20, transcendentals=0),
        compiler_params=pltpu.CompilerParams(vmem_limit_bytes=26 << 20),
        name="grad",
    )(where, a, b, ka, kb)


def add_up(refs):
    total = refs[0][...].astype(jnp.float32)
    for ref in refs[1:]:
        total += ref[...].astype(jnp.float32)
    return total.astype(jnp.bfloat16)


def first_sum_kernel(*refs):
    for j in range(4):
        refs[4 + j][...] = add_up([ref.at[j] for ref in refs[:4]])


def first_sum(parts):
    return pl.pallas_call(
        first_sum_kernel,
        in_specs=vmem(4),
        out_specs=vmem(4),
        out_shape=[jax.ShapeDtypeStruct((2, 2, RB, CB), jnp.bfloat16)] * 4,
        cost_estimate=pl.CostEstimate(flops=64 * RB * CB, bytes_accessed=6 << 20, transcendentals=0),
        compiler_params=pltpu.CompilerParams(vmem_limit_bytes=16 << 20),
        name="first_sum",
    )(*parts)


def second_sum_kernel(where, *refs):
    zh = unpack(where)[1]
    for out, h in ((refs[4], zh), (refs[5], 1 - zh)):
        out[...] = add_up([ref.at[h] for ref in refs[:4]])


def second_sum(where, parts):
    return pl.pallas_call(
        second_sum_kernel,
        in_specs=[pl.BlockSpec(memory_space=pltpu.SMEM)] + vmem(4),
        out_specs=vmem(2),
        out_shape=[jax.ShapeDtypeStruct((2, RB, CB), jnp.bfloat16)] * 2,
        cost_estimate=pl.CostEstimate(flops=16 * RB * CB, bytes_accessed=2 << 20, transcendentals=0),
        compiler_params=pltpu.CompilerParams(vmem_limit_bytes=8 << 20),
        name="second_sum",
    )(where, *parts)


def total_kernel(own, near, across_z, far, out):
    near_sum = own[...].astype(jnp.float32) + near[...].astype(jnp.float32)
    far_sum = across_z[...].astype(jnp.float32) + far[...].astype(jnp.float32)
    out[...] = (near_sum + far_sum).astype(jnp.bfloat16)


def total_call(*parts):
    return pl.pallas_call(
        total_kernel,
        in_specs=vmem(4),
        out_specs=vmem(1)[0],
        out_shape=jax.ShapeDtypeStruct((2, RB, CB), jnp.bfloat16),
        cost_estimate=pl.CostEstimate(flops=8 * RB * CB, bytes_accessed=1 << 20, transcendentals=0),
        compiler_params=pltpu.CompilerParams(vmem_limit_bytes=8 << 20),
        name="total",
    )(*parts)


def join_kernel(*refs):
    for k, ref in zip(RING, refs[:4]):
        refs[4][k] = ref[...]


def join_call(parts):
    return pl.pallas_call(
        join_kernel,
        in_specs=vmem(4),
        out_specs=vmem(1)[0],
        out_shape=jax.ShapeDtypeStruct((4, 2, RB, CB), jnp.bfloat16),
        cost_estimate=pl.CostEstimate(flops=0, bytes_accessed=1 << 20, transcendentals=0),
        compiler_params=pltpu.CompilerParams(vmem_limit_bytes=8 << 20),
        name="join",
    )(*parts)


def adam_rows(other, rb, read, mc_ref, vc_ref, unit_ref, step_ref, mr_ref, vr_ref, keep_scale):
    for cb in range(4):
        cols = slice(cb * CB, (cb + 1) * CB)
        back = lax.rem(other + 4 - (rb * 2 + cb // 2), 4)
        g = read(back, cb % 2).astype(jnp.float32)
        m = mc_ref[:, cols].astype(jnp.float32) * unit_ref[:, cb:cb + 1] + 0.1 * g
        v = vc_ref[:, cols].astype(jnp.float32) * unit_ref[:, 4 + cb:5 + cb] + 0.001 * g * g
        w = v * (bias_first * bias_first / bias_second)
        step_ref[:, cols] = m / (w * lax.rsqrt(w) + 1e-08 * bias_first)
        ms = jnp.max(jnp.abs(m), axis=1, keepdims=True)
        vs = jnp.max(v, axis=1, keepdims=True)
        keep_scale(cb, ms, vs)
        mr_ref[:, cols] = (m * (1.0 / (ms + 1e-06))).astype(jnp.bfloat16)
        vr_ref[:, cols] = (v * (1.0 / (vs + 1e-06))).astype(jnp.bfloat16)


def units_kernel(me_ref, ve_ref, out_ref, hold):
    hold[...] = jnp.zeros_like(hold)
    for part in range(ROWS // 128):
        rows = slice(part * 128, (part + 1) * 128)
        hold[0:4, :] = jnp.exp2(me_ref[:, rows].astype(jnp.float32)) * (0.9 / 127.0)
        hold[4:8, :] = jnp.exp2(ve_ref[:, rows].astype(jnp.float32)) * (0.999 / 255.0)
        out_ref[rows, :] = hold[...].T


def units_call(m_exp, v_exp):
    return pl.pallas_call(
        units_kernel,
        in_specs=vmem(2),
        out_specs=vmem(1)[0],
        out_shape=jax.ShapeDtypeStruct((ROWS, 128), jnp.float32),
        scratch_shapes=[pltpu.VMEM((128, 128), jnp.float32)],
        cost_estimate=pl.CostEstimate(flops=ROWS * 128, bytes_accessed=1 << 20, transcendentals=8 * ROWS),
        compiler_params=pltpu.CompilerParams(vmem_limit_bytes=4 << 20),
        name="units",
    )(m_exp.T, v_exp.T)


def adam_own_kernel(where, g_ref, mc_ref, vc_ref, unit_ref, step_ref, mr_ref, vr_ref, scale_ref):
    def keep_scale(cb, ms, vs):
        scale_ref[:, cb:cb + 1] = ms
        scale_ref[:, 4 + cb:5 + cb] = vs

    adam_rows(
        unpack(where)[3], pl.program_id(0), lambda back, zl: g_ref[back, zl],
        mc_ref, vc_ref, unit_ref, step_ref, mr_ref, vr_ref, keep_scale,
    )


WIDE = [
    jax.ShapeDtypeStruct((ROWS, KH), jnp.float32),
    jax.ShapeDtypeStruct((ROWS, KH), jnp.bfloat16),
    jax.ShapeDtypeStruct((ROWS, KH), jnp.bfloat16),
]


def adam_own(where, g, mc, vc, units):
    def at(i, where):
        return (where[0] // 4) % 4 * 2 + i, 0

    wide, thin = pl.BlockSpec((RB, KH), at), pl.BlockSpec((RB, 128), at)
    return pl.pallas_call(
        adam_own_kernel,
        grid_spec=pltpu.PrefetchScalarGridSpec(
            num_scalar_prefetch=1,
            grid=(2,),
            in_specs=[pl.BlockSpec((4, 2, RB, CB), lambda i, where: (0, 0, 0, 0)), wide, wide, thin],
            out_specs=[wide, wide, wide, pl.BlockSpec((RB, 128), lambda i, where: (i, 0))],
        ),
        out_shape=WIDE + [jax.ShapeDtypeStruct((2 * RB, 128), jnp.float32)],
        cost_estimate=pl.CostEstimate(flops=5 * ROWS * KH, bytes_accessed=4 << 20, transcendentals=ROWS * KH // 2),
        compiler_params=pltpu.CompilerParams(vmem_limit_bytes=16 << 20),
        name="adam_own",
    )(where, g, mc, vc, units)


def place_of(i, pos):
    k = jnp.where(i < 2, 1, jnp.where(i < 4, 3, 2))
    return lax.rem(pos + 4 - k, 4)


def adam_rest_kernel(where, g1, g3, g2, mc_ref, vc_ref, unit_ref, s0, *rest):
    step_ref, mr_ref, vr_ref, ms_ref, vs_ref, scales = rest[3:]
    _, _, pos, other = unpack(where)
    i = pl.program_id(0)
    rb = lax.rem(i, 2)
    rows = pl.ds(pl.multiple_of(place_of(i, pos) * (2 * RB) + rb * RB, 8), RB)

    @pl.when(i == 0)
    def _():
        scales[pl.ds(pl.multiple_of(pos * (2 * RB), 8), 2 * RB), :] = s0[...]

    def keep_scale(cb, ms, vs):
        scales[rows, cb:cb + 1] = ms
        scales[rows, 4 + cb:5 + cb] = vs

    def read(back, zl):
        return jnp.where(i < 2, g1[back, zl], jnp.where(i < 4, g3[back, zl], g2[back, zl]))

    adam_rows(other, rb, read, mc_ref, vc_ref, unit_ref, step_ref, mr_ref, vr_ref, keep_scale)

    @pl.when(i == 5)
    def _():
        for part in range(ROWS // 128):
            cols = slice(part * 128, (part + 1) * 128)
            turned = scales[cols, :].T
            ms_ref[:, cols] = turned[0:4, :]
            vs_ref[:, cols] = turned[4:8, :]


def adam_rest(where, g, mc, vc, units, s0, done):
    def at(i, where):
        return place_of(i, (where[0] // 4) % 4) * 2 + lax.rem(i, 2), 0

    wide, thin = pl.BlockSpec((RB, KH), at), pl.BlockSpec((RB, 128), at)
    flat = pl.BlockSpec((4, ROWS), lambda i, where: (0, 0))
    whole = pl.BlockSpec((4, 2, RB, CB), lambda i, where: (0, 0, 0, 0))
    return pl.pallas_call(
        adam_rest_kernel,
        grid_spec=pltpu.PrefetchScalarGridSpec(
            num_scalar_prefetch=1,
            grid=(6,),
            in_specs=[whole] * 3 + [wide, wide, thin, pl.BlockSpec((2 * RB, 128), lambda i, where: (0, 0))]
            + [pl.BlockSpec(memory_space=pl.ANY)] * 3,
            out_specs=[wide, wide, wide, flat, flat],
            scratch_shapes=[pltpu.VMEM((ROWS, 128), jnp.float32)],
        ),
        out_shape=WIDE + [jax.ShapeDtypeStruct((4, ROWS), jnp.float32)] * 2,
        input_output_aliases={8: 0, 9: 1, 10: 2},
        cost_estimate=pl.CostEstimate(flops=15 * ROWS * KH, bytes_accessed=12 << 20, transcendentals=2 * ROWS * KH),
        compiler_params=pltpu.CompilerParams(vmem_limit_bytes=24 << 20),
        name="adam_rest",
    )(where, *g, mc, vc, units, s0, *done)


def dot(a, b):
    return jnp.dot(a, b, preferred_element_type=jnp.float32)


def dot_t(a, b):
    return lax.dot_general(a, b, (((1,), (1,)), ((), ())), preferred_element_type=jnp.float32)


def shard_cols(shard):
    return pl.ds(pl.multiple_of(shard * ROWS, 128), ROWS)


def scale_by_gain(value, gain, shard):
    parts = []
    for part in range(ROWS // 128):
        row = gain[pl.ds(shard * (ROWS // 128) + part, 1), :]
        parts.append(value[:, part * 128:(part + 1) * 128] * row)
    return jnp.concatenate(parts, axis=1)


def half(zh, c, mine, theirs, x, kg, gain, weights, scaled):
    total = dot(mine[:, shard_cols(zh)], weights[0][...]) + dot(theirs[:, shard_cols(zh)], weights[1][...])
    inner = jnp.zeros((T, 1), jnp.float32)
    for k, shard in enumerate((2 * zh + c, 2 * zh + 1 - c)):
        value = scale_by_gain(dot_t(kg[...], weights[k][...]), gain, shard)
        scaled[:, k * ROWS:(k + 1) * ROWS] = value
        inner += jnp.sum(value * x[:, shard_cols(shard)].astype(jnp.float32), axis=1, keepdims=True)
    return total, inner


def near_kernel(where, mine, theirs, x, kg, gain, own, other, keys, inner, scaled):
    c, zh, _, _ = unpack(where)
    keys[...], inner[...] = half(zh, c, mine, theirs, x, kg, gain, (own, other), scaled)


def near_call(where, mine, theirs, tokens, key_grad, gain, own, other):
    return pl.pallas_call(
        near_kernel,
        in_specs=[pl.BlockSpec(memory_space=pltpu.SMEM)] + vmem(7),
        out_specs=vmem(3),
        out_shape=[
            jax.ShapeDtypeStruct((T, KH), jnp.float32),
            jax.ShapeDtypeStruct((T, 1), jnp.float32),
            jax.ShapeDtypeStruct((T, D // 2), jnp.float32),
        ],
        cost_estimate=pl.CostEstimate(flops=2 * T * D * KH, bytes_accessed=18 << 20, transcendentals=0),
        compiler_params=pltpu.CompilerParams(vmem_limit_bytes=30 << 20),
        name="near",
    )(where, mine, theirs, tokens, key_grad, gain, own, other)


def keys_kernel(where, mine, theirs, near, far, far_other, out):
    there = shard_cols(1 - unpack(where)[1])
    total = near[...] + dot(mine[:, there], far[...]) + dot(theirs[:, there], far_other[...])
    out[...] = total.astype(jnp.bfloat16)


def keys_call(where, mine, theirs, near, far, far_other):
    return pl.pallas_call(
        keys_kernel,
        in_specs=[pl.BlockSpec(memory_space=pltpu.SMEM)] + vmem(5),
        out_specs=vmem(1)[0],
        out_shape=jax.ShapeDtypeStruct((T, KH), jnp.bfloat16),
        cost_estimate=pl.CostEstimate(flops=T * D * KH, bytes_accessed=10 << 20, transcendentals=0),
        compiler_params=pltpu.CompilerParams(vmem_limit_bytes=20 << 20),
        name="keys",
    )(where, mine, theirs, near, far, far_other)


def back_kernel(where, x, kg, inv_ref, gain, inner_ref, scaled, far, far_other, out, hold):
    c, zh, _, _ = unpack(where)
    inner = inner_ref[...]
    shards = (2 * (1 - zh) + c, 2 * (1 - zh) + 1 - c)
    for k, (shard, weight) in enumerate(zip(shards, (far, far_other))):
        value = scale_by_gain(dot_t(kg[...], weight[...]), gain, shard)
        hold[:, k * ROWS:(k + 1) * ROWS] = value
        inner += jnp.sum(value * x[:, shard_cols(shard)].astype(jnp.float32), axis=1, keepdims=True)
    inv = inv_ref[...]
    pull = inv * inv * inv * (inner * (1.0 / D))
    for source, shards in ((scaled, (2 * zh + c, 2 * zh + 1 - c)), (hold, shards)):
        for k, shard in enumerate(shards):
            xf = x[:, shard_cols(shard)].astype(jnp.float32)
            value = inv * source[:, k * ROWS:(k + 1) * ROWS] - xf * pull
            out[:, shard_cols(shard)] = value.astype(jnp.bfloat16)


def back_call(where, tokens, key_grad, inv, gain, inner, scaled, far, far_other):
    return pl.pallas_call(
        back_kernel,
        in_specs=[pl.BlockSpec(memory_space=pltpu.SMEM)] + vmem(8),
        out_specs=vmem(1)[0],
        out_shape=jax.ShapeDtypeStruct((T, D), jnp.bfloat16),
        scratch_shapes=[pltpu.VMEM((T, D // 2), jnp.float32)],
        cost_estimate=pl.CostEstimate(flops=T * D * KH, bytes_accessed=16 << 20, transcendentals=0),
        compiler_params=pltpu.CompilerParams(vmem_limit_bytes=32 << 20),
        name="back",
    )(where, tokens, key_grad, inv, gain, inner, scaled, far, far_other)


def device_step(tokens, gain, key_grad, weight, m_code, m_exp, v_code, v_exp):
    zh, c = lax.axis_index("zh"), lax.axis_index("c")
    y, x = lax.axis_index("y"), lax.axis_index("x")
    pos = jnp.where(c == 0, x, y)
    pos_other = jnp.where(c == 0, y, x)
    where = (c + 2 * zh + 4 * pos + 16 * pos_other).astype(jnp.int32).reshape(1)

    gain = gain.reshape(D // 128, 128)

    far = send(weight, across)
    kg_other = send(key_grad, partner)
    w_other = send(weight, partner)

    mine, theirs, inv = norm_call(where, tokens, gain)
    received = send(theirs, partner)
    parts = grad_call(where, mine, received, key_grad, kg_other)
    parts = [parts[0]] + [send(parts[k], around(k)) for k in RING[1:]]
    near_keys, inner, scaled = near_call(where, mine, theirs, tokens, key_grad, gain, weight, w_other)
    units = units_call(m_exp, v_exp)
    parts = list(first_sum(parts))
    far_other = send(far, partner)
    parts = [parts[0]] + [send(parts[k], around(k, True)) for k in RING[1:]]
    keys = keys_call(where, mine, theirs, near_keys, far, far_other)
    keep, give = second_sum(where, parts)
    near = send(keep, zl_partner)
    across_z = send(give, across)
    opposite_z = send(give, opposite)
    total = total_call(keep, near, across_z, opposite_z)

    total = join_call([total] + send_ring(total, True))
    got = send_ring(total, False)
    *done, scales = adam_own(where, total, m_code, v_code, units)
    token_grad = back_call(where, tokens, key_grad, inv, gain, inner, scaled, far, far_other)
    outs = adam_rest(where, got, m_code, v_code, units, scales, done)
    step, m_rel, v_rel, m_scale, v_scale = outs
    return keys, token_grad, step, m_rel, m_scale.T, v_rel, v_scale.T


def solution(mesh):
    inner = Mesh(mesh.devices.reshape(2, 2, 4, 4, 2), AXES)
    tok = P(AXES, None)
    row = P(("zh", "c"), None)

    return jax.shard_map(
        device_step,
        mesh=inner,
        in_specs=(tok, P(None), tok, row, row, row, row, row),
        out_specs=(tok, tok, row, row, row, row, row),
        check_vma=False,
    )
```

profile of v0, /device:TPU:68, one launch (start us, length us, event | category | flops | bytes accessed | tf_op | source)
XLA Modules:
  0.0 126.9 jit_solution(14794750942935121184)
XLA Ops:
  0.8 2.0 %copy-done = bf16[384,4608]{1,0:T(8,128)(2,1)S(1)} copy-done((bf16[384,4608]{1,0:T(8,128)(2,1)S(1)}, bf16[384,4608]{1,0:T(8,128)(2,1)}, u32[]{:S(2)}) %copy-start) | copy-done | bytes 3538968
  2.8 0.7 copy-done.5
  3.6 1.9 %norm.1 = (bf16[384,2304]{1,0:T(8,128)(2,1)S(1)}, bf16[384,2304]{1,0:T(8,128)(2,1)S(1)}, f32[384,1]{1,0:T(8,128)S(1)}) custom-call(s32[1]{0:T(128)} %bitcast.where, bf16[384,4608]{1,0:T(8,128)(2,1)S(1)} %copy-done, f32[36,128]{1,0:T(8,128)S(1)} %bitcast.6), custom_call_target="tpu_custom_call" | custom-call | flops 10616832 | bytes 7077888 | tf_op jit(solution)/shard_map/norm/pallas_call | solution.py:96
  6.1 4.2 %collective-permute-done.4.kb_ref = bf16[384,1024]{1,0:T(8,128)(2,1)S(1)} collective-permute-done((bf16[384,1024]{1,0:T(8,128)(2,1)S(1)}, bf16[384,1024]{1,0:T(8,128)(2,1)S(1)}, u32[]{:S(2)}, u32[]{:S(2)}) %collective-permute-start.4) | collective-permute-done | bytes 786464 | tf_op jit(solution)/shard_map/ppermute | solution.py:64
  10.3 6.6 %grad.1 = (bf16[4,2,2,144,256]{4,3,2,1,0:T(8,128)(2,1)S(1)}, bf16[4,2,2,144,256]{4,3,2,1,0:T(8,128)(2,1)S(1)}, bf16[4,2,2,144,256]{4,3,2,1,0:T(8,128)(2,1)S(1)}, bf16[4,2,2,144,256]{4,3,2,1,0:T(8,128)(2,1)S(1)}) custom-call(s32[1]{0:T(128)} %bitcast.where, bf16[384,2304]{1,0:T(8,128)(2,1)S(1)} %get-tuple-element.32.mine.a_ref, ...), custom_call_target="tpu_custom_call" | custom-call | flops 3623878656 | bytes 10485760 | tf_op jit(solution)/shard_map/grad/pallas_call | solution.py:140
  16.9 1.3 collective-permute-start.5
  18.2 0.8 collective-permute-start.6
  19.0 1.7 %collective-permute-start.7 = (bf16[4,2,2,144,256]{4,3,2,1,0:T(8,128)(2,1)S(1)}, bf16[4,2,2,144,256]{4,3,2,1,0:T(8,128)(2,1)S(1)}, u32[]{:S(2)}, u32[]{:S(2)}) collective-permute-start(bf16[4,2,2,144,256]{4,3,2,1,0:T(8,128)(2,1)S(1)} %get-tuple-element.41), channel_id=1, source_target_pairs={{0,4},{1,5},{2,6},{3,7},{4,0},{5,1},{6,2},{7,3},{8,12},{9,13},{10,... | collective-permute-start | bytes 3538952 | tf_op jit(solution)/shard_map/ppermute | solution.py:64
  20.7 33.2 %collective-permute-done.1.far = bf16[1152,1024]{1,0:T(8,128)(2,1)S(1)} collective-permute-done((bf16[1152,1024]{1,0:T(8,128)(2,1)}, bf16[1152,1024]{1,0:T(8,128)(2,1)S(1)}, u32[]{:S(2)}, u32[]{:S(2)}) %collective-permute-start.1) | collective-permute-done | bytes 2359328 | tf_op jit(solution)/shard_map/ppermute | solution.py:64
  54.6 1.6 %collective-permute-start.8 = (bf16[2,2,144,256]{3,2,1,0:T(8,128)(2,1)S(1)}, bf16[2,2,144,256]{3,2,1,0:T(8,128)(2,1)S(1)}, u32[]{:S(2)}, u32[]{:S(2)}) collective-permute-start(bf16[2,2,144,256]{3,2,1,0:T(8,128)(2,1)S(1)} %get-tuple-element.43), channel_id=1, source_target_pairs={{0,8},{1,9},{2,10},{3,11},{4,12},{5,13},{6,14},{7,15},{8,16},{9,17... | collective-permute-start | bytes 884744 | tf_op jit(solution)/shard_map/ppermute | solution.py:64
  56.2 1.7 %collective-permute-start.9 = (bf16[2,2,144,256]{3,2,1,0:T(8,128)(2,1)S(1)}, bf16[2,2,144,256]{3,2,1,0:T(8,128)(2,1)S(1)}, u32[]{:S(2)}, u32[]{:S(2)}) collective-permute-start(bf16[2,2,144,256]{3,2,1,0:T(8,128)(2,1)S(1)} %get-tuple-element.44), channel_id=1, source_target_pairs={{0,24},{1,25},{2,26},{3,27},{4,28},{5,29},{6,30},{7,31},{8,0},{9,1... | collective-permute-start | bytes 884744 | tf_op jit(solution)/shard_map/ppermute | solution.py:64
  57.9 2.0 %collective-permute-start.10 = (bf16[2,2,144,256]{3,2,1,0:T(8,128)(2,1)S(1)}, bf16[2,2,144,256]{3,2,1,0:T(8,128)(2,1)S(1)}, u32[]{:S(2)}, u32[]{:S(2)}) collective-permute-start(bf16[2,2,144,256]{3,2,1,0:T(8,128)(2,1)S(1)} %get-tuple-element.45), channel_id=1, source_target_pairs={{0,16},{1,17},{2,18},{3,19},{4,20},{5,21},{6,22},{7,23},{8,24},{9,... | collective-permute-start | bytes 884744 | tf_op jit(solution)/shard_map/ppermute | solution.py:64
  59.9 2.7 %collective-permute-done.8.refs_1_ = bf16[2,2,144,256]{3,2,1,0:T(8,128)(2,1)S(1)} collective-permute-done((bf16[2,2,144,256]{3,2,1,0:T(8,128)(2,1)S(1)}, bf16[2,2,144,256]{3,2,1,0:T(8,128)(2,1)S(1)}, u32[]{:S(2)}, u32[]{:S(2)}) %collective-permute-start.8) | collective-permute-done | bytes 294944 | tf_op jit(solution)/shard_map/ppermute | solution.py:64
  62.9 4.0 %collective-permute-done.10.refs_3_ = bf16[2,2,144,256]{3,2,1,0:T(8,128)(2,1)S(1)} collective-permute-done((bf16[2,2,144,256]{3,2,1,0:T(8,128)(2,1)S(1)}, bf16[2,2,144,256]{3,2,1,0:T(8,128)(2,1)S(1)}, u32[]{:S(2)}, u32[]{:S(2)}) %collective-permute-start.10) | collective-permute-done | bytes 294944 | tf_op jit(solution)/shard_map/ppermute | solution.py:64
  67.1 2.9 %collective-permute-start.11 = (bf16[2,144,256]{2,1,0:T(8,128)(2,1)S(1)}, bf16[2,144,256]{2,1,0:T(8,128)(2,1)S(1)}, u32[]{:S(2)}, u32[]{:S(2)}) collective-permute-start(bf16[2,144,256]{2,1,0:T(8,128)(2,1)S(1)} %get-tuple-element.46.own), channel_id=1, source_target_pairs={{0,1},{1,0},{2,3},{3,2},{4,5},{5,4},{6,7},{7,6},{8,9},{9,8},{10,11... | collective-permute-start | bytes 442376 | tf_op jit(solution)/shard_map/ppermute | solution.py:64
  70.0 1.6 %collective-permute-start.12 = (bf16[2,144,256]{2,1,0:T(8,128)(2,1)S(1)}, bf16[2,144,256]{2,1,0:T(8,128)(2,1)S(1)}, u32[]{:S(2)}, u32[]{:S(2)}) collective-permute-start(bf16[2,144,256]{2,1,0:T(8,128)(2,1)S(1)} %get-tuple-element.47), channel_id=1, source_target_pairs={{0,65},{1,64},{2,67},{3,66},{4,69},{5,68},{6,71},{7,70},{8,73},{9,... | collective-permute-start | bytes 442376 | tf_op jit(solution)/shard_map/ppermute | solution.py:64
  71.6 1.6 %collective-permute-done.11.near = bf16[2,144,256]{2,1,0:T(8,128)(2,1)S(1)} collective-permute-done((bf16[2,144,256]{2,1,0:T(8,128)(2,1)S(1)}, bf16[2,144,256]{2,1,0:T(8,128)(2,1)S(1)}, u32[]{:S(2)}, u32[]{:S(2)}) %collective-permute-start.11) | collective-permute-done | bytes 147488 | tf_op jit(solution)/shard_map/ppermute | solution.py:64
  73.2 3.6 %collective-permute-done.13.far = bf16[2,144,256]{2,1,0:T(8,128)(2,1)S(1)} collective-permute-done((bf16[2,144,256]{2,1,0:T(8,128)(2,1)S(1)}, bf16[2,144,256]{2,1,0:T(8,128)(2,1)S(1)}, u32[]{:S(2)}, u32[]{:S(2)}) %collective-permute-start.13) | collective-permute-done | bytes 147488 | tf_op jit(solution)/shard_map/ppermute | solution.py:64
  77.1 2.1 %collective-permute-start.16 = (bf16[2,144,256]{2,1,0:T(8,128)(2,1)S(1)}, bf16[2,144,256]{2,1,0:T(8,128)(2,1)S(1)}, u32[]{:S(2)}, u32[]{:S(2)}) collective-permute-start(bf16[2,144,256]{2,1,0:T(8,128)(2,1)S(1)} %total.1.refs_0_), channel_id=1, source_target_pairs={{0,16},{1,17},{2,18},{3,19},{4,20},{5,21},{6,22},{7,23},{8,24},{9,... | collective-permute-start | bytes 442376 | tf_op jit(solution)/shard_map/ppermute | solution.py:64
  79.2 2.1 %collective-permute-start.15 = (bf16[2,144,256]{2,1,0:T(8,128)(2,1)S(1)}, bf16[2,144,256]{2,1,0:T(8,128)(2,1)S(1)}, u32[]{:S(2)}, u32[]{:S(2)}) collective-permute-start(bf16[2,144,256]{2,1,0:T(8,128)(2,1)S(1)} %total.1.refs_0_), channel_id=1, source_target_pairs={{0,24},{1,25},{2,26},{3,27},{4,28},{5,29},{6,30},{7,31},{8,0},{9,1... | collective-permute-start | bytes 442376 | tf_op jit(solution)/shard_map/ppermute | solution.py:64
  81.3 2.5 %collective-permute-done.16.refs_3_ = bf16[2,144,256]{2,1,0:T(8,128)(2,1)S(1)} collective-permute-done((bf16[2,144,256]{2,1,0:T(8,128)(2,1)S(1)}, bf16[2,144,256]{2,1,0:T(8,128)(2,1)S(1)}, u32[]{:S(2)}, u32[]{:S(2)}) %collective-permute-start.16) | collective-permute-done | bytes 147488 | tf_op jit(solution)/shard_map/ppermute | solution.py:64
  83.8 0.9 collective-permute-done.15.refs_2_
  84.7 2.9 %collective-permute-done.14.refs_1_ = bf16[2,144,256]{2,1,0:T(8,128)(2,1)S(1)} collective-permute-done((bf16[2,144,256]{2,1,0:T(8,128)(2,1)S(1)}, bf16[2,144,256]{2,1,0:T(8,128)(2,1)S(1)}, u32[]{:S(2)}, u32[]{:S(2)}) %collective-permute-start.14) | collective-permute-done | bytes 147488 | tf_op jit(solution)/shard_map/ppermute | solution.py:64
  87.7 1.5 %collective-permute-start.19 = (bf16[4,2,144,256]{3,2,1,0:T(8,128)(2,1)S(1)}, bf16[4,2,144,256]{3,2,1,0:T(8,128)(2,1)S(1)}, u32[]{:S(2)}, u32[]{:S(2)}) collective-permute-start(bf16[4,2,144,256]{3,2,1,0:T(8,128)(2,1)S(1)} %join.1.g_ref), channel_id=1, source_target_pairs={{0,4},{1,5},{2,6},{3,7},{4,0},{5,1},{6,2},{7,3},{8,12},{9,13},{10,... | collective-permute-start | bytes 1769480 | tf_op jit(solution)/shard_map/ppermute | solution.py:64
  89.2 6.5 %collective-permute-start.18 = (bf16[4,2,144,256]{3,2,1,0:T(8,128)(2,1)S(1)}, bf16[4,2,144,256]{3,2,1,0:T(8,128)(2,1)S(1)}, u32[]{:S(2)}, u32[]{:S(2)}) collective-permute-start(bf16[4,2,144,256]{3,2,1,0:T(8,128)(2,1)S(1)} %join.1.g_ref), channel_id=1, source_target_pairs={{0,6},{1,7},{2,0},{3,1},{4,2},{5,3},{6,4},{7,5},{8,14},{9,15},{10,... | collective-permute-start | bytes 1769480 | tf_op jit(solution)/shard_map/ppermute | solution.py:64
  95.6 2.0 %collective-permute-start.17 = (bf16[4,2,144,256]{3,2,1,0:T(8,128)(2,1)S(1)}, bf16[4,2,144,256]{3,2,1,0:T(8,128)(2,1)S(1)}, u32[]{:S(2)}, u32[]{:S(2)}) collective-permute-start(bf16[4,2,144,256]{3,2,1,0:T(8,128)(2,1)S(1)} %join.1.g_ref), channel_id=1, source_target_pairs={{0,2},{1,3},{2,4},{3,5},{4,6},{5,7},{6,0},{7,1},{8,10},{9,11},{10,... | collective-permute-start | bytes 1769480 | tf_op jit(solution)/shard_map/ppermute | solution.py:64
  98.0 4.4 %near.1 = (f32[384,1024]{1,0:T(8,128)S(1)}, f32[384,1]{1,0:T(8,128)S(1)}, f32[384,2304]{1,0:T(8,128)S(1)}) custom-call(s32[1]{0:T(128)} %bitcast.where, bf16[384,2304]{1,0:T(8,128)(2,1)S(1)} %get-tuple-element.32.mine.a_ref, bf16[384,2304]{1,0:T(8,128)(2,1)S(1)} %get-tuple-element.33.theirs, bf16[384,4608]{1,0:T(8,128)(2,1)S(1)} %copy-done.1, ...), custom_call_target="tpu_custom_call" | custom-call | flops 3623878656 | bytes 18874368 | tf_op jit(solution)/shard_map/near/pallas_call | solution.py:409
  102.4 2.6 %adam_own.1 = (f32[1152,1024]{1,0:T(8,128)}, bf16[1152,1024]{1,0:T(8,128)(2,1)}, bf16[1152,1024]{1,0:T(8,128)(2,1)}, f32[288,128]{1,0:T(8,128)S(1)}) custom-call(s32[1]{0:T(128)} %bitcast.where, bf16[4,2,144,256]{3,2,1,0:T(8,128)(2,1)S(1)} %join.1.g_ref, bf16[1152,1024]{1,0:T(8,128)(2,1)S(1)} %copy-done.2, bf16[1152,1024]{1,0:T(8,128)(2,1)S(1)} %copy-done.3, ...), custom_call_target="tpu_custom_call" | custom-call | flops 5898240 | bytes 4194304 | tf_op jit(solution)/shard_map/adam_own/pallas_call | solution.py:299
  105.0 6.9 %collective-permute-done.18.g3 = bf16[4,2,144,256]{3,2,1,0:T(8,128)(2,1)S(1)} collective-permute-done((bf16[4,2,144,256]{3,2,1,0:T(8,128)(2,1)S(1)}, bf16[4,2,144,256]{3,2,1,0:T(8,128)(2,1)S(1)}, u32[]{:S(2)}, u32[]{:S(2)}) %collective-permute-start.18) | collective-permute-done | bytes 589856 | tf_op jit(solution)/shard_map/ppermute | solution.py:64
  111.8 6.4 %adam_rest.1 = (f32[1152,1024]{1,0:T(8,128)}, bf16[1152,1024]{1,0:T(8,128)(2,1)}, bf16[1152,1024]{1,0:T(8,128)(2,1)}, f32[4,1152]{1,0:T(4,128)}, f32[4,1152]{1,0:T(4,128)}) custom-call(s32[1]{0:T(128)} %bitcast.where, bf16[4,2,144,256]{3,2,1,0:T(8,128)(2,1)S(1)} %collective-permute-done.17.g1, ...), custom_call_target="tpu_custom_call", output_to_operand_aliasing={{0}: (8, {}), {1}: (9, {}), {2}: (10, {})} | custom-call | flops 17694720 | bytes 12582912 | tf_op jit(solution)/shard_map/adam_rest/pallas_call | solution.py:355
  118.3 3.1 %keys.1 = bf16[384,1024]{1,0:T(8,128)(2,1)} custom-call(s32[1]{0:T(128)} %bitcast.where, bf16[384,2304]{1,0:T(8,128)(2,1)S(1)} %get-tuple-element.32.mine.a_ref, bf16[384,2304]{1,0:T(8,128)(2,1)S(1)} %get-tuple-element.33.theirs, f32[384,1024]{1,0:T(8,128)S(1)} %get-tuple-element.34.near, bf16[1152,1024]{1,0:T(8,128)(2,1)S(1)} %collective-permute-done.1.far, ...), custom_call_target="tpu_custom_call" | custom-call | flops 1811939328 | bytes 10485760 | tf_op jit(solution)/shard_map/keys/pallas_call | solution.py:431
  121.3 5.6 %back.1 = bf16[384,4608]{1,0:T(8,128)(2,1)} custom-call(s32[1]{0:T(128)} %bitcast.where, bf16[384,4608]{1,0:T(8,128)(2,1)S(1)} %copy-done.1, bf16[384,1024]{1,0:T(8,128)(2,1)S(1)} %copy-done.4, f32[384,1]{1,0:T(8,128)S(1)} %get-tuple-element.35.inv_ref, f32[36,128]{1,0:T(8,128)S(1)} %bitcast.8, f32[384,1]{1,0:T(8,128)S(1)} %get-tuple-element.36.inner_ref, ...), custom_call_target="tpu_custom_call" | custom-call | flops 1811939328 | bytes 16777216 | tf_op jit(solution)/shard_map/back/pallas_call | solution.py:460
  (42 shorter events, 2.6 us)
Async XLA Ops:
  0.6 53.3 %collective-permute-start.1 = (bf16[1152,1024]{1,0:T(8,128)(2,1)}, bf16[1152,1024]{1,0:T(8,128)(2,1)S(1)}, u32[]{:S(2)}, u32[]{:S(2)}) collective-permute-start(bf16[1152,1024]{1,0:T(8,128)(2,1)} %own.1), channel_id=1, source_target_pairs={{0,65},{1,64},{2,67},{3,66},{4,69},{5,68},{6,71},{7,70},{8,73},{9,... | collective-permute-start | bytes 7077896 | tf_op jit(solution)/shard_map/ppermute | solution.py:64
  0.8 2.0 %copy-start = (bf16[384,4608]{1,0:T(8,128)(2,1)S(1)}, bf16[384,4608]{1,0:T(8,128)(2,1)}, u32[]{:S(2)}) copy-start(bf16[384,4608]{1,0:T(8,128)(2,1)} %x.3) | copy-start | bytes 10616836
  2.8 0.7 copy-start.5
  3.5 2.0 %copy-start.4 = (bf16[384,1024]{1,0:T(8,128)(2,1)S(1)}, bf16[384,1024]{1,0:T(8,128)(2,1)}, u32[]{:S(2)}) copy-start(bf16[384,1024]{1,0:T(8,128)(2,1)} %ka_ref.1) | copy-start | bytes 2359300
  3.6 2.5 %copy-start.9 = (bf16[1152,1024]{1,0:T(8,128)(2,1)S(1)}, bf16[1152,1024]{1,0:T(8,128)(2,1)}, u32[]{:S(2)}) copy-start(bf16[1152,1024]{1,0:T(8,128)(2,1)} %own.1) | copy-start | bytes 7077892
  5.4 4.9 %collective-permute-start.3 = (bf16[384,2304]{1,0:T(8,128)(2,1)S(1)}, bf16[384,2304]{1,0:T(8,128)(2,1)S(1)}, u32[]{:S(2)}, u32[]{:S(2)}) collective-permute-start(bf16[384,2304]{1,0:T(8,128)(2,1)S(1)} %get-tuple-element.33.theirs), channel_id=1, source_target_pairs={{0,32},{1,33},{2,34},{3,35},{4,36},{5,37},{6,38},{7,39},{8,40},{9,... | collective-permute-start | bytes 5308424 | tf_op jit(solution)/shard_map/ppermute | solution.py:64
  5.5 4.8 %collective-permute-start.4 = (bf16[384,1024]{1,0:T(8,128)(2,1)S(1)}, bf16[384,1024]{1,0:T(8,128)(2,1)S(1)}, u32[]{:S(2)}, u32[]{:S(2)}) collective-permute-start(bf16[384,1024]{1,0:T(8,128)(2,1)S(1)} %copy-done.4), channel_id=1, source_target_pairs={{0,32},{1,33},{2,34},{3,35},{4,36},{5,37},{6,38},{7,39},{8,40},{9,... | collective-permute-start | bytes 2359304 | tf_op jit(solution)/shard_map/ppermute | solution.py:64
  6.0 91.9 %collective-permute-start = (bf16[1152,1024]{1,0:T(8,128)(2,1)S(1)}, bf16[1152,1024]{1,0:T(8,128)(2,1)S(1)}, u32[]{:S(2)}, u32[]{:S(2)}) collective-permute-start(bf16[1152,1024]{1,0:T(8,128)(2,1)S(1)} %copy-done.9), channel_id=1, source_target_pairs={{0,32},{1,33},{2,34},{3,35},{4,36},{5,37},{6,38},{7,39},{8,40},{9,... | collective-permute-start | bytes 7077896 | tf_op jit(solution)/shard_map/ppermute | solution.py:64
  16.9 37.0 %collective-permute-start.5 = (bf16[4,2,2,144,256]{4,3,2,1,0:T(8,128)(2,1)S(1)}, bf16[4,2,2,144,256]{4,3,2,1,0:T(8,128)(2,1)S(1)}, u32[]{:S(2)}, u32[]{:S(2)}) collective-permute-start(bf16[4,2,2,144,256]{4,3,2,1,0:T(8,128)(2,1)S(1)} %get-tuple-element.39), channel_id=1, source_target_pairs={{0,2},{1,3},{2,4},{3,5},{4,6},{5,7},{6,0},{7,1},{8,10},{9,11},{10,... | collective-permute-start | bytes 3538952 | tf_op jit(solution)/shard_map/ppermute | solution.py:64
  18.2 35.7 %collective-permute-start.6 = (bf16[4,2,2,144,256]{4,3,2,1,0:T(8,128)(2,1)S(1)}, bf16[4,2,2,144,256]{4,3,2,1,0:T(8,128)(2,1)S(1)}, u32[]{:S(2)}, u32[]{:S(2)}) collective-permute-start(bf16[4,2,2,144,256]{4,3,2,1,0:T(8,128)(2,1)S(1)} %get-tuple-element.40), channel_id=1, source_target_pairs={{0,6},{1,7},{2,0},{3,1},{4,2},{5,3},{6,4},{7,5},{8,14},{9,15},{10,... | collective-permute-start | bytes 3538952 | tf_op jit(solution)/shard_map/ppermute | solution.py:64
  19.0 34.9 %collective-permute-start.7 = (bf16[4,2,2,144,256]{4,3,2,1,0:T(8,128)(2,1)S(1)}, bf16[4,2,2,144,256]{4,3,2,1,0:T(8,128)(2,1)S(1)}, u32[]{:S(2)}, u32[]{:S(2)}) collective-permute-start(bf16[4,2,2,144,256]{4,3,2,1,0:T(8,128)(2,1)S(1)} %get-tuple-element.41), channel_id=1, source_target_pairs={{0,4},{1,5},{2,6},{3,7},{4,0},{5,1},{6,2},{7,3},{8,12},{9,13},{10,... | collective-permute-start | bytes 3538952 | tf_op jit(solution)/shard_map/ppermute | solution.py:64
  53.9 64.3 %collective-permute-start.2 = (bf16[1152,1024]{1,0:T(8,128)(2,1)S(1)}, bf16[1152,1024]{1,0:T(8,128)(2,1)S(1)}, u32[]{:S(2)}, u32[]{:S(2)}) collective-permute-start(bf16[1152,1024]{1,0:T(8,128)(2,1)S(1)} %collective-permute-done.1.far), channel_id=1, source_target_pairs={{0,32},{1,33},{2,34},{3,35},{4,36},{5,37},{6,38},{7,39},{8,40},{9,... | collective-permute-start | bytes 7077896 | tf_op jit(solution)/shard_map/ppermute | solution.py:64
  53.9 43.7 %copy-start.7 = (s32[1152,4]{0,1:T(4,128)S(1)}, s32[1152,4]{0,1:T(4,128)}, u32[]{:S(2)}) copy-start(s32[1152,4]{0,1:T(4,128)} %param.13) | copy-start | bytes 55300
  53.9 43.7 %copy-start.8 = (s32[1152,4]{0,1:T(4,128)S(1)}, s32[1152,4]{0,1:T(4,128)}, u32[]{:S(2)}) copy-start(s32[1152,4]{0,1:T(4,128)} %param.15) | copy-start | bytes 55300
  54.0 44.0 %copy-start.10 = (bf16[1152,1024]{1,0:T(8,128)(2,1)S(1)}, bf16[1152,1024]{1,0:T(8,128)(2,1)}, u32[]{:S(2)}) copy-start(bf16[1152,1024]{1,0:T(8,128)(2,1)} %own.1) | copy-start | bytes 7077892
  54.6 43.4 %copy-start.1 = (bf16[384,4608]{1,0:T(8,128)(2,1)S(1)}, bf16[384,4608]{1,0:T(8,128)(2,1)}, u32[]{:S(2)}) copy-start(bf16[384,4608]{1,0:T(8,128)(2,1)} %x.3) | copy-start | bytes 10616836
  54.6 43.4 %copy-start.6 = (f32[4608]{0:T(1024)S(1)}, f32[4608]{0:T(1024)}, u32[]{:S(2)}) copy-start(f32[4608]{0:T(1024)} %param.9) | copy-start | bytes 55300
  54.6 8.0 %collective-permute-start.8 = (bf16[2,2,144,256]{3,2,1,0:T(8,128)(2,1)S(1)}, bf16[2,2,144,256]{3,2,1,0:T(8,128)(2,1)S(1)}, u32[]{:S(2)}, u32[]{:S(2)}) collective-permute-start(bf16[2,2,144,256]{3,2,1,0:T(8,128)(2,1)S(1)} %get-tuple-element.43), channel_id=1, source_target_pairs={{0,8},{1,9},{2,10},{3,11},{4,12},{5,13},{6,14},{7,15},{8,16},{9,17... | collective-permute-start | bytes 884744 | tf_op jit(solution)/shard_map/ppermute | solution.py:64
  56.2 6.7 %collective-permute-start.9 = (bf16[2,2,144,256]{3,2,1,0:T(8,128)(2,1)S(1)}, bf16[2,2,144,256]{3,2,1,0:T(8,128)(2,1)S(1)}, u32[]{:S(2)}, u32[]{:S(2)}) collective-permute-start(bf16[2,2,144,256]{3,2,1,0:T(8,128)(2,1)S(1)} %get-tuple-element.44), channel_id=1, source_target_pairs={{0,24},{1,25},{2,26},{3,27},{4,28},{5,29},{6,30},{7,31},{8,0},{9,1... | collective-permute-start | bytes 884744 | tf_op jit(solution)/shard_map/ppermute | solution.py:64
  57.9 9.1 %collective-permute-start.10 = (bf16[2,2,144,256]{3,2,1,0:T(8,128)(2,1)S(1)}, bf16[2,2,144,256]{3,2,1,0:T(8,128)(2,1)S(1)}, u32[]{:S(2)}, u32[]{:S(2)}) collective-permute-start(bf16[2,2,144,256]{3,2,1,0:T(8,128)(2,1)S(1)} %get-tuple-element.45), channel_id=1, source_target_pairs={{0,16},{1,17},{2,18},{3,19},{4,20},{5,21},{6,22},{7,23},{8,24},{9,... | collective-permute-start | bytes 884744 | tf_op jit(solution)/shard_map/ppermute | solution.py:64
  67.1 6.0 %collective-permute-start.11 = (bf16[2,144,256]{2,1,0:T(8,128)(2,1)S(1)}, bf16[2,144,256]{2,1,0:T(8,128)(2,1)S(1)}, u32[]{:S(2)}, u32[]{:S(2)}) collective-permute-start(bf16[2,144,256]{2,1,0:T(8,128)(2,1)S(1)} %get-tuple-element.46.own), channel_id=1, source_target_pairs={{0,1},{1,0},{2,3},{3,2},{4,5},{5,4},{6,7},{7,6},{8,9},{9,8},{10,11... | collective-permute-start | bytes 442376 | tf_op jit(solution)/shard_map/ppermute | solution.py:64
  70.0 6.7 %collective-permute-start.13 = (bf16[2,144,256]{2,1,0:T(8,128)(2,1)S(1)}, bf16[2,144,256]{2,1,0:T(8,128)(2,1)S(1)}, u32[]{:S(2)}, u32[]{:S(2)}) collective-permute-start(bf16[2,144,256]{2,1,0:T(8,128)(2,1)S(1)} %get-tuple-element.47), channel_id=1, source_target_pairs={{0,64},{1,65},{2,66},{3,67},{4,68},{5,69},{6,70},{7,71},{8,72},{9,... | collective-permute-start | bytes 442376 | tf_op jit(solution)/shard_map/ppermute | solution.py:64
  70.0 7.0 %collective-permute-start.12 = (bf16[2,144,256]{2,1,0:T(8,128)(2,1)S(1)}, bf16[2,144,256]{2,1,0:T(8,128)(2,1)S(1)}, u32[]{:S(2)}, u32[]{:S(2)}) collective-permute-start(bf16[2,144,256]{2,1,0:T(8,128)(2,1)S(1)} %get-tuple-element.47), channel_id=1, source_target_pairs={{0,65},{1,64},{2,67},{3,66},{4,69},{5,68},{6,71},{7,70},{8,73},{9,... | collective-permute-start | bytes 442376 | tf_op jit(solution)/shard_map/ppermute | solution.py:64
  77.1 6.7 %collective-permute-start.16 = (bf16[2,144,256]{2,1,0:T(8,128)(2,1)S(1)}, bf16[2,144,256]{2,1,0:T(8,128)(2,1)S(1)}, u32[]{:S(2)}, u32[]{:S(2)}) collective-permute-start(bf16[2,144,256]{2,1,0:T(8,128)(2,1)S(1)} %total.1.refs_0_), channel_id=1, source_target_pairs={{0,16},{1,17},{2,18},{3,19},{4,20},{5,21},{6,22},{7,23},{8,24},{9,... | collective-permute-start | bytes 442376 | tf_op jit(solution)/shard_map/ppermute | solution.py:64
  79.2 5.5 %collective-permute-start.15 = (bf16[2,144,256]{2,1,0:T(8,128)(2,1)S(1)}, bf16[2,144,256]{2,1,0:T(8,128)(2,1)S(1)}, u32[]{:S(2)}, u32[]{:S(2)}) collective-permute-start(bf16[2,144,256]{2,1,0:T(8,128)(2,1)S(1)} %total.1.refs_0_), channel_id=1, source_target_pairs={{0,24},{1,25},{2,26},{3,27},{4,28},{5,29},{6,30},{7,31},{8,0},{9,1... | collective-permute-start | bytes 442376 | tf_op jit(solution)/shard_map/ppermute | solution.py:64
  81.3 6.4 %collective-permute-start.14 = (bf16[2,144,256]{2,1,0:T(8,128)(2,1)S(1)}, bf16[2,144,256]{2,1,0:T(8,128)(2,1)S(1)}, u32[]{:S(2)}, u32[]{:S(2)}) collective-permute-start(bf16[2,144,256]{2,1,0:T(8,128)(2,1)S(1)} %total.1.refs_0_), channel_id=1, source_target_pairs={{0,8},{1,9},{2,10},{3,11},{4,12},{5,13},{6,14},{7,15},{8,16},{9,17... | collective-permute-start | bytes 442376 | tf_op jit(solution)/shard_map/ppermute | solution.py:64
  87.7 17.3 %collective-permute-start.19 = (bf16[4,2,144,256]{3,2,1,0:T(8,128)(2,1)S(1)}, bf16[4,2,144,256]{3,2,1,0:T(8,128)(2,1)S(1)}, u32[]{:S(2)}, u32[]{:S(2)}) collective-permute-start(bf16[4,2,144,256]{3,2,1,0:T(8,128)(2,1)S(1)} %join.1.g_ref), channel_id=1, source_target_pairs={{0,4},{1,5},{2,6},{3,7},{4,0},{5,1},{6,2},{7,3},{8,12},{9,13},{10,... | collective-permute-start | bytes 1769480 | tf_op jit(solution)/shard_map/ppermute | solution.py:64
  89.2 22.7 %collective-permute-start.18 = (bf16[4,2,144,256]{3,2,1,0:T(8,128)(2,1)S(1)}, bf16[4,2,144,256]{3,2,1,0:T(8,128)(2,1)S(1)}, u32[]{:S(2)}, u32[]{:S(2)}) collective-permute-start(bf16[4,2,144,256]{3,2,1,0:T(8,128)(2,1)S(1)} %join.1.g_ref), channel_id=1, source_target_pairs={{0,6},{1,7},{2,0},{3,1},{4,2},{5,3},{6,4},{7,5},{8,14},{9,15},{10,... | collective-permute-start | bytes 1769480 | tf_op jit(solution)/shard_map/ppermute | solution.py:64
  95.6 16.2 %collective-permute-start.17 = (bf16[4,2,144,256]{3,2,1,0:T(8,128)(2,1)S(1)}, bf16[4,2,144,256]{3,2,1,0:T(8,128)(2,1)S(1)}, u32[]{:S(2)}, u32[]{:S(2)}) collective-permute-start(bf16[4,2,144,256]{3,2,1,0:T(8,128)(2,1)S(1)} %join.1.g_ref), channel_id=1, source_target_pairs={{0,2},{1,3},{2,4},{3,5},{4,6},{5,7},{6,0},{7,1},{8,10},{9,11},{10,... | collective-permute-start | bytes 1769480 | tf_op jit(solution)/shard_map/ppermute | solution.py:64
  97.9 4.5 %copy-start.2 = (bf16[1152,1024]{1,0:T(8,128)(2,1)S(1)}, bf16[1152,1024]{1,0:T(8,128)(2,1)}, u32[]{:S(2)}) copy-start(bf16[1152,1024]{1,0:T(8,128)(2,1)} %mc_ref.3) | copy-start | bytes 7077892
  97.9 4.5 %copy-start.3 = (bf16[1152,1024]{1,0:T(8,128)(2,1)S(1)}, bf16[1152,1024]{1,0:T(8,128)(2,1)}, u32[]{:S(2)}) copy-start(bf16[1152,1024]{1,0:T(8,128)(2,1)} %vc_ref.3) | copy-start | bytes 7077892
where the time goes:
time: 127 us
  waiting for transfers between devices  63.1 us (50%)
  Pallas kernels  31.6 us (25%)
  starting transfers between devices  28.6 us (23%)
  local copies, waits for them, and re-layouts  2.78 us (2%)
    ppermute x20, waiting for transfers between devices, send(): return lax.ppermute(value, AXES, pairs(move))  63.1 us
    ppermute x20, starting transfers between devices, send(): return lax.ppermute(value, AXES, pairs(move))  28.6 us
    pallas_call x1, Pallas kernels, grad_call(): pl.pallas_call(grad_kernel, grid_spec=pltpu.PrefetchScalarGridSpec(num_sc...  6.59 us
    pallas_call x1, Pallas kernels, adam_rest(): pl.pallas_call(adam_rest_kernel, grid_spec=pltpu.PrefetchScalarGridSpec(n...  6.4 us
    pallas_call x1, Pallas kernels, back_call(): pl.pallas_call(back_kernel, in_specs=[pl.BlockSpec(memory_space=pltpu.SME...  5.59 us
    pallas_call x1, Pallas kernels, near_call(): pl.pallas_call(near_kernel, in_specs=[pl.BlockSpec(memory_space=pltpu.SME...  4.4 us
    pallas_call x1, Pallas kernels, keys_call(): pl.pallas_call(keys_kernel, in_specs=[pl.BlockSpec(memory_space=pltpu.SME...  3.09 us
    unnamed x22, local copies, waits for them, and re-layouts  2.78 us
  transfers between devices with their start and end apart: 20, of which 12 were waited for; matrix products, arithmetic and copies ran while one was open for 0% of the time, Pallas kernels for 18%

commit v1 on v0

v1 whole, which is shorter than its diff:
```python
import functools

import jax
import jax.numpy as jnp
from jax import lax
from jax.experimental import pallas as pl
from jax.experimental.pallas import tpu as pltpu
from jax.sharding import Mesh, PartitionSpec as P


bias_first = 0.9999734386011124
bias_second = 0.0952078528862904

AXES = ("zh", "c", "y", "x", "zl")

D = 4608
KH = 1024
ROWS = 1152
T = 384
RING = (0, 1, 3, 2)
RB, CB = 144, 256


def index_of(zh, c, y, x, zl):
    return (((zh * 2 + c) * 4 + y) * 4 + x) * 2 + zl


def pairs(move):
    out = []
    for zh in range(2):
        for c in range(2):
            for y in range(4):
                for x in range(4):
                    for zl in range(2):
                        to = move(zh, c, y, x, zl)
                        out.append((index_of(zh, c, y, x, zl), index_of(*to)))
    return out


def partner(zh, c, y, x, zl):
    return zh, 1 - c, y, x, zl


def across(zh, c, y, x, zl):
    return 1 - zh, c, y, x, 1 - zl


def zl_partner(zh, c, y, x, zl):
    return zh, c, y, x, 1 - zl


def opposite(zh, c, y, x, zl):
    return 1 - zh, c, y, x, zl


def around(step, second=False):
    def move(zh, c, y, x, zl):
        if (c == 0) != second:
            return zh, c, y, (x + step) % 4, zl
        return zh, c, (y + step) % 4, x, zl

    return move


def send(value, move):
    return lax.ppermute(value, AXES, pairs(move))


def send_ring(value, second):
    return [send(value, around(k, second)) for k in RING[1:]]


def unpack(where):
    w = where[0]
    return w % 2, (w // 2) % 2, (w // 4) % 4, w // 16


def vmem(n):
    return [pl.BlockSpec(memory_space=pltpu.VMEM)] * n


STEP = 64


def norm_columns(x, inv, gain, core, rows, out):
    for half in range(2):
        for part in range(ROWS // 128):
            at = (half * 2 + core) * (ROWS // 128) + part
            cols = pl.ds(pl.multiple_of(at * 128, 128), 128)
            value = x[rows, cols].astype(jnp.float32) * inv[rows, :] * gain[pl.ds(at, 1), :]
            out[rows, half * ROWS + part * 128:half * ROWS + (part + 1) * 128] = value.astype(jnp.bfloat16)


def norm_kernel(where, x_hbm, gain_hbm, theirs, inv, x, gain, sems):
    rows = [slice(k * STEP, (k + 1) * STEP) for k in range(T // STEP)]
    copies = [pltpu.make_async_copy(x_hbm.at[r], x.at[r], sems.at[k]) for k, r in enumerate(rows)]
    gain_copy = pltpu.make_async_copy(gain_hbm, gain, sems.at[len(rows)])
    gain_copy.start()
    for copy in copies:
        copy.start()
    gain_copy.wait()
    c = unpack(where)[0]
    for copy, r in zip(copies, rows):
        copy.wait()
        xf = x[r, :].astype(jnp.float32)
        inv[r, :] = lax.rsqrt(jnp.mean(xf * xf, axis=1, keepdims=True) + 1e-06)
        norm_columns(x, inv, gain, 1 - c, r, theirs)


def norm_call(where, tokens, gain):
    return pl.pallas_call(
        norm_kernel,
        in_specs=[pl.BlockSpec(memory_space=pltpu.SMEM)] + [pl.BlockSpec(memory_space=pl.ANY)] * 2,
        out_specs=vmem(4),
        out_shape=[
            jax.ShapeDtypeStruct((T, D // 2), jnp.bfloat16),
            jax.ShapeDtypeStruct((T, 1), jnp.float32),
            jax.ShapeDtypeStruct((T, D), jnp.bfloat16),
            jax.ShapeDtypeStruct((D // 128, 128), jnp.float32),
        ],
        scratch_shapes=[pltpu.SemaphoreType.DMA((T // STEP + 1,))],
        cost_estimate=pl.CostEstimate(flops=4 * T * D, bytes_accessed=4 * T * D, transcendentals=T),
        compiler_params=pltpu.CompilerParams(vmem_limit_bytes=47 << 20),
        name="norm",
    )(where, tokens, gain)


def flip(in_ref, out_ref):
    for part in range(D // 2 // 128):
        cols = slice(part * 128, (part + 1) * 128)
        out_ref[cols, :] = in_ref[:, cols].T


def mine_kernel(where, x, inv, gain, mine, mine_t):
    for k in range(T // STEP):
        norm_columns(x, inv, gain, unpack(where)[0], slice(k * STEP, (k + 1) * STEP), mine)
    flip(mine, mine_t)


def mine_call(where, tokens, inv, gain):
    return pl.pallas_call(
        mine_kernel,
        in_specs=[pl.BlockSpec(memory_space=pltpu.SMEM)] + vmem(3),
        out_specs=vmem(2),
        out_shape=[
            jax.ShapeDtypeStruct((T, D // 2), jnp.bfloat16),
            jax.ShapeDtypeStruct((D // 2, T), jnp.bfloat16),
        ],
        cost_estimate=pl.CostEstimate(flops=2 * T * D, bytes_accessed=3 * T * D, transcendentals=0),
        compiler_params=pltpu.CompilerParams(vmem_limit_bytes=6 << 20),
        name="mine",
    )(where, tokens, inv, gain)


def grad_columns(where, a_ref, b_ref, ka_ref, kb_ref, k, out):
    _, _, pos, other = unpack(where)
    cols = pl.ds(pl.multiple_of(lax.rem(pos + k, 4) * CB, 128), CB)
    for zh in range(2):
        rows = slice(zh * ROWS, (zh + 1) * ROWS)
        acc = dot(a_ref[rows, :], ka_ref[:, cols]) + dot(b_ref[rows, :], kb_ref[:, cols])
        for o in range(4):
            for zl in range(2):
                at = (o * 2 + zl) * RB
                out[lax.rem(o + 4 - other, 4), zh, zl] = acc[at:at + RB, :].astype(out.dtype)


def first_grad_kernel(where, a_ref, b_in, ka_ref, kb_ref, b_ref, out):
    flip(b_in, b_ref)
    grad_columns(where, a_ref, b_ref, ka_ref, kb_ref, 2, out)


def grad_kernel(ks, where, *refs):
    for k, out in zip(ks, refs[4:]):
        grad_columns(where, *refs[:4], k, out)


def grad_call(ks, where, a, b, ka, kb, dtype=jnp.bfloat16, first=False):
    out = [jax.ShapeDtypeStruct((4, 2, 2, RB, CB), dtype)] * len(ks)
    return pl.pallas_call(
        first_grad_kernel if first else functools.partial(grad_kernel, ks),
        in_specs=[pl.BlockSpec(memory_space=pltpu.SMEM)] + vmem(4),
        out_specs=vmem(len(ks) + first),
        out_shape=[jax.ShapeDtypeStruct((D // 2, T), jnp.bfloat16)] * first + out,
        cost_estimate=pl.CostEstimate(flops=T * D * KH // 2 * len(ks), bytes_accessed=6 << 20, transcendentals=0),
        compiler_params=pltpu.CompilerParams(vmem_limit_bytes=8 << 20),
        name="grad",
    )(where, a, b, ka, kb)


def add_up(refs):
    total = refs[0][...].astype(jnp.float32)
    for ref in refs[1:]:
        total += ref[...].astype(jnp.float32)
    return total


def first_sum_kernel(*refs):
    for j in range(4):
        refs[4 + j][...] = add_up([ref.at[j] for ref in refs[:4]]).astype(refs[4 + j].dtype)


def first_sum(parts):
    return pl.pallas_call(
        first_sum_kernel,
        in_specs=vmem(4),
        out_specs=vmem(4),
        out_shape=[jax.ShapeDtypeStruct((2, 2, RB, CB), kind) for kind in (jnp.float32,) + (jnp.bfloat16,) * 3],
        cost_estimate=pl.CostEstimate(flops=64 * RB * CB, bytes_accessed=6 << 20, transcendentals=0),
        compiler_params=pltpu.CompilerParams(vmem_limit_bytes=8 << 20),
        name="first_sum",
    )(*parts)


def second_sum_kernel(where, *refs):
    zh = unpack(where)[1]
    for out, h in ((refs[4], zh), (refs[5], 1 - zh)):
        out[...] = add_up([ref.at[h] for ref in refs[:4]]).astype(jnp.bfloat16)


def second_sum(where, parts):
    return pl.pallas_call(
        second_sum_kernel,
        in_specs=[pl.BlockSpec(memory_space=pltpu.SMEM)] + vmem(4),
        out_specs=vmem(2),
        out_shape=[jax.ShapeDtypeStruct((2, RB, CB), jnp.bfloat16)] * 2,
        cost_estimate=pl.CostEstimate(flops=16 * RB * CB, bytes_accessed=2 << 20, transcendentals=0),
        compiler_params=pltpu.CompilerParams(vmem_limit_bytes=4 << 20),
        name="second_sum",
    )(where, *parts)


def total_kernel(own, near, across_z, far, out):
    near_sum = own[...].astype(jnp.float32) + near[...].astype(jnp.float32)
    far_sum = across_z[...].astype(jnp.float32) + far[...].astype(jnp.float32)
    out[...] = (near_sum + far_sum).astype(jnp.bfloat16)


def total_call(*parts):
    return pl.pallas_call(
        total_kernel,
        in_specs=vmem(4),
        out_specs=vmem(1)[0],
        out_shape=jax.ShapeDtypeStruct((2, RB, CB), jnp.bfloat16),
        cost_estimate=pl.CostEstimate(flops=8 * RB * CB, bytes_accessed=1 << 20, transcendentals=0),
        compiler_params=pltpu.CompilerParams(vmem_limit_bytes=4 << 20),
        name="total",
    )(*parts)


def join_kernel(*refs):
    for k, ref in zip(RING, refs[:4]):
        refs[4][k] = ref[...]


def join_call(parts):
    return pl.pallas_call(
        join_kernel,
        in_specs=vmem(4),
        out_specs=vmem(1)[0],
        out_shape=jax.ShapeDtypeStruct((4, 2, RB, CB), jnp.bfloat16),
        cost_estimate=pl.CostEstimate(flops=0, bytes_accessed=1 << 20, transcendentals=0),
        compiler_params=pltpu.CompilerParams(vmem_limit_bytes=4 << 20),
        name="join",
    )(*parts)


SCALE = bias_first * bias_first / bias_second


def old_kernel(me_ref, ve_ref, mc_ref, vc_ref, m_ref, w_ref, hold):
    hold[...] = jnp.zeros_like(hold)
    for part in range(ROWS // 128):
        rows = slice(part * 128, (part + 1) * 128)
        hold[0:4, :] = jnp.exp2(me_ref[:, rows].astype(jnp.float32)) * (0.9 / 127.0)
        hold[4:8, :] = jnp.exp2(ve_ref[:, rows].astype(jnp.float32)) * (0.999 * SCALE / 255.0)
        unit = hold[...].T
        for cb in range(4):
            cols = slice(cb * CB, (cb + 1) * CB)
            m_ref[rows, cols] = mc_ref[rows, cols].astype(jnp.float32) * unit[:, cb:cb + 1]
            w_ref[rows, cols] = vc_ref[rows, cols].astype(jnp.float32) * unit[:, 4 + cb:5 + cb]


def old_call(m_exp, v_exp, m_code, v_code):
    return pl.pallas_call(
        old_kernel,
        in_specs=vmem(4),
        out_specs=vmem(2),
        out_shape=[jax.ShapeDtypeStruct((ROWS, KH), jnp.float32)] * 2,
        scratch_shapes=[pltpu.VMEM((128, 128), jnp.float32)],
        cost_estimate=pl.CostEstimate(flops=4 * ROWS * KH, bytes_accessed=14 << 20, transcendentals=8 * ROWS),
        compiler_params=pltpu.CompilerParams(vmem_limit_bytes=12 << 20),
        name="old",
    )(m_exp.T, v_exp.T, m_code, v_code)


def adam_rows(other, half, read, m_old, w_old, step_ref, mr_ref, vr_ref, keep_scale):
    lane = lax.broadcasted_iota(jnp.int32, (RB, 128), 1)
    for b in range(4):
        rows = slice(b * RB, (b + 1) * RB)
        back = lax.rem(other + 8 - (2 * half + b // 2), 4)
        g = read(back, b % 2).astype(jnp.float32)
        m = m_old[rows, :] + 0.1 * g
        w = w_old[rows, :] + (0.001 * SCALE) * (g * g)
        step_ref[rows, :] = m / (w * lax.rsqrt(w) + 1e-08 * bias_first)
        ms = jnp.max(jnp.abs(m), axis=1, keepdims=True)
        vs = jnp.max(w, axis=1, keepdims=True) * (1.0 / SCALE)
        keep_scale(b, lane, ms, vs)
        mr_ref[rows, :] = (m * (1.0 / (ms + 1e-06))).astype(jnp.bfloat16)
        vr_ref[rows, :] = (w * ((1.0 / SCALE) / (vs + 1e-06))).astype(jnp.bfloat16)


def adam_own_kernel(where, g_ref, m_old, w_old, step_ref, mr_ref, vr_ref, scale_ref):
    _, _, p, other = unpack(where)

    def keep_scale(b, lane, ms, vs):
        scale_ref[b * RB:(b + 1) * RB, :] = jnp.where(lane == p, ms, jnp.where(lane == 4 + p, vs, 0.0))

    adam_rows(
        other, pl.program_id(0), lambda back, zl: g_ref[back, zl],
        m_old, w_old, step_ref, mr_ref, vr_ref, keep_scale,
    )


WIDE = [
    jax.ShapeDtypeStruct((ROWS, KH), jnp.float32),
    jax.ShapeDtypeStruct((ROWS, KH), jnp.bfloat16),
    jax.ShapeDtypeStruct((ROWS, KH), jnp.bfloat16),
]


def adam_own(where, g, old):
    wide = pl.BlockSpec((4 * RB, CB), lambda i, where: (i, (where[0] // 4) % 4))
    thin = pl.BlockSpec((4 * RB, 128), lambda i, where: (i, 0))
    return pl.pallas_call(
        adam_own_kernel,
        grid_spec=pltpu.PrefetchScalarGridSpec(
            num_scalar_prefetch=1,
            grid=(2,),
            in_specs=[pl.BlockSpec((4, 2, RB, CB), lambda i, where: (0, 0, 0, 0)), wide, wide],
            out_specs=[wide, wide, wide, thin],
        ),
        out_shape=WIDE + [jax.ShapeDtypeStruct((ROWS, 128), jnp.float32)],
        cost_estimate=pl.CostEstimate(flops=5 * ROWS * KH, bytes_accessed=4 << 20, transcendentals=ROWS * KH // 2),
        compiler_params=pltpu.CompilerParams(vmem_limit_bytes=10 << 20),
        name="adam_own",
    )(where, g, *old)


def place_of(ks, i, pos):
    k = ks[0]
    for n in range(1, len(ks)):
        k = jnp.where(i < 2 * n, k, ks[n])
    return lax.rem(pos + 4 - k, 4)


def adam_more_kernel(ks, last, where, *refs):
    n = len(ks)
    gs, (m_old, w_old, s0) = refs[:n], refs[n:n + 3]
    step_ref, mr_ref, vr_ref = refs[n + 6:n + 9]
    scales = refs[-1]
    _, _, pos, other = unpack(where)
    i = pl.program_id(0)
    p, half = place_of(ks, i, pos), lax.rem(i, 2)

    @pl.when(i == 0)
    def _():
        scales[...] = s0[...]

    def keep_scale(b, lane, ms, vs):
        rows = pl.ds(pl.multiple_of(half * (4 * RB) + b * RB, 8), RB)
        scales[rows, :] = jnp.where(lane == p, ms, jnp.where(lane == 4 + p, vs, scales[rows, :]))

    def read(back, zl):
        g = gs[0][back, zl]
        for k in range(1, n):
            g = jnp.where(i < 2 * k, g, gs[k][back, zl])
        return g

    adam_rows(other, half, read, m_old, w_old, step_ref, mr_ref, vr_ref, keep_scale)

    if last:
        @pl.when(i == 2 * n - 1)
        def _():
            for part in range(ROWS // 128):
                cols = slice(part * 128, (part + 1) * 128)
                turned = scales[cols, :].T
                refs[n + 9][:, cols] = turned[0:4, :]
                refs[n + 10][:, cols] = turned[4:8, :]


def adam_more(ks, last, where, g, old, s0, done):
    n = len(ks)
    wide = pl.BlockSpec((4 * RB, CB), lambda i, where: (lax.rem(i, 2), place_of(ks, i, (where[0] // 4) % 4)))
    flat = pl.BlockSpec((4, ROWS), lambda i, where: (0, 0))
    tall = pl.BlockSpec((ROWS, 128), lambda i, where: (0, 0))
    whole = pl.BlockSpec((4, 2, RB, CB), lambda i, where: (0, 0, 0, 0))
    scale_shapes = [jax.ShapeDtypeStruct((4, ROWS), jnp.float32)] * 2 if last else [jax.ShapeDtypeStruct((ROWS, 128), jnp.float32)]
    return pl.pallas_call(
        functools.partial(adam_more_kernel, ks, last),
        grid_spec=pltpu.PrefetchScalarGridSpec(
            num_scalar_prefetch=1,
            grid=(2 * n,),
            in_specs=[whole] * n + [wide, wide, tall] + [pl.BlockSpec(memory_space=pl.ANY)] * 3,
            out_specs=[wide, wide, wide] + ([flat, flat] if last else [tall]),
            scratch_shapes=[pltpu.VMEM((ROWS, 128), jnp.float32)] * last,
        ),
        out_shape=WIDE + scale_shapes,
        input_output_aliases={n + 4: 0, n + 5: 1, n + 6: 2},
        cost_estimate=pl.CostEstimate(flops=5 * n * ROWS * KH, bytes_accessed=n * (4 << 20), transcendentals=n * ROWS * KH // 2),
        compiler_params=pltpu.CompilerParams(vmem_limit_bytes=12 << 20),
        name="adam_more",
    )(where, *g, *old, s0, *done)


def dot(a, b):
    return jnp.dot(a, b, preferred_element_type=jnp.float32)


def dot_t(a, b):
    return lax.dot_general(a, b, (((1,), (1,)), ((), ())), preferred_element_type=jnp.float32)


def shard_cols(shard):
    return pl.ds(pl.multiple_of(shard * ROWS, 128), ROWS)


def scale_by_gain(value, gain, shard):
    parts = []
    for part in range(ROWS // 128):
        row = gain[pl.ds(shard * (ROWS // 128) + part, 1), :]
        parts.append(value[:, part * 128:(part + 1) * 128] * row)
    return jnp.concatenate(parts, axis=1)


def half(zh, c, mine, theirs, x, kg, gain, weights, scaled):
    total = dot(mine[:, shard_cols(zh)], weights[0][...]) + dot(theirs[:, shard_cols(zh)], weights[1][...])
    inner = jnp.zeros((T, 1), jnp.float32)
    for k, shard in enumerate((2 * zh + c, 2 * zh + 1 - c)):
        value = scale_by_gain(dot_t(kg[...], weights[k][...]), gain, shard)
        scaled[:, k * ROWS:(k + 1) * ROWS] = value
        inner += jnp.sum(value * x[:, shard_cols(shard)].astype(jnp.float32), axis=1, keepdims=True)
    return total, inner


def near_kernel(where, mine, theirs, x, kg, gain, own, other, keys, inner, scaled):
    c, zh, _, _ = unpack(where)
    keys[...], inner[...] = half(zh, c, mine, theirs, x, kg, gain, (own, other), scaled)


def near_call(where, mine, theirs, tokens, key_grad, gain, own, other):
    return pl.pallas_call(
        near_kernel,
        in_specs=[pl.BlockSpec(memory_space=pltpu.SMEM)] + vmem(7),
        out_specs=vmem(3),
        out_shape=[
            jax.ShapeDtypeStruct((T, KH), jnp.float32),
            jax.ShapeDtypeStruct((T, 1), jnp.float32),
            jax.ShapeDtypeStruct((T, D // 2), jnp.float32),
        ],
        cost_estimate=pl.CostEstimate(flops=2 * T * D * KH, bytes_accessed=18 << 20, transcendentals=0),
        compiler_params=pltpu.CompilerParams(vmem_limit_bytes=12 << 20),
        name="near",
    )(where, mine, theirs, tokens, key_grad, gain, own, other)


def keys_kernel(where, mine, theirs, near, far, far_other, out):
    there = shard_cols(1 - unpack(where)[1])
    total = near[...] + dot(mine[:, there], far[...]) + dot(theirs[:, there], far_other[...])
    out[...] = total.astype(jnp.bfloat16)


def keys_call(where, mine, theirs, near, far, far_other):
    return pl.pallas_call(
        keys_kernel,
        in_specs=[pl.BlockSpec(memory_space=pltpu.SMEM)] + vmem(5),
        out_specs=vmem(1)[0],
        out_shape=jax.ShapeDtypeStruct((T, KH), jnp.bfloat16),
        cost_estimate=pl.CostEstimate(flops=T * D * KH, bytes_accessed=10 << 20, transcendentals=0),
        compiler_params=pltpu.CompilerParams(vmem_limit_bytes=6 << 20),
        name="keys",
    )(where, mine, theirs, near, far, far_other)


def back_kernel(where, x, kg, inv_ref, gain, inner_ref, scaled, far, far_other, out, hold):
    c, zh, _, _ = unpack(where)
    inner = inner_ref[...]
    shards = (2 * (1 - zh) + c, 2 * (1 - zh) + 1 - c)
    for k, (shard, weight) in enumerate(zip(shards, (far, far_other))):
        value = scale_by_gain(dot_t(kg[...], weight[...]), gain, shard)
        hold[:, k * ROWS:(k + 1) * ROWS] = value
        inner += jnp.sum(value * x[:, shard_cols(shard)].astype(jnp.float32), axis=1, keepdims=True)
    inv = inv_ref[...]
    pull = inv * inv * inv * (inner * (1.0 / D))
    for source, shards in ((scaled, (2 * zh + c, 2 * zh + 1 - c)), (hold, shards)):
        for k, shard in enumerate(shards):
            xf = x[:, shard_cols(shard)].astype(jnp.float32)
            value = inv * source[:, k * ROWS:(k + 1) * ROWS] - xf * pull
            out[:, shard_cols(shard)] = value.astype(jnp.bfloat16)


def back_call(where, tokens, key_grad, inv, gain, inner, scaled, far, far_other):
    return pl.pallas_call(
        back_kernel,
        in_specs=[pl.BlockSpec(memory_space=pltpu.SMEM)] + vmem(8),
        out_specs=vmem(1)[0],
        out_shape=jax.ShapeDtypeStruct((T, D), jnp.bfloat16),
        scratch_shapes=[pltpu.VMEM((T, D // 2), jnp.float32)],
        cost_estimate=pl.CostEstimate(flops=T * D * KH, bytes_accessed=16 << 20, transcendentals=0),
        compiler_params=pltpu.CompilerParams(vmem_limit_bytes=14 << 20),
        name="back",
    )(where, tokens, key_grad, inv, gain, inner, scaled, far, far_other)


def device_step(tokens, gain, key_grad, weight, m_code, m_exp, v_code, v_exp):
    zh, c = lax.axis_index("zh"), lax.axis_index("c")
    y, x = lax.axis_index("y"), lax.axis_index("x")
    pos = jnp.where(c == 0, x, y)
    pos_other = jnp.where(c == 0, y, x)
    where = (c + 2 * zh + 4 * pos + 16 * pos_other).astype(jnp.int32).reshape(1)

    gain = gain.reshape(D // 128, 128)

    far = send(weight, across)
    kg_other = send(key_grad, partner)
    w_other = send(weight, partner)

    theirs, inv, tokens, gain = norm_call(where, tokens, gain)
    received = send(theirs, partner)
    mine, mine_t = mine_call(where, tokens, inv, gain)
    received_t, part2 = grad_call((2,), where, mine_t, received, key_grad, kg_other, first=True)
    part2 = send(part2, around(2))
    part1, part3 = grad_call((1, 3), where, mine_t, received_t, key_grad, kg_other)
    part1, part3 = send(part1, around(1)), send(part3, around(3))
    part0, = grad_call((0,), where, mine_t, received_t, key_grad, kg_other, dtype=jnp.float32)
    parts = [part0, part1, part3, part2]
    near_keys, inner, scaled = near_call(where, mine, theirs, tokens, key_grad, gain, weight, w_other)
    old = old_call(m_exp, v_exp, m_code, v_code)
    parts = list(first_sum(parts))
    far_other = send(far, partner)
    parts = [parts[0]] + [send(parts[k], around(k, True)) for k in RING[1:]]
    keys = keys_call(where, mine, theirs, near_keys, far, far_other)
    keep, give = second_sum(where, parts)
    near = send(keep, zl_partner)
    across_z = send(give, across)
    opposite_z = send(give, opposite)
    total = total_call(keep, near, across_z, opposite_z)

    total = join_call([total] + send_ring(total, True))
    got = send_ring(total, False)
    *done, scales = adam_own(where, total, old)
    token_grad = back_call(where, tokens, key_grad, inv, gain, inner, scaled, far, far_other)
    outs = adam_more(RING[1:], True, where, got, old, scales, done)
    step, m_rel, v_rel, m_scale, v_scale = outs
    return keys, token_grad, step, m_rel, m_scale.T, v_rel, v_scale.T


def solution(mesh):
    inner = Mesh(mesh.devices.reshape(2, 2, 4, 4, 2), AXES)
    tok = P(AXES, None)
    row = P(("zh", "c"), None)

    return jax.shard_map(
        device_step,
        mesh=inner,
        in_specs=(tok, P(None), tok, row, row, row, row, row),
        out_specs=(tok, tok, row, row, row, row, row),
        check_vma=False,
    )
```

time: 127 us -> 129 us (1.016)
  the two profiles are of different devices: /device:TPU:68 before, /device:TPU:36 now
where the time goes in v1:
time: 129 us
  waiting for transfers between devices  60.8 us (47%)
  Pallas kernels  35.6 us (28%)
  starting transfers between devices  31.1 us (24%)
    ppermute x20, waiting for transfers between devices, send(): return lax.ppermute(value, AXES, pairs(move))  60.8 us
    ppermute x20, starting transfers between devices, send(): return lax.ppermute(value, AXES, pairs(move))  31.1 us
    pallas_call x1, Pallas kernels, near_call(): pl.pallas_call(near_kernel, in_specs=[pl.BlockSpec(memory_space=pltpu.SME...  6.08 us
    pallas_call x1, Pallas kernels, adam_more(): pl.pallas_call(functools.partial(adam_more_kernel, ks, last), grid_spec=p...  5.63 us
    pallas_call x1, Pallas kernels, back_call(): pl.pallas_call(back_kernel, in_specs=[pl.BlockSpec(memory_space=pltpu.SME...  5.59 us
    pallas_call x3, Pallas kernels, grad_call(): pl.pallas_call(first_grad_kernel if first else functools.partial(grad_ker...  5.46 us
    pallas_call x1, Pallas kernels, norm_call(): pl.pallas_call(norm_kernel, in_specs=[pl.BlockSpec(memory_space=pltpu.SME...  3.82 us
    pallas_call x1, Pallas kernels, keys_call(): pl.pallas_call(keys_kernel, in_specs=[pl.BlockSpec(memory_space=pltpu.SME...  3.1 us
  transfers between devices with their start and end apart: 20, of which 12 were waited for; matrix products, arithmetic and copies ran while one was open for 0% of the time, Pallas kernels for 21%

profile of v1, /device:TPU:36, one launch (start us, length us, event | category | flops | bytes accessed | tf_op | source)
XLA Modules:
  0.0 129.0 jit_solution(13365845155616193264)
XLA Ops:
  0.6 2.0 %collective-permute-start.1 = (bf16[1152,1024]{1,0:T(8,128)(2,1)}, bf16[1152,1024]{1,0:T(8,128)(2,1)S(1)}, u32[]{:S(2)}, u32[]{:S(2)}) collective-permute-start(bf16[1152,1024]{1,0:T(8,128)(2,1)} %own.1), channel_id=1, source_target_pairs={{0,65},{1,64},{2,67},{3,66},{4,69},{5,68},{6,71},{7,70},{8,73},{9,... | collective-permute-start | bytes 7077896 | tf_op jit(solution)/shard_map/ppermute | solution.py:66
  3.4 3.8 %norm.1 = (bf16[384,2304]{1,0:T(8,128)(2,1)S(1)}, f32[384,1]{1,0:T(8,128)S(1)}, bf16[384,4608]{1,0:T(8,128)(2,1)S(1)}, f32[36,128]{1,0:T(8,128)S(1)}) custom-call(s32[1]{0:T(128)} %bitcast.where, bf16[384,4608]{1,0:T(8,128)(2,1)} %x_hbm.1, f32[36,128]{1,0:T(8,128)S(1)} %bitcast.6), custom_call_target="tpu_custom_call" | custom-call | flops 7077888 | bytes 7077888 | tf_op jit(solution)/shard_map/norm/pallas_call | solution.py:111
  7.9 1.4 %mine.1 = (bf16[384,2304]{1,0:T(8,128)(2,1)S(1)}, bf16[2304,384]{1,0:T(8,128)(2,1)S(1)}) custom-call(s32[1]{0:T(128)} %bitcast.where, bf16[384,4608]{1,0:T(8,128)(2,1)S(1)} %get-tuple-element.37.x, f32[384,1]{1,0:T(8,128)S(1)} %get-tuple-element.38.inv.inv_ref, f32[36,128]{1,0:T(8,128)S(1)} %get-tuple-element.39.gain), custom_call_target="tpu_custom_call" | custom-call | flops 3538944 | bytes 5308416 | tf_op jit(solution)/shard_map/mine/pallas_call | solution.py:141
  9.3 2.8 %collective-permute-done.4.kb_ref.refs_3_ = bf16[384,1024]{1,0:T(8,128)(2,1)S(1)} collective-permute-done((bf16[384,1024]{1,0:T(8,128)(2,1)S(1)}, bf16[384,1024]{1,0:T(8,128)(2,1)S(1)}, u32[]{:S(2)}, u32[]{:S(2)}) %collective-permute-start.4) | collective-permute-done | bytes 786464 | tf_op jit(solution)/shard_map/ppermute | solution.py:66
  12.1 1.4 %grad.3 = (bf16[2304,384]{1,0:T(8,128)(2,1)S(1)}, bf16[4,2,2,144,256]{4,3,2,1,0:T(8,128)(2,1)S(1)}) custom-call(s32[1]{0:T(128)} %bitcast.where, bf16[2304,384]{1,0:T(8,128)(2,1)S(1)} %get-tuple-element.45.a_ref.refs_0_, bf16[384,2304]{1,0:T(8,128)(2,1)S(1)} %collective-permute-done.3.b_in, bf16[384,1024]{1,0:T(8,128)(2,1)S(1)} %copy-done, ...), custom_call_target="tpu_custom_call" | custom-call | flops 905969664 | bytes 6291456 | tf_op jit(solution)/shard_map/grad/pallas_call | solution.py:179
  14.1 2.6 %grad.5 = (bf16[4,2,2,144,256]{4,3,2,1,0:T(8,128)(2,1)S(1)}, bf16[4,2,2,144,256]{4,3,2,1,0:T(8,128)(2,1)S(1)}) custom-call(s32[1]{0:T(128)} %bitcast.where, bf16[2304,384]{1,0:T(8,128)(2,1)S(1)} %get-tuple-element.45.a_ref.refs_0_, bf16[2304,384]{1,0:T(8,128)(2,1)S(1)} %get-tuple-element.46.refs_1_, bf16[384,1024]{1,0:T(8,128)(2,1)S(1)} %copy-done, ...), custom_call_target="tpu_custom_call" | custom-call | flops 1811939328 | bytes 6291456 | tf_op jit(solution)/shard_map/grad/pallas_call | solution.py:179
  16.8 2.2 %collective-permute-start.5 = (bf16[4,2,2,144,256]{4,3,2,1,0:T(8,128)(2,1)S(1)}, bf16[4,2,2,144,256]{4,3,2,1,0:T(8,128)(2,1)S(1)}, u32[]{:S(2)}, u32[]{:S(2)}) collective-permute-start(bf16[4,2,2,144,256]{4,3,2,1,0:T(8,128)(2,1)S(1)} %get-tuple-element.47), channel_id=1, source_target_pairs={{0,2},{1,3},{2,4},{3,5},{4,6},{5,7},{6,0},{7,1},{8,10},{9,11},{10,... | collective-permute-start | bytes 3538952 | tf_op jit(solution)/shard_map/ppermute | solution.py:66
  19.1 35.0 %collective-permute-done.1.far = bf16[1152,1024]{1,0:T(8,128)(2,1)S(1)} collective-permute-done((bf16[1152,1024]{1,0:T(8,128)(2,1)}, bf16[1152,1024]{1,0:T(8,128)(2,1)S(1)}, u32[]{:S(2)}, u32[]{:S(2)}) %collective-permute-start.1) | collective-permute-done | bytes 2359328 | tf_op jit(solution)/shard_map/ppermute | solution.py:66
  54.1 1.4 %grad.4.refs_0_ = f32[4,2,2,144,256]{4,3,2,1,0:T(8,128)S(1)} custom-call(s32[1]{0:T(128)} %bitcast.where, bf16[2304,384]{1,0:T(8,128)(2,1)S(1)} %get-tuple-element.45.a_ref.refs_0_, bf16[2304,384]{1,0:T(8,128)(2,1)S(1)} %get-tuple-element.46.refs_1_, bf16[384,1024]{1,0:T(8,128)(2,1)S(1)} %copy-done, bf16[384,1024]{1,0:T(8,128)(2,1)S(1)} %collective-permute-done.4.kb_ref.refs_3_), custom_call_target="tpu_custom_call" | custom-call | flops 905969664 | bytes 6291456 | tf_op jit(solution)/shard_map/grad/pallas_call | solution.py:179
  56.1 1.6 %collective-permute-start.8 = (bf16[2,2,144,256]{3,2,1,0:T(8,128)(2,1)S(1)}, bf16[2,2,144,256]{3,2,1,0:T(8,128)(2,1)S(1)}, u32[]{:S(2)}, u32[]{:S(2)}) collective-permute-start(bf16[2,2,144,256]{3,2,1,0:T(8,128)(2,1)S(1)} %get-tuple-element.51), channel_id=1, source_target_pairs={{0,8},{1,9},{2,10},{3,11},{4,12},{5,13},{6,14},{7,15},{8,16},{9,17... | collective-permute-start | bytes 884744 | tf_op jit(solution)/shard_map/ppermute | solution.py:66
  57.7 1.7 %collective-permute-start.9 = (bf16[2,2,144,256]{3,2,1,0:T(8,128)(2,1)S(1)}, bf16[2,2,144,256]{3,2,1,0:T(8,128)(2,1)S(1)}, u32[]{:S(2)}, u32[]{:S(2)}) collective-permute-start(bf16[2,2,144,256]{3,2,1,0:T(8,128)(2,1)S(1)} %get-tuple-element.52), channel_id=1, source_target_pairs={{0,24},{1,25},{2,26},{3,27},{4,28},{5,29},{6,30},{7,31},{8,0},{9,1... | collective-permute-start | bytes 884744 | tf_op jit(solution)/shard_map/ppermute | solution.py:66
  59.4 2.0 %collective-permute-start.10 = (bf16[2,2,144,256]{3,2,1,0:T(8,128)(2,1)S(1)}, bf16[2,2,144,256]{3,2,1,0:T(8,128)(2,1)S(1)}, u32[]{:S(2)}, u32[]{:S(2)}) collective-permute-start(bf16[2,2,144,256]{3,2,1,0:T(8,128)(2,1)S(1)} %get-tuple-element.53), channel_id=1, source_target_pairs={{0,16},{1,17},{2,18},{3,19},{4,20},{5,21},{6,22},{7,23},{8,24},{9,... | collective-permute-start | bytes 884744 | tf_op jit(solution)/shard_map/ppermute | solution.py:66
  61.4 2.7 %collective-permute-done.8.refs_1_ = bf16[2,2,144,256]{3,2,1,0:T(8,128)(2,1)S(1)} collective-permute-done((bf16[2,2,144,256]{3,2,1,0:T(8,128)(2,1)S(1)}, bf16[2,2,144,256]{3,2,1,0:T(8,128)(2,1)S(1)}, u32[]{:S(2)}, u32[]{:S(2)}) %collective-permute-start.8) | collective-permute-done | bytes 294944 | tf_op jit(solution)/shard_map/ppermute | solution.py:66
  64.4 4.0 %collective-permute-done.10.refs_3_ = bf16[2,2,144,256]{3,2,1,0:T(8,128)(2,1)S(1)} collective-permute-done((bf16[2,2,144,256]{3,2,1,0:T(8,128)(2,1)S(1)}, bf16[2,2,144,256]{3,2,1,0:T(8,128)(2,1)S(1)}, u32[]{:S(2)}, u32[]{:S(2)}) %collective-permute-start.10) | collective-permute-done | bytes 294944 | tf_op jit(solution)/shard_map/ppermute | solution.py:66
  68.6 2.3 %collective-permute-start.11 = (bf16[2,144,256]{2,1,0:T(8,128)(2,1)S(1)}, bf16[2,144,256]{2,1,0:T(8,128)(2,1)S(1)}, u32[]{:S(2)}, u32[]{:S(2)}) collective-permute-start(bf16[2,144,256]{2,1,0:T(8,128)(2,1)S(1)} %get-tuple-element.54.own), channel_id=1, source_target_pairs={{0,1},{1,0},{2,3},{3,2},{4,5},{5,4},{6,7},{7,6},{8,9},{9,8},{10,11... | collective-permute-start | bytes 442376 | tf_op jit(solution)/shard_map/ppermute | solution.py:66
  70.9 2.1 %collective-permute-start.13 = (bf16[2,144,256]{2,1,0:T(8,128)(2,1)S(1)}, bf16[2,144,256]{2,1,0:T(8,128)(2,1)S(1)}, u32[]{:S(2)}, u32[]{:S(2)}) collective-permute-start(bf16[2,144,256]{2,1,0:T(8,128)(2,1)S(1)} %get-tuple-element.55), channel_id=1, source_target_pairs={{0,64},{1,65},{2,66},{3,67},{4,68},{5,69},{6,70},{7,71},{8,72},{9,... | collective-permute-start | bytes 442376 | tf_op jit(solution)/shard_map/ppermute | solution.py:66
  73.3 2.0 %collective-permute-done.11.near = bf16[2,144,256]{2,1,0:T(8,128)(2,1)S(1)} collective-permute-done((bf16[2,144,256]{2,1,0:T(8,128)(2,1)S(1)}, bf16[2,144,256]{2,1,0:T(8,128)(2,1)S(1)}, u32[]{:S(2)}, u32[]{:S(2)}) %collective-permute-start.11) | collective-permute-done | bytes 147488 | tf_op jit(solution)/shard_map/ppermute | solution.py:66
  75.3 2.4 %collective-permute-done.13.far = bf16[2,144,256]{2,1,0:T(8,128)(2,1)S(1)} collective-permute-done((bf16[2,144,256]{2,1,0:T(8,128)(2,1)S(1)}, bf16[2,144,256]{2,1,0:T(8,128)(2,1)S(1)}, u32[]{:S(2)}, u32[]{:S(2)}) %collective-permute-start.13) | collective-permute-done | bytes 147488 | tf_op jit(solution)/shard_map/ppermute | solution.py:66
  77.7 1.5 %collective-permute-done.12.across_z = bf16[2,144,256]{2,1,0:T(8,128)(2,1)S(1)} collective-permute-done((bf16[2,144,256]{2,1,0:T(8,128)(2,1)S(1)}, bf16[2,144,256]{2,1,0:T(8,128)(2,1)S(1)}, u32[]{:S(2)}, u32[]{:S(2)}) %collective-permute-start.12) | collective-permute-done | bytes 147488 | tf_op jit(solution)/shard_map/ppermute | solution.py:66
  79.2 2.9 %collective-permute-start.16 = (bf16[2,144,256]{2,1,0:T(8,128)(2,1)S(1)}, bf16[2,144,256]{2,1,0:T(8,128)(2,1)S(1)}, u32[]{:S(2)}, u32[]{:S(2)}) collective-permute-start(bf16[2,144,256]{2,1,0:T(8,128)(2,1)S(1)} %total.1.refs_0_), channel_id=1, source_target_pairs={{0,16},{1,17},{2,18},{3,19},{4,20},{5,21},{6,22},{7,23},{8,24},{9,... | collective-permute-start | bytes 442376 | tf_op jit(solution)/shard_map/ppermute | solution.py:66
  84.1 1.8 %collective-permute-done.16.refs_3_ = bf16[2,144,256]{2,1,0:T(8,128)(2,1)S(1)} collective-permute-done((bf16[2,144,256]{2,1,0:T(8,128)(2,1)S(1)}, bf16[2,144,256]{2,1,0:T(8,128)(2,1)S(1)}, u32[]{:S(2)}, u32[]{:S(2)}) %collective-permute-start.16) | collective-permute-done | bytes 147488 | tf_op jit(solution)/shard_map/ppermute | solution.py:66
  87.3 2.4 %collective-permute-done.14.refs_1_ = bf16[2,144,256]{2,1,0:T(8,128)(2,1)S(1)} collective-permute-done((bf16[2,144,256]{2,1,0:T(8,128)(2,1)S(1)}, bf16[2,144,256]{2,1,0:T(8,128)(2,1)S(1)}, u32[]{:S(2)}, u32[]{:S(2)}) %collective-permute-start.14) | collective-permute-done | bytes 147488 | tf_op jit(solution)/shard_map/ppermute | solution.py:66
  89.8 2.3 %collective-permute-start.19 = (bf16[4,2,144,256]{3,2,1,0:T(8,128)(2,1)S(1)}, bf16[4,2,144,256]{3,2,1,0:T(8,128)(2,1)S(1)}, u32[]{:S(2)}, u32[]{:S(2)}) collective-permute-start(bf16[4,2,144,256]{3,2,1,0:T(8,128)(2,1)S(1)} %join.1.g_ref), channel_id=1, source_target_pairs={{0,4},{1,5},{2,6},{3,7},{4,0},{5,1},{6,2},{7,3},{8,12},{9,13},{10,... | collective-permute-start | bytes 1769480 | tf_op jit(solution)/shard_map/ppermute | solution.py:66
  92.1 6.4 %collective-permute-start.18 = (bf16[4,2,144,256]{3,2,1,0:T(8,128)(2,1)S(1)}, bf16[4,2,144,256]{3,2,1,0:T(8,128)(2,1)S(1)}, u32[]{:S(2)}, u32[]{:S(2)}) collective-permute-start(bf16[4,2,144,256]{3,2,1,0:T(8,128)(2,1)S(1)} %join.1.g_ref), channel_id=1, source_target_pairs={{0,6},{1,7},{2,0},{3,1},{4,2},{5,3},{6,4},{7,5},{8,14},{9,15},{10,... | collective-permute-start | bytes 1769480 | tf_op jit(solution)/shard_map/ppermute | solution.py:66
  98.5 2.0 %collective-permute-start.17 = (bf16[4,2,144,256]{3,2,1,0:T(8,128)(2,1)S(1)}, bf16[4,2,144,256]{3,2,1,0:T(8,128)(2,1)S(1)}, u32[]{:S(2)}, u32[]{:S(2)}) collective-permute-start(bf16[4,2,144,256]{3,2,1,0:T(8,128)(2,1)S(1)} %join.1.g_ref), channel_id=1, source_target_pairs={{0,2},{1,3},{2,4},{3,5},{4,6},{5,7},{6,0},{7,1},{8,10},{9,11},{10,... | collective-permute-start | bytes 1769480 | tf_op jit(solution)/shard_map/ppermute | solution.py:66
  100.5 1.6 %old.1 = (f32[1152,1024]{1,0:T(8,128)S(1)}, f32[1152,1024]{1,0:T(8,128)S(1)}) custom-call(s32[4,1152]{1,0:T(4,128)S(1)} %bitcast.7, s32[4,1152]{1,0:T(4,128)S(1)} %bitcast.8, bf16[1152,1024]{1,0:T(8,128)(2,1)S(1)} %copy-done.1, bf16[1152,1024]{1,0:T(8,128)(2,1)S(1)} %copy-done.2), custom_call_target="tpu_custom_call" | custom-call | flops 4718592 | bytes 14680064 | tf_op jit(solution)/shard_map/old/pallas_call | solution.py:284
  102.1 6.1 %near.1 = (f32[384,1024]{1,0:T(8,128)S(1)}, f32[384,1]{1,0:T(8,128)S(1)}, f32[384,2304]{1,0:T(8,128)S(1)}) custom-call(s32[1]{0:T(128)} %bitcast.where, bf16[384,2304]{1,0:T(8,128)(2,1)S(1)} %get-tuple-element.40.mine, bf16[384,2304]{1,0:T(8,128)(2,1)S(1)} %get-tuple-element.41.theirs, bf16[384,4608]{1,0:T(8,128)(2,1)S(1)} %get-tuple-element.37.x, ...), custom_call_target="tpu_custom_call" | custom-call | flops 3623878656 | bytes 18874368 | tf_op jit(solution)/shard_map/near/pallas_call | solution.py:451
  108.2 2.1 %adam_own.1 = (f32[1152,1024]{1,0:T(8,128)}, bf16[1152,1024]{1,0:T(8,128)(2,1)}, bf16[1152,1024]{1,0:T(8,128)(2,1)}, f32[1152,128]{1,0:T(8,128)S(1)}) custom-call(s32[1]{0:T(128)} %bitcast.where, bf16[4,2,144,256]{3,2,1,0:T(8,128)(2,1)S(1)} %join.1.g_ref, f32[1152,1024]{1,0:T(8,128)S(1)} %get-tuple-element.56.m_old.refs_3_, ...), custom_call_target="tpu_custom_call" | custom-call | flops 5898240 | bytes 4194304 | tf_op jit(solution)/shard_map/adam_own/pallas_call | solution.py:334
  110.3 4.4 %collective-permute-done.18.refs_1_ = bf16[4,2,144,256]{3,2,1,0:T(8,128)(2,1)S(1)} collective-permute-done((bf16[4,2,144,256]{3,2,1,0:T(8,128)(2,1)S(1)}, bf16[4,2,144,256]{3,2,1,0:T(8,128)(2,1)S(1)}, u32[]{:S(2)}, u32[]{:S(2)}) %collective-permute-start.18) | collective-permute-done | bytes 589856 | tf_op jit(solution)/shard_map/ppermute | solution.py:66
  114.7 5.6 %adam_more.1 = (f32[1152,1024]{1,0:T(8,128)}, bf16[1152,1024]{1,0:T(8,128)(2,1)}, bf16[1152,1024]{1,0:T(8,128)(2,1)}, f32[4,1152]{1,0:T(4,128)}, f32[4,1152]{1,0:T(4,128)}) custom-call(s32[1]{0:T(128)} %bitcast.where, bf16[4,2,144,256]{3,2,1,0:T(8,128)(2,1)S(1)} %collective-permute-done.17.refs_0_, ...), custom_call_target="tpu_custom_call", output_to_operand_aliasing={{0}: (7, {}), {1}: (8, {}), {2}: (9, {})} | custom-call | flops 17694720 | bytes 12582912 | tf_op jit(solution)/shard_map/adam_more/pallas_call | solution.py:398
  120.3 3.1 %keys.1 = bf16[384,1024]{1,0:T(8,128)(2,1)} custom-call(s32[1]{0:T(128)} %bitcast.where, bf16[384,2304]{1,0:T(8,128)(2,1)S(1)} %get-tuple-element.40.mine, bf16[384,2304]{1,0:T(8,128)(2,1)S(1)} %get-tuple-element.41.theirs, f32[384,1024]{1,0:T(8,128)S(1)} %get-tuple-element.42.near, bf16[1152,1024]{1,0:T(8,128)(2,1)S(1)} %collective-permute-done.1.far, ...), custom_call_target="tpu_custom_call" | custom-call | flops 1811939328 | bytes 10485760 | tf_op jit(solution)/shard_map/keys/pallas_call | solution.py:473
  123.4 5.6 %back.1 = bf16[384,4608]{1,0:T(8,128)(2,1)} custom-call(s32[1]{0:T(128)} %bitcast.where, bf16[384,4608]{1,0:T(8,128)(2,1)S(1)} %get-tuple-element.37.x, bf16[384,1024]{1,0:T(8,128)(2,1)S(1)} %copy-done, f32[384,1]{1,0:T(8,128)S(1)} %get-tuple-element.38.inv.inv_ref, f32[36,128]{1,0:T(8,128)S(1)} %get-tuple-element.39.gain, ...), custom_call_target="tpu_custom_call" | custom-call | flops 1811939328 | bytes 16777216 | tf_op jit(solution)/shard_map/back/pallas_call | solution.py:502
  (35 shorter events, 7.0 us)
Async XLA Ops:
  0.6 6.7 %copy-start = (bf16[384,1024]{1,0:T(8,128)(2,1)S(1)}, bf16[384,1024]{1,0:T(8,128)(2,1)}, u32[]{:S(2)}) copy-start(bf16[384,1024]{1,0:T(8,128)(2,1)} %refs_2_.3) | copy-start | bytes 2359300
  0.6 53.5 %collective-permute-start.1 = (bf16[1152,1024]{1,0:T(8,128)(2,1)}, bf16[1152,1024]{1,0:T(8,128)(2,1)S(1)}, u32[]{:S(2)}, u32[]{:S(2)}) collective-permute-start(bf16[1152,1024]{1,0:T(8,128)(2,1)} %own.1), channel_id=1, source_target_pairs={{0,65},{1,64},{2,67},{3,66},{4,69},{5,68},{6,71},{7,70},{8,73},{9,... | collective-permute-start | bytes 7077896 | tf_op jit(solution)/shard_map/ppermute | solution.py:66
  2.6 0.7 copy-start.3
  7.2 4.9 %collective-permute-start.3 = (bf16[384,2304]{1,0:T(8,128)(2,1)S(1)}, bf16[384,2304]{1,0:T(8,128)(2,1)S(1)}, u32[]{:S(2)}, u32[]{:S(2)}) collective-permute-start(bf16[384,2304]{1,0:T(8,128)(2,1)S(1)} %get-tuple-element.41.theirs), channel_id=1, source_target_pairs={{0,32},{1,33},{2,34},{3,35},{4,36},{5,37},{6,38},{7,39},{8,40},{9,... | collective-permute-start | bytes 5308424 | tf_op jit(solution)/shard_map/ppermute | solution.py:66
  7.3 4.8 %collective-permute-start.4 = (bf16[384,1024]{1,0:T(8,128)(2,1)S(1)}, bf16[384,1024]{1,0:T(8,128)(2,1)S(1)}, u32[]{:S(2)}, u32[]{:S(2)}) collective-permute-start(bf16[384,1024]{1,0:T(8,128)(2,1)S(1)} %copy-done), channel_id=1, source_target_pairs={{0,32},{1,33},{2,34},{3,35},{4,36},{5,37},{6,38},{7,39},{8,40},{9,... | collective-permute-start | bytes 2359304 | tf_op jit(solution)/shard_map/ppermute | solution.py:66
  7.8 94.3 %collective-permute-start = (bf16[1152,1024]{1,0:T(8,128)(2,1)}, bf16[1152,1024]{1,0:T(8,128)(2,1)S(1)}, u32[]{:S(2)}, u32[]{:S(2)}) collective-permute-start(bf16[1152,1024]{1,0:T(8,128)(2,1)} %own.1), channel_id=1, source_target_pairs={{0,32},{1,33},{2,34},{3,35},{4,36},{5,37},{6,38},{7,39},{8,40},{9,... | collective-permute-start | bytes 7077896 | tf_op jit(solution)/shard_map/ppermute | solution.py:66
  13.5 42.0 %collective-permute-start.7 = (bf16[4,2,2,144,256]{4,3,2,1,0:T(8,128)(2,1)S(1)}, bf16[4,2,2,144,256]{4,3,2,1,0:T(8,128)(2,1)S(1)}, u32[]{:S(2)}, u32[]{:S(2)}) collective-permute-start(bf16[4,2,2,144,256]{4,3,2,1,0:T(8,128)(2,1)S(1)} %get-tuple-element.49), channel_id=1, source_target_pairs={{0,4},{1,5},{2,6},{3,7},{4,0},{5,1},{6,2},{7,3},{8,12},{9,13},{10,... | collective-permute-start | bytes 3538952 | tf_op jit(solution)/shard_map/ppermute | solution.py:66
  16.8 38.8 %collective-permute-start.5 = (bf16[4,2,2,144,256]{4,3,2,1,0:T(8,128)(2,1)S(1)}, bf16[4,2,2,144,256]{4,3,2,1,0:T(8,128)(2,1)S(1)}, u32[]{:S(2)}, u32[]{:S(2)}) collective-permute-start(bf16[4,2,2,144,256]{4,3,2,1,0:T(8,128)(2,1)S(1)} %get-tuple-element.47), channel_id=1, source_target_pairs={{0,2},{1,3},{2,4},{3,5},{4,6},{5,7},{6,0},{7,1},{8,10},{9,11},{10,... | collective-permute-start | bytes 3538952 | tf_op jit(solution)/shard_map/ppermute | solution.py:66
  18.9 36.6 %collective-permute-start.6 = (bf16[4,2,2,144,256]{4,3,2,1,0:T(8,128)(2,1)S(1)}, bf16[4,2,2,144,256]{4,3,2,1,0:T(8,128)(2,1)S(1)}, u32[]{:S(2)}, u32[]{:S(2)}) collective-permute-start(bf16[4,2,2,144,256]{4,3,2,1,0:T(8,128)(2,1)S(1)} %get-tuple-element.48), channel_id=1, source_target_pairs={{0,6},{1,7},{2,0},{3,1},{4,2},{5,3},{6,4},{7,5},{8,14},{9,15},{10,... | collective-permute-start | bytes 3538952 | tf_op jit(solution)/shard_map/ppermute | solution.py:66
  54.1 66.2 %collective-permute-start.2 = (bf16[1152,1024]{1,0:T(8,128)(2,1)S(1)}, bf16[1152,1024]{1,0:T(8,128)(2,1)S(1)}, u32[]{:S(2)}, u32[]{:S(2)}) collective-permute-start(bf16[1152,1024]{1,0:T(8,128)(2,1)S(1)} %collective-permute-done.1.far), channel_id=1, source_target_pairs={{0,32},{1,33},{2,34},{3,35},{4,36},{5,37},{6,38},{7,39},{8,40},{9,... | collective-permute-start | bytes 7077896 | tf_op jit(solution)/shard_map/ppermute | solution.py:66
  55.5 44.9 %copy-start.2 = (bf16[1152,1024]{1,0:T(8,128)(2,1)S(1)}, bf16[1152,1024]{1,0:T(8,128)(2,1)}, u32[]{:S(2)}) copy-start(bf16[1152,1024]{1,0:T(8,128)(2,1)} %vc_ref.1) | copy-start | bytes 7077892
  56.1 44.4 %copy-start.1 = (bf16[1152,1024]{1,0:T(8,128)(2,1)S(1)}, bf16[1152,1024]{1,0:T(8,128)(2,1)}, u32[]{:S(2)}) copy-start(bf16[1152,1024]{1,0:T(8,128)(2,1)} %mc_ref.1) | copy-start | bytes 7077892
  56.1 44.4 %copy-start.4 = (s32[1152,4]{0,1:T(4,128)S(1)}, s32[1152,4]{0,1:T(4,128)}, u32[]{:S(2)}) copy-start(s32[1152,4]{0,1:T(4,128)} %param.13) | copy-start | bytes 55300
  56.1 44.4 %copy-start.5 = (s32[1152,4]{0,1:T(4,128)S(1)}, s32[1152,4]{0,1:T(4,128)}, u32[]{:S(2)}) copy-start(s32[1152,4]{0,1:T(4,128)} %param.15) | copy-start | bytes 55300
  56.1 8.0 %collective-permute-start.8 = (bf16[2,2,144,256]{3,2,1,0:T(8,128)(2,1)S(1)}, bf16[2,2,144,256]{3,2,1,0:T(8,128)(2,1)S(1)}, u32[]{:S(2)}, u32[]{:S(2)}) collective-permute-start(bf16[2,2,144,256]{3,2,1,0:T(8,128)(2,1)S(1)} %get-tuple-element.51), channel_id=1, source_target_pairs={{0,8},{1,9},{2,10},{3,11},{4,12},{5,13},{6,14},{7,15},{8,16},{9,17... | collective-permute-start | bytes 884744 | tf_op jit(solution)/shard_map/ppermute | solution.py:66
  57.7 6.7 %collective-permute-start.9 = (bf16[2,2,144,256]{3,2,1,0:T(8,128)(2,1)S(1)}, bf16[2,2,144,256]{3,2,1,0:T(8,128)(2,1)S(1)}, u32[]{:S(2)}, u32[]{:S(2)}) collective-permute-start(bf16[2,2,144,256]{3,2,1,0:T(8,128)(2,1)S(1)} %get-tuple-element.52), channel_id=1, source_target_pairs={{0,24},{1,25},{2,26},{3,27},{4,28},{5,29},{6,30},{7,31},{8,0},{9,1... | collective-permute-start | bytes 884744 | tf_op jit(solution)/shard_map/ppermute | solution.py:66
  59.4 9.1 %collective-permute-start.10 = (bf16[2,2,144,256]{3,2,1,0:T(8,128)(2,1)S(1)}, bf16[2,2,144,256]{3,2,1,0:T(8,128)(2,1)S(1)}, u32[]{:S(2)}, u32[]{:S(2)}) collective-permute-start(bf16[2,2,144,256]{3,2,1,0:T(8,128)(2,1)S(1)} %get-tuple-element.53), channel_id=1, source_target_pairs={{0,16},{1,17},{2,18},{3,19},{4,20},{5,21},{6,22},{7,23},{8,24},{9,... | collective-permute-start | bytes 884744 | tf_op jit(solution)/shard_map/ppermute | solution.py:66
  68.6 6.7 %collective-permute-start.11 = (bf16[2,144,256]{2,1,0:T(8,128)(2,1)S(1)}, bf16[2,144,256]{2,1,0:T(8,128)(2,1)S(1)}, u32[]{:S(2)}, u32[]{:S(2)}) collective-permute-start(bf16[2,144,256]{2,1,0:T(8,128)(2,1)S(1)} %get-tuple-element.54.own), channel_id=1, source_target_pairs={{0,1},{1,0},{2,3},{3,2},{4,5},{5,4},{6,7},{7,6},{8,9},{9,8},{10,11... | collective-permute-start | bytes 442376 | tf_op jit(solution)/shard_map/ppermute | solution.py:66
  70.9 6.7 %collective-permute-start.13 = (bf16[2,144,256]{2,1,0:T(8,128)(2,1)S(1)}, bf16[2,144,256]{2,1,0:T(8,128)(2,1)S(1)}, u32[]{:S(2)}, u32[]{:S(2)}) collective-permute-start(bf16[2,144,256]{2,1,0:T(8,128)(2,1)S(1)} %get-tuple-element.55), channel_id=1, source_target_pairs={{0,64},{1,65},{2,66},{3,67},{4,68},{5,69},{6,70},{7,71},{8,72},{9,... | collective-permute-start | bytes 442376 | tf_op jit(solution)/shard_map/ppermute | solution.py:66
  73.0 6.2 %collective-permute-start.12 = (bf16[2,144,256]{2,1,0:T(8,128)(2,1)S(1)}, bf16[2,144,256]{2,1,0:T(8,128)(2,1)S(1)}, u32[]{:S(2)}, u32[]{:S(2)}) collective-permute-start(bf16[2,144,256]{2,1,0:T(8,128)(2,1)S(1)} %get-tuple-element.55), channel_id=1, source_target_pairs={{0,65},{1,64},{2,67},{3,66},{4,69},{5,68},{6,71},{7,70},{8,73},{9,... | collective-permute-start | bytes 442376 | tf_op jit(solution)/shard_map/ppermute | solution.py:66
  79.2 6.7 %collective-permute-start.16 = (bf16[2,144,256]{2,1,0:T(8,128)(2,1)S(1)}, bf16[2,144,256]{2,1,0:T(8,128)(2,1)S(1)}, u32[]{:S(2)}, u32[]{:S(2)}) collective-permute-start(bf16[2,144,256]{2,1,0:T(8,128)(2,1)S(1)} %total.1.refs_0_), channel_id=1, source_target_pairs={{0,16},{1,17},{2,18},{3,19},{4,20},{5,21},{6,22},{7,23},{8,24},{9,... | collective-permute-start | bytes 442376 | tf_op jit(solution)/shard_map/ppermute | solution.py:66
  82.1 5.2 %collective-permute-start.15 = (bf16[2,144,256]{2,1,0:T(8,128)(2,1)S(1)}, bf16[2,144,256]{2,1,0:T(8,128)(2,1)S(1)}, u32[]{:S(2)}, u32[]{:S(2)}) collective-permute-start(bf16[2,144,256]{2,1,0:T(8,128)(2,1)S(1)} %total.1.refs_0_), channel_id=1, source_target_pairs={{0,24},{1,25},{2,26},{3,27},{4,28},{5,29},{6,30},{7,31},{8,0},{9,1... | collective-permute-start | bytes 442376 | tf_op jit(solution)/shard_map/ppermute | solution.py:66
  83.4 6.4 %collective-permute-start.14 = (bf16[2,144,256]{2,1,0:T(8,128)(2,1)S(1)}, bf16[2,144,256]{2,1,0:T(8,128)(2,1)S(1)}, u32[]{:S(2)}, u32[]{:S(2)}) collective-permute-start(bf16[2,144,256]{2,1,0:T(8,128)(2,1)S(1)} %total.1.refs_0_), channel_id=1, source_target_pairs={{0,8},{1,9},{2,10},{3,11},{4,12},{5,13},{6,14},{7,15},{8,16},{9,17... | collective-permute-start | bytes 442376 | tf_op jit(solution)/shard_map/ppermute | solution.py:66
  89.8 20.5 %collective-permute-start.19 = (bf16[4,2,144,256]{3,2,1,0:T(8,128)(2,1)S(1)}, bf16[4,2,144,256]{3,2,1,0:T(8,128)(2,1)S(1)}, u32[]{:S(2)}, u32[]{:S(2)}) collective-permute-start(bf16[4,2,144,256]{3,2,1,0:T(8,128)(2,1)S(1)} %join.1.g_ref), channel_id=1, source_target_pairs={{0,4},{1,5},{2,6},{3,7},{4,0},{5,1},{6,2},{7,3},{8,12},{9,13},{10,... | collective-permute-start | bytes 1769480 | tf_op jit(solution)/shard_map/ppermute | solution.py:66
  92.1 22.6 %collective-permute-start.18 = (bf16[4,2,144,256]{3,2,1,0:T(8,128)(2,1)S(1)}, bf16[4,2,144,256]{3,2,1,0:T(8,128)(2,1)S(1)}, u32[]{:S(2)}, u32[]{:S(2)}) collective-permute-start(bf16[4,2,144,256]{3,2,1,0:T(8,128)(2,1)S(1)} %join.1.g_ref), channel_id=1, source_target_pairs={{0,6},{1,7},{2,0},{3,1},{4,2},{5,3},{6,4},{7,5},{8,14},{9,15},{10,... | collective-permute-start | bytes 1769480 | tf_op jit(solution)/shard_map/ppermute | solution.py:66
  98.5 16.2 %collective-permute-start.17 = (bf16[4,2,144,256]{3,2,1,0:T(8,128)(2,1)S(1)}, bf16[4,2,144,256]{3,2,1,0:T(8,128)(2,1)S(1)}, u32[]{:S(2)}, u32[]{:S(2)}) collective-permute-start(bf16[4,2,144,256]{3,2,1,0:T(8,128)(2,1)S(1)} %join.1.g_ref), channel_id=1, source_target_pairs={{0,2},{1,3},{2,4},{3,5},{4,6},{5,7},{6,0},{7,1},{8,10},{9,11},{10,... | collective-permute-start | bytes 1769480 | tf_op jit(solution)/shard_map/ppermute | solution.py:66

commit v2 on v1

--- a/solution.py
+++ b/solution.py
@@ -110,7 +110,7 @@
 def norm_call(where, tokens, gain):
     return pl.pallas_call(
         norm_kernel,
-        in_specs=[pl.BlockSpec(memory_space=pltpu.SMEM)] + [pl.BlockSpec(memory_space=pl.ANY)] * 2,
+        in_specs=[pl.BlockSpec(memory_space=pltpu.SMEM)] + [pl.BlockSpec(memory_space=pltpu.HBM)] * 2,
         out_specs=vmem(4),
         out_shape=[
             jax.ShapeDtypeStruct((T, D // 2), jnp.bfloat16),
@@ -120,9 +120,9 @@
         ],
         scratch_shapes=[pltpu.SemaphoreType.DMA((T // STEP + 1,))],
         cost_estimate=pl.CostEstimate(flops=4 * T * D, bytes_accessed=4 * T * D, transcendentals=T),
-        compiler_params=pltpu.CompilerParams(vmem_limit_bytes=47 << 20),
+        compiler_params=pltpu.CompilerParams(vmem_limit_bytes=8 << 20),
         name="norm",
-    )(where, tokens, gain)
+    )(where, *(pltpu.with_memory_space_constraint(v, pltpu.HBM) for v in (tokens, gain)))
 
 
 def flip(in_ref, out_ref):

time: 129 us -> 129 us (level)
  waiting for transfers between devices: 60.8 us -> 63.1 us
  Pallas kernels: 35.6 us -> 34 us
    ppermute x20, waiting for transfers between devices: 60.8 us -> 63.1 us  [send(): return lax.ppermute(value, AXES, pairs(move))]
    pallas_call x1, Pallas kernels: 6.08 us -> 4.38 us  [near_call(): pl.pallas_call(near_kernel, in_specs=[pl.BlockSpec(memory_space=pltpu.SME...]
  transfers between devices with their start and end apart: 20 -> 20, of which waited for: 12 -> 12; matrix products, arithmetic and copies ran while one was open for 0% -> 0% of each run, Pallas kernels for 21% -> 20%
where the time goes in v2:
time: 129 us
  waiting for transfers between devices  63.1 us (49%)
  Pallas kernels  34 us (26%)
  starting transfers between devices  31.1 us (24%)
    ppermute x20, waiting for transfers between devices, send(): return lax.ppermute(value, AXES, pairs(move))  63.1 us
    ppermute x20, starting transfers between devices, send(): return lax.ppermute(value, AXES, pairs(move))  31.1 us
    pallas_call x1, Pallas kernels, adam_more(): pl.pallas_call(functools.partial(adam_more_kernel, ks, last), grid_spec=p...  5.63 us
    pallas_call x1, Pallas kernels, back_call(): pl.pallas_call(back_kernel, in_specs=[pl.BlockSpec(memory_space=pltpu.SME...  5.6 us
    pallas_call x3, Pallas kernels, grad_call(): pl.pallas_call(first_grad_kernel if first else functools.partial(grad_ker...  5.45 us
    pallas_call x1, Pallas kernels, near_call(): pl.pallas_call(near_kernel, in_specs=[pl.BlockSpec(memory_space=pltpu.SME...  4.38 us
    pallas_call x1, Pallas kernels, norm_call(): pl.pallas_call(norm_kernel, in_specs=[pl.BlockSpec(memory_space=pltpu.SME...  3.98 us
    pallas_call x1, Pallas kernels, keys_call(): pl.pallas_call(keys_kernel, in_specs=[pl.BlockSpec(memory_space=pltpu.SME...  3.1 us
  transfers between devices with their start and end apart: 20, of which 12 were waited for; matrix products, arithmetic and copies ran while one was open for 0% of the time, Pallas kernels for 20%

profile of v2, /device:TPU:36, one launch (start us, length us, event | category | flops | bytes accessed | tf_op | source)
XLA Modules:
  0.0 129.0 jit_solution(18114298268628324570)
XLA Ops:
  0.6 2.0 %collective-permute-start.1 = (bf16[1152,1024]{1,0:T(8,128)(2,1)}, bf16[1152,1024]{1,0:T(8,128)(2,1)S(1)}, u32[]{:S(2)}, u32[]{:S(2)}) collective-permute-start(bf16[1152,1024]{1,0:T(8,128)(2,1)} %own.1), channel_id=1, source_target_pairs={{0,65},{1,64},{2,67},{3,66},{4,69},{5,68},{6,71},{7,70},{8,73},{9,... | collective-permute-start | bytes 7077896 | tf_op jit(solution)/shard_map/ppermute | solution.py:66
  2.6 4.0 %norm.1 = (bf16[384,2304]{1,0:T(8,128)(2,1)S(1)}, f32[384,1]{1,0:T(8,128)S(1)}, bf16[384,4608]{1,0:T(8,128)(2,1)S(1)}, f32[36,128]{1,0:T(8,128)S(1)}) custom-call(s32[1]{0:T(128)} %bitcast.where, bf16[384,4608]{1,0:T(8,128)(2,1)} %x_hbm.1, f32[36,128]{1,0:T(8,128)} %bitcast.8), custom_call_target="tpu_custom_call" | custom-call | flops 7077888 | bytes 7077888 | tf_op jit(solution)/shard_map/norm/pallas_call | solution.py:111
  7.3 1.4 %mine.1 = (bf16[384,2304]{1,0:T(8,128)(2,1)S(1)}, bf16[2304,384]{1,0:T(8,128)(2,1)S(1)}) custom-call(s32[1]{0:T(128)} %bitcast.where, bf16[384,4608]{1,0:T(8,128)(2,1)S(1)} %get-tuple-element.37.x, f32[384,1]{1,0:T(8,128)S(1)} %get-tuple-element.38.inv.inv_ref, f32[36,128]{1,0:T(8,128)S(1)} %get-tuple-element.39.gain), custom_call_target="tpu_custom_call" | custom-call | flops 3538944 | bytes 5308416 | tf_op jit(solution)/shard_map/mine/pallas_call | solution.py:141
  8.8 2.8 %collective-permute-done.4.kb_ref.refs_3_ = bf16[384,1024]{1,0:T(8,128)(2,1)S(1)} collective-permute-done((bf16[384,1024]{1,0:T(8,128)(2,1)S(1)}, bf16[384,1024]{1,0:T(8,128)(2,1)S(1)}, u32[]{:S(2)}, u32[]{:S(2)}) %collective-permute-start.4) | collective-permute-done | bytes 786464 | tf_op jit(solution)/shard_map/ppermute | solution.py:66
  11.5 1.4 %grad.3 = (bf16[2304,384]{1,0:T(8,128)(2,1)S(1)}, bf16[4,2,2,144,256]{4,3,2,1,0:T(8,128)(2,1)S(1)}) custom-call(s32[1]{0:T(128)} %bitcast.where, bf16[2304,384]{1,0:T(8,128)(2,1)S(1)} %get-tuple-element.45.a_ref.refs_0_, bf16[384,2304]{1,0:T(8,128)(2,1)S(1)} %collective-permute-done.3.b_in, bf16[384,1024]{1,0:T(8,128)(2,1)S(1)} %copy-done, ...), custom_call_target="tpu_custom_call" | custom-call | flops 905969664 | bytes 6291456 | tf_op jit(solution)/shard_map/grad/pallas_call | solution.py:179
  13.6 2.6 %grad.5 = (bf16[4,2,2,144,256]{4,3,2,1,0:T(8,128)(2,1)S(1)}, bf16[4,2,2,144,256]{4,3,2,1,0:T(8,128)(2,1)S(1)}) custom-call(s32[1]{0:T(128)} %bitcast.where, bf16[2304,384]{1,0:T(8,128)(2,1)S(1)} %get-tuple-element.45.a_ref.refs_0_, bf16[2304,384]{1,0:T(8,128)(2,1)S(1)} %get-tuple-element.46.refs_1_, bf16[384,1024]{1,0:T(8,128)(2,1)S(1)} %copy-done, ...), custom_call_target="tpu_custom_call" | custom-call | flops 1811939328 | bytes 6291456 | tf_op jit(solution)/shard_map/grad/pallas_call | solution.py:179
  16.2 2.2 %collective-permute-start.5 = (bf16[4,2,2,144,256]{4,3,2,1,0:T(8,128)(2,1)S(1)}, bf16[4,2,2,144,256]{4,3,2,1,0:T(8,128)(2,1)S(1)}, u32[]{:S(2)}, u32[]{:S(2)}) collective-permute-start(bf16[4,2,2,144,256]{4,3,2,1,0:T(8,128)(2,1)S(1)} %get-tuple-element.47), channel_id=1, source_target_pairs={{0,2},{1,3},{2,4},{3,5},{4,6},{5,7},{6,0},{7,1},{8,10},{9,11},{10,... | collective-permute-start | bytes 3538952 | tf_op jit(solution)/shard_map/ppermute | solution.py:66
  18.5 35.6 %collective-permute-done.1.far = bf16[1152,1024]{1,0:T(8,128)(2,1)S(1)} collective-permute-done((bf16[1152,1024]{1,0:T(8,128)(2,1)}, bf16[1152,1024]{1,0:T(8,128)(2,1)S(1)}, u32[]{:S(2)}, u32[]{:S(2)}) %collective-permute-start.1) | collective-permute-done | bytes 2359328 | tf_op jit(solution)/shard_map/ppermute | solution.py:66
  56.1 1.6 %collective-permute-start.8 = (bf16[2,2,144,256]{3,2,1,0:T(8,128)(2,1)S(1)}, bf16[2,2,144,256]{3,2,1,0:T(8,128)(2,1)S(1)}, u32[]{:S(2)}, u32[]{:S(2)}) collective-permute-start(bf16[2,2,144,256]{3,2,1,0:T(8,128)(2,1)S(1)} %get-tuple-element.51), channel_id=1, source_target_pairs={{0,8},{1,9},{2,10},{3,11},{4,12},{5,13},{6,14},{7,15},{8,16},{9,17... | collective-permute-start | bytes 884744 | tf_op jit(solution)/shard_map/ppermute | solution.py:66
  57.7 1.7 %collective-permute-start.9 = (bf16[2,2,144,256]{3,2,1,0:T(8,128)(2,1)S(1)}, bf16[2,2,144,256]{3,2,1,0:T(8,128)(2,1)S(1)}, u32[]{:S(2)}, u32[]{:S(2)}) collective-permute-start(bf16[2,2,144,256]{3,2,1,0:T(8,128)(2,1)S(1)} %get-tuple-element.52), channel_id=1, source_target_pairs={{0,24},{1,25},{2,26},{3,27},{4,28},{5,29},{6,30},{7,31},{8,0},{9,1... | collective-permute-start | bytes 884744 | tf_op jit(solution)/shard_map/ppermute | solution.py:66
  59.4 2.0 %collective-permute-start.10 = (bf16[2,2,144,256]{3,2,1,0:T(8,128)(2,1)S(1)}, bf16[2,2,144,256]{3,2,1,0:T(8,128)(2,1)S(1)}, u32[]{:S(2)}, u32[]{:S(2)}) collective-permute-start(bf16[2,2,144,256]{3,2,1,0:T(8,128)(2,1)S(1)} %get-tuple-element.53), channel_id=1, source_target_pairs={{0,16},{1,17},{2,18},{3,19},{4,20},{5,21},{6,22},{7,23},{8,24},{9,... | collective-permute-start | bytes 884744 | tf_op jit(solution)/shard_map/ppermute | solution.py:66
  61.4 2.7 %collective-permute-done.8.refs_1_ = bf16[2,2,144,256]{3,2,1,0:T(8,128)(2,1)S(1)} collective-permute-done((bf16[2,2,144,256]{3,2,1,0:T(8,128)(2,1)S(1)}, bf16[2,2,144,256]{3,2,1,0:T(8,128)(2,1)S(1)}, u32[]{:S(2)}, u32[]{:S(2)}) %collective-permute-start.8) | collective-permute-done | bytes 294944 | tf_op jit(solution)/shard_map/ppermute | solution.py:66
  64.4 4.0 %collective-permute-done.10.refs_3_ = bf16[2,2,144,256]{3,2,1,0:T(8,128)(2,1)S(1)} collective-permute-done((bf16[2,2,144,256]{3,2,1,0:T(8,128)(2,1)S(1)}, bf16[2,2,144,256]{3,2,1,0:T(8,128)(2,1)S(1)}, u32[]{:S(2)}, u32[]{:S(2)}) %collective-permute-start.10) | collective-permute-done | bytes 294944 | tf_op jit(solution)/shard_map/ppermute | solution.py:66
  68.6 2.3 %collective-permute-start.11 = (bf16[2,144,256]{2,1,0:T(8,128)(2,1)S(1)}, bf16[2,144,256]{2,1,0:T(8,128)(2,1)S(1)}, u32[]{:S(2)}, u32[]{:S(2)}) collective-permute-start(bf16[2,144,256]{2,1,0:T(8,128)(2,1)S(1)} %get-tuple-element.54.own), channel_id=1, source_target_pairs={{0,1},{1,0},{2,3},{3,2},{4,5},{5,4},{6,7},{7,6},{8,9},{9,8},{10,11... | collective-permute-start | bytes 442376 | tf_op jit(solution)/shard_map/ppermute | solution.py:66
  70.9 2.1 %collective-permute-start.13 = (bf16[2,144,256]{2,1,0:T(8,128)(2,1)S(1)}, bf16[2,144,256]{2,1,0:T(8,128)(2,1)S(1)}, u32[]{:S(2)}, u32[]{:S(2)}) collective-permute-start(bf16[2,144,256]{2,1,0:T(8,128)(2,1)S(1)} %get-tuple-element.55), channel_id=1, source_target_pairs={{0,64},{1,65},{2,66},{3,67},{4,68},{5,69},{6,70},{7,71},{8,72},{9,... | collective-permute-start | bytes 442376 | tf_op jit(solution)/shard_map/ppermute | solution.py:66
  73.3 2.0 %collective-permute-done.11.near = bf16[2,144,256]{2,1,0:T(8,128)(2,1)S(1)} collective-permute-done((bf16[2,144,256]{2,1,0:T(8,128)(2,1)S(1)}, bf16[2,144,256]{2,1,0:T(8,128)(2,1)S(1)}, u32[]{:S(2)}, u32[]{:S(2)}) %collective-permute-start.11) | collective-permute-done | bytes 147488 | tf_op jit(solution)/shard_map/ppermute | solution.py:66
  75.3 2.4 %collective-permute-done.13.far = bf16[2,144,256]{2,1,0:T(8,128)(2,1)S(1)} collective-permute-done((bf16[2,144,256]{2,1,0:T(8,128)(2,1)S(1)}, bf16[2,144,256]{2,1,0:T(8,128)(2,1)S(1)}, u32[]{:S(2)}, u32[]{:S(2)}) %collective-permute-start.13) | collective-permute-done | bytes 147488 | tf_op jit(solution)/shard_map/ppermute | solution.py:66
  77.7 1.5 %collective-permute-done.12.across_z = bf16[2,144,256]{2,1,0:T(8,128)(2,1)S(1)} collective-permute-done((bf16[2,144,256]{2,1,0:T(8,128)(2,1)S(1)}, bf16[2,144,256]{2,1,0:T(8,128)(2,1)S(1)}, u32[]{:S(2)}, u32[]{:S(2)}) %collective-permute-start.12) | collective-permute-done | bytes 147488 | tf_op jit(solution)/shard_map/ppermute | solution.py:66
  79.3 2.9 %collective-permute-start.16 = (bf16[2,144,256]{2,1,0:T(8,128)(2,1)S(1)}, bf16[2,144,256]{2,1,0:T(8,128)(2,1)S(1)}, u32[]{:S(2)}, u32[]{:S(2)}) collective-permute-start(bf16[2,144,256]{2,1,0:T(8,128)(2,1)S(1)} %total.1.refs_0_), channel_id=1, source_target_pairs={{0,16},{1,17},{2,18},{3,19},{4,20},{5,21},{6,22},{7,23},{8,24},{9,... | collective-permute-start | bytes 442376 | tf_op jit(solution)/shard_map/ppermute | solution.py:66
  84.2 1.8 %collective-permute-done.16.refs_3_ = bf16[2,144,256]{2,1,0:T(8,128)(2,1)S(1)} collective-permute-done((bf16[2,144,256]{2,1,0:T(8,128)(2,1)S(1)}, bf16[2,144,256]{2,1,0:T(8,128)(2,1)S(1)}, u32[]{:S(2)}, u32[]{:S(2)}) %collective-permute-start.16) | collective-permute-done | bytes 147488 | tf_op jit(solution)/shard_map/ppermute | solution.py:66
  86.0 1.4 %collective-permute-done.15.refs_2_ = bf16[2,144,256]{2,1,0:T(8,128)(2,1)S(1)} collective-permute-done((bf16[2,144,256]{2,1,0:T(8,128)(2,1)S(1)}, bf16[2,144,256]{2,1,0:T(8,128)(2,1)S(1)}, u32[]{:S(2)}, u32[]{:S(2)}) %collective-permute-start.15) | collective-permute-done | bytes 147488 | tf_op jit(solution)/shard_map/ppermute | solution.py:66
  87.4 2.4 %collective-permute-done.14.refs_1_ = bf16[2,144,256]{2,1,0:T(8,128)(2,1)S(1)} collective-permute-done((bf16[2,144,256]{2,1,0:T(8,128)(2,1)S(1)}, bf16[2,144,256]{2,1,0:T(8,128)(2,1)S(1)}, u32[]{:S(2)}, u32[]{:S(2)}) %collective-permute-start.14) | collective-permute-done | bytes 147488 | tf_op jit(solution)/shard_map/ppermute | solution.py:66
  89.8 2.3 %collective-permute-start.19 = (bf16[4,2,144,256]{3,2,1,0:T(8,128)(2,1)S(1)}, bf16[4,2,144,256]{3,2,1,0:T(8,128)(2,1)S(1)}, u32[]{:S(2)}, u32[]{:S(2)}) collective-permute-start(bf16[4,2,144,256]{3,2,1,0:T(8,128)(2,1)S(1)} %join.1.g_ref), channel_id=1, source_target_pairs={{0,4},{1,5},{2,6},{3,7},{4,0},{5,1},{6,2},{7,3},{8,12},{9,13},{10,... | collective-permute-start | bytes 1769480 | tf_op jit(solution)/shard_map/ppermute | solution.py:66
  92.1 6.4 %collective-permute-start.18 = (bf16[4,2,144,256]{3,2,1,0:T(8,128)(2,1)S(1)}, bf16[4,2,144,256]{3,2,1,0:T(8,128)(2,1)S(1)}, u32[]{:S(2)}, u32[]{:S(2)}) collective-permute-start(bf16[4,2,144,256]{3,2,1,0:T(8,128)(2,1)S(1)} %join.1.g_ref), channel_id=1, source_target_pairs={{0,6},{1,7},{2,0},{3,1},{4,2},{5,3},{6,4},{7,5},{8,14},{9,15},{10,... | collective-permute-start | bytes 1769480 | tf_op jit(solution)/shard_map/ppermute | solution.py:66
  98.5 2.0 %collective-permute-start.17 = (bf16[4,2,144,256]{3,2,1,0:T(8,128)(2,1)S(1)}, bf16[4,2,144,256]{3,2,1,0:T(8,128)(2,1)S(1)}, u32[]{:S(2)}, u32[]{:S(2)}) collective-permute-start(bf16[4,2,144,256]{3,2,1,0:T(8,128)(2,1)S(1)} %join.1.g_ref), channel_id=1, source_target_pairs={{0,2},{1,3},{2,4},{3,5},{4,6},{5,7},{6,0},{7,1},{8,10},{9,11},{10,... | collective-permute-start | bytes 1769480 | tf_op jit(solution)/shard_map/ppermute | solution.py:66
  100.5 1.6 %old.1 = (f32[1152,1024]{1,0:T(8,128)S(1)}, f32[1152,1024]{1,0:T(8,128)S(1)}) custom-call(s32[4,1152]{1,0:T(4,128)S(1)} %bitcast.6, s32[4,1152]{1,0:T(4,128)S(1)} %bitcast.7, bf16[1152,1024]{1,0:T(8,128)(2,1)S(1)} %copy-done.1, bf16[1152,1024]{1,0:T(8,128)(2,1)S(1)} %copy-done.2), custom_call_target="tpu_custom_call" | custom-call | flops 4718592 | bytes 14680064 | tf_op jit(solution)/shard_map/old/pallas_call | solution.py:284
  102.1 4.4 %near.1 = (f32[384,1024]{1,0:T(8,128)S(1)}, f32[384,1]{1,0:T(8,128)S(1)}, f32[384,2304]{1,0:T(8,128)S(1)}) custom-call(s32[1]{0:T(128)} %bitcast.where, bf16[384,2304]{1,0:T(8,128)(2,1)S(1)} %get-tuple-element.40.mine, bf16[384,2304]{1,0:T(8,128)(2,1)S(1)} %get-tuple-element.41.theirs, bf16[384,4608]{1,0:T(8,128)(2,1)S(1)} %get-tuple-element.37.x, ...), custom_call_target="tpu_custom_call" | custom-call | flops 3623878656 | bytes 18874368 | tf_op jit(solution)/shard_map/near/pallas_call | solution.py:451
  106.5 2.1 %adam_own.1 = (f32[1152,1024]{1,0:T(8,128)}, bf16[1152,1024]{1,0:T(8,128)(2,1)}, bf16[1152,1024]{1,0:T(8,128)(2,1)}, f32[1152,128]{1,0:T(8,128)S(1)}) custom-call(s32[1]{0:T(128)} %bitcast.where, bf16[4,2,144,256]{3,2,1,0:T(8,128)(2,1)S(1)} %join.1.g_ref, f32[1152,1024]{1,0:T(8,128)S(1)} %get-tuple-element.56.m_old.refs_3_, ...), custom_call_target="tpu_custom_call" | custom-call | flops 5898240 | bytes 4194304 | tf_op jit(solution)/shard_map/adam_own/pallas_call | solution.py:334
  108.6 6.1 %collective-permute-done.18.refs_1_ = bf16[4,2,144,256]{3,2,1,0:T(8,128)(2,1)S(1)} collective-permute-done((bf16[4,2,144,256]{3,2,1,0:T(8,128)(2,1)S(1)}, bf16[4,2,144,256]{3,2,1,0:T(8,128)(2,1)S(1)}, u32[]{:S(2)}, u32[]{:S(2)}) %collective-permute-start.18) | collective-permute-done | bytes 589856 | tf_op jit(solution)/shard_map/ppermute | solution.py:66
  114.7 5.6 %adam_more.1 = (f32[1152,1024]{1,0:T(8,128)}, bf16[1152,1024]{1,0:T(8,128)(2,1)}, bf16[1152,1024]{1,0:T(8,128)(2,1)}, f32[4,1152]{1,0:T(4,128)}, f32[4,1152]{1,0:T(4,128)}) custom-call(s32[1]{0:T(128)} %bitcast.where, bf16[4,2,144,256]{3,2,1,0:T(8,128)(2,1)S(1)} %collective-permute-done.17.refs_0_, ...), custom_call_target="tpu_custom_call", output_to_operand_aliasing={{0}: (7, {}), {1}: (8, {}), {2}: (9, {})} | custom-call | flops 17694720 | bytes 12582912 | tf_op jit(solution)/shard_map/adam_more/pallas_call | solution.py:398
  120.3 3.1 %keys.1 = bf16[384,1024]{1,0:T(8,128)(2,1)} custom-call(s32[1]{0:T(128)} %bitcast.where, bf16[384,2304]{1,0:T(8,128)(2,1)S(1)} %get-tuple-element.40.mine, bf16[384,2304]{1,0:T(8,128)(2,1)S(1)} %get-tuple-element.41.theirs, f32[384,1024]{1,0:T(8,128)S(1)} %get-tuple-element.42.near, bf16[1152,1024]{1,0:T(8,128)(2,1)S(1)} %collective-permute-done.1.far, ...), custom_call_target="tpu_custom_call" | custom-call | flops 1811939328 | bytes 10485760 | tf_op jit(solution)/shard_map/keys/pallas_call | solution.py:473
  123.4 5.6 %back.1 = bf16[384,4608]{1,0:T(8,128)(2,1)} custom-call(s32[1]{0:T(128)} %bitcast.where, bf16[384,4608]{1,0:T(8,128)(2,1)S(1)} %get-tuple-element.37.x, bf16[384,1024]{1,0:T(8,128)(2,1)S(1)} %copy-done, f32[384,1]{1,0:T(8,128)S(1)} %get-tuple-element.38.inv.inv_ref, f32[36,128]{1,0:T(8,128)S(1)} %get-tuple-element.39.gain, ...), custom_call_target="tpu_custom_call" | custom-call | flops 1811939328 | bytes 16777216 | tf_op jit(solution)/shard_map/back/pallas_call | solution.py:502
  (35 shorter events, 6.3 us)
Async XLA Ops:
  0.6 6.1 %copy-start = (bf16[384,1024]{1,0:T(8,128)(2,1)S(1)}, bf16[384,1024]{1,0:T(8,128)(2,1)}, u32[]{:S(2)}) copy-start(bf16[384,1024]{1,0:T(8,128)(2,1)} %refs_2_.3) | copy-start | bytes 2359300
  0.6 53.5 %collective-permute-start.1 = (bf16[1152,1024]{1,0:T(8,128)(2,1)}, bf16[1152,1024]{1,0:T(8,128)(2,1)S(1)}, u32[]{:S(2)}, u32[]{:S(2)}) collective-permute-start(bf16[1152,1024]{1,0:T(8,128)(2,1)} %own.1), channel_id=1, source_target_pairs={{0,65},{1,64},{2,67},{3,66},{4,69},{5,68},{6,71},{7,70},{8,73},{9,... | collective-permute-start | bytes 7077896 | tf_op jit(solution)/shard_map/ppermute | solution.py:66
  2.6 4.6 %copy-start.5 = (bf16[1152,1024]{1,0:T(8,128)(2,1)S(1)}, bf16[1152,1024]{1,0:T(8,128)(2,1)}, u32[]{:S(2)}) copy-start(bf16[1152,1024]{1,0:T(8,128)(2,1)} %own.1) | copy-start | bytes 7077892
  6.6 4.9 %collective-permute-start.3 = (bf16[384,2304]{1,0:T(8,128)(2,1)S(1)}, bf16[384,2304]{1,0:T(8,128)(2,1)S(1)}, u32[]{:S(2)}, u32[]{:S(2)}) collective-permute-start(bf16[384,2304]{1,0:T(8,128)(2,1)S(1)} %get-tuple-element.41.theirs), channel_id=1, source_target_pairs={{0,32},{1,33},{2,34},{3,35},{4,36},{5,37},{6,38},{7,39},{8,40},{9,... | collective-permute-start | bytes 5308424 | tf_op jit(solution)/shard_map/ppermute | solution.py:66
  6.7 4.8 %collective-permute-start.4 = (bf16[384,1024]{1,0:T(8,128)(2,1)S(1)}, bf16[384,1024]{1,0:T(8,128)(2,1)S(1)}, u32[]{:S(2)}, u32[]{:S(2)}) collective-permute-start(bf16[384,1024]{1,0:T(8,128)(2,1)S(1)} %copy-done), channel_id=1, source_target_pairs={{0,32},{1,33},{2,34},{3,35},{4,36},{5,37},{6,38},{7,39},{8,40},{9,... | collective-permute-start | bytes 2359304 | tf_op jit(solution)/shard_map/ppermute | solution.py:66
  7.2 94.9 %collective-permute-start = (bf16[1152,1024]{1,0:T(8,128)(2,1)S(1)}, bf16[1152,1024]{1,0:T(8,128)(2,1)S(1)}, u32[]{:S(2)}, u32[]{:S(2)}) collective-permute-start(bf16[1152,1024]{1,0:T(8,128)(2,1)S(1)} %copy-done.5), channel_id=1, source_target_pairs={{0,32},{1,33},{2,34},{3,35},{4,36},{5,37},{6,38},{7,39},{8,40},{9,... | collective-permute-start | bytes 7077896 | tf_op jit(solution)/shard_map/ppermute | solution.py:66
  13.0 42.5 %collective-permute-start.7 = (bf16[4,2,2,144,256]{4,3,2,1,0:T(8,128)(2,1)S(1)}, bf16[4,2,2,144,256]{4,3,2,1,0:T(8,128)(2,1)S(1)}, u32[]{:S(2)}, u32[]{:S(2)}) collective-permute-start(bf16[4,2,2,144,256]{4,3,2,1,0:T(8,128)(2,1)S(1)} %get-tuple-element.49), channel_id=1, source_target_pairs={{0,4},{1,5},{2,6},{3,7},{4,0},{5,1},{6,2},{7,3},{8,12},{9,13},{10,... | collective-permute-start | bytes 3538952 | tf_op jit(solution)/shard_map/ppermute | solution.py:66
  16.2 39.3 %collective-permute-start.5 = (bf16[4,2,2,144,256]{4,3,2,1,0:T(8,128)(2,1)S(1)}, bf16[4,2,2,144,256]{4,3,2,1,0:T(8,128)(2,1)S(1)}, u32[]{:S(2)}, u32[]{:S(2)}) collective-permute-start(bf16[4,2,2,144,256]{4,3,2,1,0:T(8,128)(2,1)S(1)} %get-tuple-element.47), channel_id=1, source_target_pairs={{0,2},{1,3},{2,4},{3,5},{4,6},{5,7},{6,0},{7,1},{8,10},{9,11},{10,... | collective-permute-start | bytes 3538952 | tf_op jit(solution)/shard_map/ppermute | solution.py:66
  18.3 37.2 %collective-permute-start.6 = (bf16[4,2,2,144,256]{4,3,2,1,0:T(8,128)(2,1)S(1)}, bf16[4,2,2,144,256]{4,3,2,1,0:T(8,128)(2,1)S(1)}, u32[]{:S(2)}, u32[]{:S(2)}) collective-permute-start(bf16[4,2,2,144,256]{4,3,2,1,0:T(8,128)(2,1)S(1)} %get-tuple-element.48), channel_id=1, source_target_pairs={{0,6},{1,7},{2,0},{3,1},{4,2},{5,3},{6,4},{7,5},{8,14},{9,15},{10,... | collective-permute-start | bytes 3538952 | tf_op jit(solution)/shard_map/ppermute | solution.py:66
  54.1 66.2 %collective-permute-start.2 = (bf16[1152,1024]{1,0:T(8,128)(2,1)S(1)}, bf16[1152,1024]{1,0:T(8,128)(2,1)S(1)}, u32[]{:S(2)}, u32[]{:S(2)}) collective-permute-start(bf16[1152,1024]{1,0:T(8,128)(2,1)S(1)} %collective-permute-done.1.far), channel_id=1, source_target_pairs={{0,32},{1,33},{2,34},{3,35},{4,36},{5,37},{6,38},{7,39},{8,40},{9,... | collective-permute-start | bytes 7077896 | tf_op jit(solution)/shard_map/ppermute | solution.py:66
  55.5 45.0 %copy-start.2 = (bf16[1152,1024]{1,0:T(8,128)(2,1)S(1)}, bf16[1152,1024]{1,0:T(8,128)(2,1)}, u32[]{:S(2)}) copy-start(bf16[1152,1024]{1,0:T(8,128)(2,1)} %vc_ref.1) | copy-start | bytes 7077892
  56.0 44.5 %copy-start.1 = (bf16[1152,1024]{1,0:T(8,128)(2,1)S(1)}, bf16[1152,1024]{1,0:T(8,128)(2,1)}, u32[]{:S(2)}) copy-start(bf16[1152,1024]{1,0:T(8,128)(2,1)} %mc_ref.1) | copy-start | bytes 7077892
  56.0 44.4 %copy-start.3 = (s32[1152,4]{0,1:T(4,128)S(1)}, s32[1152,4]{0,1:T(4,128)}, u32[]{:S(2)}) copy-start(s32[1152,4]{0,1:T(4,128)} %param.13) | copy-start | bytes 55300
  56.1 44.4 %copy-start.4 = (s32[1152,4]{0,1:T(4,128)S(1)}, s32[1152,4]{0,1:T(4,128)}, u32[]{:S(2)}) copy-start(s32[1152,4]{0,1:T(4,128)} %param.15) | copy-start | bytes 55300
  56.1 8.0 %collective-permute-start.8 = (bf16[2,2,144,256]{3,2,1,0:T(8,128)(2,1)S(1)}, bf16[2,2,144,256]{3,2,1,0:T(8,128)(2,1)S(1)}, u32[]{:S(2)}, u32[]{:S(2)}) collective-permute-start(bf16[2,2,144,256]{3,2,1,0:T(8,128)(2,1)S(1)} %get-tuple-element.51), channel_id=1, source_target_pairs={{0,8},{1,9},{2,10},{3,11},{4,12},{5,13},{6,14},{7,15},{8,16},{9,17... | collective-permute-start | bytes 884744 | tf_op jit(solution)/shard_map/ppermute | solution.py:66
  57.7 6.7 %collective-permute-start.9 = (bf16[2,2,144,256]{3,2,1,0:T(8,128)(2,1)S(1)}, bf16[2,2,144,256]{3,2,1,0:T(8,128)(2,1)S(1)}, u32[]{:S(2)}, u32[]{:S(2)}) collective-permute-start(bf16[2,2,144,256]{3,2,1,0:T(8,128)(2,1)S(1)} %get-tuple-element.52), channel_id=1, source_target_pairs={{0,24},{1,25},{2,26},{3,27},{4,28},{5,29},{6,30},{7,31},{8,0},{9,1... | collective-permute-start | bytes 884744 | tf_op jit(solution)/shard_map/ppermute | solution.py:66
  59.4 9.1 %collective-permute-start.10 = (bf16[2,2,144,256]{3,2,1,0:T(8,128)(2,1)S(1)}, bf16[2,2,144,256]{3,2,1,0:T(8,128)(2,1)S(1)}, u32[]{:S(2)}, u32[]{:S(2)}) collective-permute-start(bf16[2,2,144,256]{3,2,1,0:T(8,128)(2,1)S(1)} %get-tuple-element.53), channel_id=1, source_target_pairs={{0,16},{1,17},{2,18},{3,19},{4,20},{5,21},{6,22},{7,23},{8,24},{9,... | collective-permute-start | bytes 884744 | tf_op jit(solution)/shard_map/ppermute | solution.py:66
  68.6 6.7 %collective-permute-start.11 = (bf16[2,144,256]{2,1,0:T(8,128)(2,1)S(1)}, bf16[2,144,256]{2,1,0:T(8,128)(2,1)S(1)}, u32[]{:S(2)}, u32[]{:S(2)}) collective-permute-start(bf16[2,144,256]{2,1,0:T(8,128)(2,1)S(1)} %get-tuple-element.54.own), channel_id=1, source_target_pairs={{0,1},{1,0},{2,3},{3,2},{4,5},{5,4},{6,7},{7,6},{8,9},{9,8},{10,11... | collective-permute-start | bytes 442376 | tf_op jit(solution)/shard_map/ppermute | solution.py:66
  70.9 6.7 %collective-permute-start.13 = (bf16[2,144,256]{2,1,0:T(8,128)(2,1)S(1)}, bf16[2,144,256]{2,1,0:T(8,128)(2,1)S(1)}, u32[]{:S(2)}, u32[]{:S(2)}) collective-permute-start(bf16[2,144,256]{2,1,0:T(8,128)(2,1)S(1)} %get-tuple-element.55), channel_id=1, source_target_pairs={{0,64},{1,65},{2,66},{3,67},{4,68},{5,69},{6,70},{7,71},{8,72},{9,... | collective-permute-start | bytes 442376 | tf_op jit(solution)/shard_map/ppermute | solution.py:66
  73.0 6.2 %collective-permute-start.12 = (bf16[2,144,256]{2,1,0:T(8,128)(2,1)S(1)}, bf16[2,144,256]{2,1,0:T(8,128)(2,1)S(1)}, u32[]{:S(2)}, u32[]{:S(2)}) collective-permute-start(bf16[2,144,256]{2,1,0:T(8,128)(2,1)S(1)} %get-tuple-element.55), channel_id=1, source_target_pairs={{0,65},{1,64},{2,67},{3,66},{4,69},{5,68},{6,71},{7,70},{8,73},{9,... | collective-permute-start | bytes 442376 | tf_op jit(solution)/shard_map/ppermute | solution.py:66
  79.3 6.7 %collective-permute-start.16 = (bf16[2,144,256]{2,1,0:T(8,128)(2,1)S(1)}, bf16[2,144,256]{2,1,0:T(8,128)(2,1)S(1)}, u32[]{:S(2)}, u32[]{:S(2)}) collective-permute-start(bf16[2,144,256]{2,1,0:T(8,128)(2,1)S(1)} %total.1.refs_0_), channel_id=1, source_target_pairs={{0,16},{1,17},{2,18},{3,19},{4,20},{5,21},{6,22},{7,23},{8,24},{9,... | collective-permute-start | bytes 442376 | tf_op jit(solution)/shard_map/ppermute | solution.py:66
  82.2 5.2 %collective-permute-start.15 = (bf16[2,144,256]{2,1,0:T(8,128)(2,1)S(1)}, bf16[2,144,256]{2,1,0:T(8,128)(2,1)S(1)}, u32[]{:S(2)}, u32[]{:S(2)}) collective-permute-start(bf16[2,144,256]{2,1,0:T(8,128)(2,1)S(1)} %total.1.refs_0_), channel_id=1, source_target_pairs={{0,24},{1,25},{2,26},{3,27},{4,28},{5,29},{6,30},{7,31},{8,0},{9,1... | collective-permute-start | bytes 442376 | tf_op jit(solution)/shard_map/ppermute | solution.py:66
  83.4 6.4 %collective-permute-start.14 = (bf16[2,144,256]{2,1,0:T(8,128)(2,1)S(1)}, bf16[2,144,256]{2,1,0:T(8,128)(2,1)S(1)}, u32[]{:S(2)}, u32[]{:S(2)}) collective-permute-start(bf16[2,144,256]{2,1,0:T(8,128)(2,1)S(1)} %total.1.refs_0_), channel_id=1, source_target_pairs={{0,8},{1,9},{2,10},{3,11},{4,12},{5,13},{6,14},{7,15},{8,16},{9,17... | collective-permute-start | bytes 442376 | tf_op jit(solution)/shard_map/ppermute | solution.py:66
  89.8 18.8 %collective-permute-start.19 = (bf16[4,2,144,256]{3,2,1,0:T(8,128)(2,1)S(1)}, bf16[4,2,144,256]{3,2,1,0:T(8,128)(2,1)S(1)}, u32[]{:S(2)}, u32[]{:S(2)}) collective-permute-start(bf16[4,2,144,256]{3,2,1,0:T(8,128)(2,1)S(1)} %join.1.g_ref), channel_id=1, source_target_pairs={{0,4},{1,5},{2,6},{3,7},{4,0},{5,1},{6,2},{7,3},{8,12},{9,13},{10,... | collective-permute-start | bytes 1769480 | tf_op jit(solution)/shard_map/ppermute | solution.py:66
  92.1 22.6 %collective-permute-start.18 = (bf16[4,2,144,256]{3,2,1,0:T(8,128)(2,1)S(1)}, bf16[4,2,144,256]{3,2,1,0:T(8,128)(2,1)S(1)}, u32[]{:S(2)}, u32[]{:S(2)}) collective-permute-start(bf16[4,2,144,256]{3,2,1,0:T(8,128)(2,1)S(1)} %join.1.g_ref), channel_id=1, source_target_pairs={{0,6},{1,7},{2,0},{3,1},{4,2},{5,3},{6,4},{7,5},{8,14},{9,15},{10,... | collective-permute-start | bytes 1769480 | tf_op jit(solution)/shard_map/ppermute | solution.py:66
  98.5 16.2 %collective-permute-start.17 = (bf16[4,2,144,256]{3,2,1,0:T(8,128)(2,1)S(1)}, bf16[4,2,144,256]{3,2,1,0:T(8,128)(2,1)S(1)}, u32[]{:S(2)}, u32[]{:S(2)}) collective-permute-start(bf16[4,2,144,256]{3,2,1,0:T(8,128)(2,1)S(1)} %join.1.g_ref), channel_id=1, source_target_pairs={{0,2},{1,3},{2,4},{3,5},{4,6},{5,7},{6,0},{7,1},{8,10},{9,11},{10,... | collective-permute-start | bytes 1769480 | tf_op jit(solution)/shard_map/ppermute | solution.py:66

commit v3 on v2

--- a/solution.py
+++ b/solution.py
@@ -295,10 +295,10 @@
 
 def adam_rows(other, half, read, m_old, w_old, step_ref, mr_ref, vr_ref, keep_scale):
     lane = lax.broadcasted_iota(jnp.int32, (RB, 128), 1)
-    for b in range(4):
+    for b in range(2):
         rows = slice(b * RB, (b + 1) * RB)
-        back = lax.rem(other + 8 - (2 * half + b // 2), 4)
-        g = read(back, b % 2).astype(jnp.float32)
+        back = lax.rem(other + 4 - half, 4)
+        g = read(back, b).astype(jnp.float32)
         m = m_old[rows, :] + 0.1 * g
         w = w_old[rows, :] + (0.001 * SCALE) * (g * g)
         step_ref[rows, :] = m / (w * lax.rsqrt(w) + 1e-08 * bias_first)
@@ -329,13 +329,13 @@
 
 
 def adam_own(where, g, old):
-    wide = pl.BlockSpec((4 * RB, CB), lambda i, where: (i, (where[0] // 4) % 4))
-    thin = pl.BlockSpec((4 * RB, 128), lambda i, where: (i, 0))
+    wide = pl.BlockSpec((2 * RB, CB), lambda i, where: (i, (where[0] // 4) % 4))
+    thin = pl.BlockSpec((2 * RB, 128), lambda i, where: (i, 0))
     return pl.pallas_call(
         adam_own_kernel,
         grid_spec=pltpu.PrefetchScalarGridSpec(
             num_scalar_prefetch=1,
-            grid=(2,),
+            grid=(4,),
             in_specs=[pl.BlockSpec((4, 2, RB, CB), lambda i, where: (0, 0, 0, 0)), wide, wide],
             out_specs=[wide, wide, wide, thin],
         ),
@@ -349,7 +349,7 @@
 def place_of(ks, i, pos):
     k = ks[0]
     for n in range(1, len(ks)):
-        k = jnp.where(i < 2 * n, k, ks[n])
+        k = jnp.where(i < 4 * n, k, ks[n])
     return lax.rem(pos + 4 - k, 4)
 
 
@@ -360,26 +360,26 @@
     scales = refs[-1]
     _, _, pos, other = unpack(where)
     i = pl.program_id(0)
-    p, half = place_of(ks, i, pos), lax.rem(i, 2)
+    p, half = place_of(ks, i, pos), lax.rem(i, 4)
 
     @pl.when(i == 0)
     def _():
         scales[...] = s0[...]
 
     def keep_scale(b, lane, ms, vs):
-        rows = pl.ds(pl.multiple_of(half * (4 * RB) + b * RB, 8), RB)
+        rows = pl.ds(pl.multiple_of(half * (2 * RB) + b * RB, 8), RB)
         scales[rows, :] = jnp.where(lane == p, ms, jnp.where(lane == 4 + p, vs, scales[rows, :]))
 
     def read(back, zl):
         g = gs[0][back, zl]
         for k in range(1, n):
-            g = jnp.where(i < 2 * k, g, gs[k][back, zl])
+            g = jnp.where(i < 4 * k, g, gs[k][back, zl])
         return g
 
     adam_rows(other, half, read, m_old, w_old, step_ref, mr_ref, vr_ref, keep_scale)
 
     if last:
-        @pl.when(i == 2 * n - 1)
+        @pl.when(i == 4 * n - 1)
         def _():
             for part in range(ROWS // 128):
                 cols = slice(part * 128, (part + 1) * 128)
@@ -390,7 +390,7 @@
 
 def adam_more(ks, last, where, g, old, s0, done):
     n = len(ks)
-    wide = pl.BlockSpec((4 * RB, CB), lambda i, where: (lax.rem(i, 2), place_of(ks, i, (where[0] // 4) % 4)))
+    wide = pl.BlockSpec((2 * RB, CB), lambda i, where: (lax.rem(i, 4), place_of(ks, i, (where[0] // 4) % 4)))
     flat = pl.BlockSpec((4, ROWS), lambda i, where: (0, 0))
     tall = pl.BlockSpec((ROWS, 128), lambda i, where: (0, 0))
     whole = pl.BlockSpec((4, 2, RB, CB), lambda i, where: (0, 0, 0, 0))
@@ -399,7 +399,7 @@
         functools.partial(adam_more_kernel, ks, last),
         grid_spec=pltpu.PrefetchScalarGridSpec(
             num_scalar_prefetch=1,
-            grid=(2 * n,),
+            grid=(4 * n,),
             in_specs=[whole] * n + [wide, wide, tall] + [pl.BlockSpec(memory_space=pl.ANY)] * 3,
             out_specs=[wide, wide, wide] + ([flat, flat] if last else [tall]),
             scratch_shapes=[pltpu.VMEM((ROWS, 128), jnp.float32)] * last,

time: 129 us -> 131 us (1.016)
  Pallas kernels: 34 us -> 36.2 us
    pallas_call x1, Pallas kernels: 5.63 us -> 7.44 us  [adam_more(): pl.pallas_call(functools.partial(adam_more_kernel, ks, last), grid_spec=p...]
  transfers between devices with their start and end apart: 20 -> 20, of which waited for: 12 -> 12; matrix products, arithmetic and copies ran while one was open for 0% -> 0% of each run, Pallas kernels for 20% -> 21%
where the time goes in v3:
time: 131 us
  waiting for transfers between devices  62.7 us (48%)
  Pallas kernels  36.2 us (28%)
  starting transfers between devices  31.1 us (24%)
    ppermute x20, waiting for transfers between devices, send(): return lax.ppermute(value, AXES, pairs(move))  62.7 us
    ppermute x20, starting transfers between devices, send(): return lax.ppermute(value, AXES, pairs(move))  31.1 us
    pallas_call x1, Pallas kernels, adam_more(): pl.pallas_call(functools.partial(adam_more_kernel, ks, last), grid_spec=p...  7.44 us
    pallas_call x1, Pallas kernels, back_call(): pl.pallas_call(back_kernel, in_specs=[pl.BlockSpec(memory_space=pltpu.SME...  5.6 us
    pallas_call x3, Pallas kernels, grad_call(): pl.pallas_call(first_grad_kernel if first else functools.partial(grad_ker...  5.45 us
    pallas_call x1, Pallas kernels, near_call(): pl.pallas_call(near_kernel, in_specs=[pl.BlockSpec(memory_space=pltpu.SME...  4.38 us
    pallas_call x1, Pallas kernels, norm_call(): pl.pallas_call(norm_kernel, in_specs=[pl.BlockSpec(memory_space=pltpu.SME...  3.98 us
    pallas_call x1, Pallas kernels, keys_call(): pl.pallas_call(keys_kernel, in_specs=[pl.BlockSpec(memory_space=pltpu.SME...  3.1 us
  transfers between devices with their start and end apart: 20, of which 12 were waited for; matrix products, arithmetic and copies ran while one was open for 0% of the time, Pallas kernels for 21%

profile of v3, /device:TPU:36, one launch (start us, length us, event | category | flops | bytes accessed | tf_op | source)
XLA Modules:
  0.0 130.9 jit_solution(12940775352313588608)
XLA Ops:
  0.6 2.0 %collective-permute-start.1 = (bf16[1152,1024]{1,0:T(8,128)(2,1)}, bf16[1152,1024]{1,0:T(8,128)(2,1)S(1)}, u32[]{:S(2)}, u32[]{:S(2)}) collective-permute-start(bf16[1152,1024]{1,0:T(8,128)(2,1)} %own.1), channel_id=1, source_target_pairs={{0,65},{1,64},{2,67},{3,66},{4,69},{5,68},{6,71},{7,70},{8,73},{9,... | collective-permute-start | bytes 7077896 | tf_op jit(solution)/shard_map/ppermute | solution.py:66
  2.6 4.0 %norm.1 = (bf16[384,2304]{1,0:T(8,128)(2,1)S(1)}, f32[384,1]{1,0:T(8,128)S(1)}, bf16[384,4608]{1,0:T(8,128)(2,1)S(1)}, f32[36,128]{1,0:T(8,128)S(1)}) custom-call(s32[1]{0:T(128)} %bitcast.where, bf16[384,4608]{1,0:T(8,128)(2,1)} %x_hbm.1, f32[36,128]{1,0:T(8,128)} %bitcast.8), custom_call_target="tpu_custom_call" | custom-call | flops 7077888 | bytes 7077888 | tf_op jit(solution)/shard_map/norm/pallas_call | solution.py:111
  7.3 1.4 %mine.1 = (bf16[384,2304]{1,0:T(8,128)(2,1)S(1)}, bf16[2304,384]{1,0:T(8,128)(2,1)S(1)}) custom-call(s32[1]{0:T(128)} %bitcast.where, bf16[384,4608]{1,0:T(8,128)(2,1)S(1)} %get-tuple-element.37.x, f32[384,1]{1,0:T(8,128)S(1)} %get-tuple-element.38.inv.inv_ref, f32[36,128]{1,0:T(8,128)S(1)} %get-tuple-element.39.gain), custom_call_target="tpu_custom_call" | custom-call | flops 3538944 | bytes 5308416 | tf_op jit(solution)/shard_map/mine/pallas_call | solution.py:141
  8.8 2.8 %collective-permute-done.4.kb_ref.refs_3_ = bf16[384,1024]{1,0:T(8,128)(2,1)S(1)} collective-permute-done((bf16[384,1024]{1,0:T(8,128)(2,1)S(1)}, bf16[384,1024]{1,0:T(8,128)(2,1)S(1)}, u32[]{:S(2)}, u32[]{:S(2)}) %collective-permute-start.4) | collective-permute-done | bytes 786464 | tf_op jit(solution)/shard_map/ppermute | solution.py:66
  11.5 1.4 %grad.3 = (bf16[2304,384]{1,0:T(8,128)(2,1)S(1)}, bf16[4,2,2,144,256]{4,3,2,1,0:T(8,128)(2,1)S(1)}) custom-call(s32[1]{0:T(128)} %bitcast.where, bf16[2304,384]{1,0:T(8,128)(2,1)S(1)} %get-tuple-element.45.a_ref.refs_0_, bf16[384,2304]{1,0:T(8,128)(2,1)S(1)} %collective-permute-done.3.b_in, bf16[384,1024]{1,0:T(8,128)(2,1)S(1)} %copy-done, ...), custom_call_target="tpu_custom_call" | custom-call | flops 905969664 | bytes 6291456 | tf_op jit(solution)/shard_map/grad/pallas_call | solution.py:179
  13.6 2.6 %grad.5 = (bf16[4,2,2,144,256]{4,3,2,1,0:T(8,128)(2,1)S(1)}, bf16[4,2,2,144,256]{4,3,2,1,0:T(8,128)(2,1)S(1)}) custom-call(s32[1]{0:T(128)} %bitcast.where, bf16[2304,384]{1,0:T(8,128)(2,1)S(1)} %get-tuple-element.45.a_ref.refs_0_, bf16[2304,384]{1,0:T(8,128)(2,1)S(1)} %get-tuple-element.46.refs_1_, bf16[384,1024]{1,0:T(8,128)(2,1)S(1)} %copy-done, ...), custom_call_target="tpu_custom_call" | custom-call | flops 1811939328 | bytes 6291456 | tf_op jit(solution)/shard_map/grad/pallas_call | solution.py:179
  16.2 2.2 %collective-permute-start.5 = (bf16[4,2,2,144,256]{4,3,2,1,0:T(8,128)(2,1)S(1)}, bf16[4,2,2,144,256]{4,3,2,1,0:T(8,128)(2,1)S(1)}, u32[]{:S(2)}, u32[]{:S(2)}) collective-permute-start(bf16[4,2,2,144,256]{4,3,2,1,0:T(8,128)(2,1)S(1)} %get-tuple-element.47), channel_id=1, source_target_pairs={{0,2},{1,3},{2,4},{3,5},{4,6},{5,7},{6,0},{7,1},{8,10},{9,11},{10,... | collective-permute-start | bytes 3538952 | tf_op jit(solution)/shard_map/ppermute | solution.py:66
  18.5 35.6 %collective-permute-done.1.far = bf16[1152,1024]{1,0:T(8,128)(2,1)S(1)} collective-permute-done((bf16[1152,1024]{1,0:T(8,128)(2,1)}, bf16[1152,1024]{1,0:T(8,128)(2,1)S(1)}, u32[]{:S(2)}, u32[]{:S(2)}) %collective-permute-start.1) | collective-permute-done | bytes 2359328 | tf_op jit(solution)/shard_map/ppermute | solution.py:66
  56.1 1.6 %collective-permute-start.8 = (bf16[2,2,144,256]{3,2,1,0:T(8,128)(2,1)S(1)}, bf16[2,2,144,256]{3,2,1,0:T(8,128)(2,1)S(1)}, u32[]{:S(2)}, u32[]{:S(2)}) collective-permute-start(bf16[2,2,144,256]{3,2,1,0:T(8,128)(2,1)S(1)} %get-tuple-element.51), channel_id=1, source_target_pairs={{0,8},{1,9},{2,10},{3,11},{4,12},{5,13},{6,14},{7,15},{8,16},{9,17... | collective-permute-start | bytes 884744 | tf_op jit(solution)/shard_map/ppermute | solution.py:66
  57.7 1.7 %collective-permute-start.9 = (bf16[2,2,144,256]{3,2,1,0:T(8,128)(2,1)S(1)}, bf16[2,2,144,256]{3,2,1,0:T(8,128)(2,1)S(1)}, u32[]{:S(2)}, u32[]{:S(2)}) collective-permute-start(bf16[2,2,144,256]{3,2,1,0:T(8,128)(2,1)S(1)} %get-tuple-element.52), channel_id=1, source_target_pairs={{0,24},{1,25},{2,26},{3,27},{4,28},{5,29},{6,30},{7,31},{8,0},{9,1... | collective-permute-start | bytes 884744 | tf_op jit(solution)/shard_map/ppermute | solution.py:66
  59.4 2.0 %collective-permute-start.10 = (bf16[2,2,144,256]{3,2,1,0:T(8,128)(2,1)S(1)}, bf16[2,2,144,256]{3,2,1,0:T(8,128)(2,1)S(1)}, u32[]{:S(2)}, u32[]{:S(2)}) collective-permute-start(bf16[2,2,144,256]{3,2,1,0:T(8,128)(2,1)S(1)} %get-tuple-element.53), channel_id=1, source_target_pairs={{0,16},{1,17},{2,18},{3,19},{4,20},{5,21},{6,22},{7,23},{8,24},{9,... | collective-permute-start | bytes 884744 | tf_op jit(solution)/shard_map/ppermute | solution.py:66
  61.4 2.7 %collective-permute-done.8.refs_1_ = bf16[2,2,144,256]{3,2,1,0:T(8,128)(2,1)S(1)} collective-permute-done((bf16[2,2,144,256]{3,2,1,0:T(8,128)(2,1)S(1)}, bf16[2,2,144,256]{3,2,1,0:T(8,128)(2,1)S(1)}, u32[]{:S(2)}, u32[]{:S(2)}) %collective-permute-start.8) | collective-permute-done | bytes 294944 | tf_op jit(solution)/shard_map/ppermute | solution.py:66
  64.4 4.0 %collective-permute-done.10.refs_3_ = bf16[2,2,144,256]{3,2,1,0:T(8,128)(2,1)S(1)} collective-permute-done((bf16[2,2,144,256]{3,2,1,0:T(8,128)(2,1)S(1)}, bf16[2,2,144,256]{3,2,1,0:T(8,128)(2,1)S(1)}, u32[]{:S(2)}, u32[]{:S(2)}) %collective-permute-start.10) | collective-permute-done | bytes 294944 | tf_op jit(solution)/shard_map/ppermute | solution.py:66
  68.6 2.3 %collective-permute-start.11 = (bf16[2,144,256]{2,1,0:T(8,128)(2,1)S(1)}, bf16[2,144,256]{2,1,0:T(8,128)(2,1)S(1)}, u32[]{:S(2)}, u32[]{:S(2)}) collective-permute-start(bf16[2,144,256]{2,1,0:T(8,128)(2,1)S(1)} %get-tuple-element.54.own), channel_id=1, source_target_pairs={{0,1},{1,0},{2,3},{3,2},{4,5},{5,4},{6,7},{7,6},{8,9},{9,8},{10,11... | collective-permute-start | bytes 442376 | tf_op jit(solution)/shard_map/ppermute | solution.py:66
  70.9 2.1 %collective-permute-start.13 = (bf16[2,144,256]{2,1,0:T(8,128)(2,1)S(1)}, bf16[2,144,256]{2,1,0:T(8,128)(2,1)S(1)}, u32[]{:S(2)}, u32[]{:S(2)}) collective-permute-start(bf16[2,144,256]{2,1,0:T(8,128)(2,1)S(1)} %get-tuple-element.55), channel_id=1, source_target_pairs={{0,64},{1,65},{2,66},{3,67},{4,68},{5,69},{6,70},{7,71},{8,72},{9,... | collective-permute-start | bytes 442376 | tf_op jit(solution)/shard_map/ppermute | solution.py:66
  73.3 2.0 %collective-permute-done.11.near = bf16[2,144,256]{2,1,0:T(8,128)(2,1)S(1)} collective-permute-done((bf16[2,144,256]{2,1,0:T(8,128)(2,1)S(1)}, bf16[2,144,256]{2,1,0:T(8,128)(2,1)S(1)}, u32[]{:S(2)}, u32[]{:S(2)}) %collective-permute-start.11) | collective-permute-done | bytes 147488 | tf_op jit(solution)/shard_map/ppermute | solution.py:66
  75.3 2.4 %collective-permute-done.13.far = bf16[2,144,256]{2,1,0:T(8,128)(2,1)S(1)} collective-permute-done((bf16[2,144,256]{2,1,0:T(8,128)(2,1)S(1)}, bf16[2,144,256]{2,1,0:T(8,128)(2,1)S(1)}, u32[]{:S(2)}, u32[]{:S(2)}) %collective-permute-start.13) | collective-permute-done | bytes 147488 | tf_op jit(solution)/shard_map/ppermute | solution.py:66
  77.7 1.5 %collective-permute-done.12.across_z = bf16[2,144,256]{2,1,0:T(8,128)(2,1)S(1)} collective-permute-done((bf16[2,144,256]{2,1,0:T(8,128)(2,1)S(1)}, bf16[2,144,256]{2,1,0:T(8,128)(2,1)S(1)}, u32[]{:S(2)}, u32[]{:S(2)}) %collective-permute-start.12) | collective-permute-done | bytes 147488 | tf_op jit(solution)/shard_map/ppermute | solution.py:66
  79.3 2.9 %collective-permute-start.16 = (bf16[2,144,256]{2,1,0:T(8,128)(2,1)S(1)}, bf16[2,144,256]{2,1,0:T(8,128)(2,1)S(1)}, u32[]{:S(2)}, u32[]{:S(2)}) collective-permute-start(bf16[2,144,256]{2,1,0:T(8,128)(2,1)S(1)} %total.1.refs_0_), channel_id=1, source_target_pairs={{0,16},{1,17},{2,18},{3,19},{4,20},{5,21},{6,22},{7,23},{8,24},{9,... | collective-permute-start | bytes 442376 | tf_op jit(solution)/shard_map/ppermute | solution.py:66
  84.2 1.8 %collective-permute-done.16.refs_3_ = bf16[2,144,256]{2,1,0:T(8,128)(2,1)S(1)} collective-permute-done((bf16[2,144,256]{2,1,0:T(8,128)(2,1)S(1)}, bf16[2,144,256]{2,1,0:T(8,128)(2,1)S(1)}, u32[]{:S(2)}, u32[]{:S(2)}) %collective-permute-start.16) | collective-permute-done | bytes 147488 | tf_op jit(solution)/shard_map/ppermute | solution.py:66
  86.0 1.4 %collective-permute-done.15.refs_2_ = bf16[2,144,256]{2,1,0:T(8,128)(2,1)S(1)} collective-permute-done((bf16[2,144,256]{2,1,0:T(8,128)(2,1)S(1)}, bf16[2,144,256]{2,1,0:T(8,128)(2,1)S(1)}, u32[]{:S(2)}, u32[]{:S(2)}) %collective-permute-start.15) | collective-permute-done | bytes 147488 | tf_op jit(solution)/shard_map/ppermute | solution.py:66
  87.4 2.4 %collective-permute-done.14.refs_1_ = bf16[2,144,256]{2,1,0:T(8,128)(2,1)S(1)} collective-permute-done((bf16[2,144,256]{2,1,0:T(8,128)(2,1)S(1)}, bf16[2,144,256]{2,1,0:T(8,128)(2,1)S(1)}, u32[]{:S(2)}, u32[]{:S(2)}) %collective-permute-start.14) | collective-permute-done | bytes 147488 | tf_op jit(solution)/shard_map/ppermute | solution.py:66
  89.8 2.3 %collective-permute-start.19 = (bf16[4,2,144,256]{3,2,1,0:T(8,128)(2,1)S(1)}, bf16[4,2,144,256]{3,2,1,0:T(8,128)(2,1)S(1)}, u32[]{:S(2)}, u32[]{:S(2)}) collective-permute-start(bf16[4,2,144,256]{3,2,1,0:T(8,128)(2,1)S(1)} %join.1.g_ref), channel_id=1, source_target_pairs={{0,4},{1,5},{2,6},{3,7},{4,0},{5,1},{6,2},{7,3},{8,12},{9,13},{10,... | collective-permute-start | bytes 1769480 | tf_op jit(solution)/shard_map/ppermute | solution.py:66
  92.1 6.4 %collective-permute-start.18 = (bf16[4,2,144,256]{3,2,1,0:T(8,128)(2,1)S(1)}, bf16[4,2,144,256]{3,2,1,0:T(8,128)(2,1)S(1)}, u32[]{:S(2)}, u32[]{:S(2)}) collective-permute-start(bf16[4,2,144,256]{3,2,1,0:T(8,128)(2,1)S(1)} %join.1.g_ref), channel_id=1, source_target_pairs={{0,6},{1,7},{2,0},{3,1},{4,2},{5,3},{6,4},{7,5},{8,14},{9,15},{10,... | collective-permute-start | bytes 1769480 | tf_op jit(solution)/shard_map/ppermute | solution.py:66
  98.5 2.0 %collective-permute-start.17 = (bf16[4,2,144,256]{3,2,1,0:T(8,128)(2,1)S(1)}, bf16[4,2,144,256]{3,2,1,0:T(8,128)(2,1)S(1)}, u32[]{:S(2)}, u32[]{:S(2)}) collective-permute-start(bf16[4,2,144,256]{3,2,1,0:T(8,128)(2,1)S(1)} %join.1.g_ref), channel_id=1, source_target_pairs={{0,2},{1,3},{2,4},{3,5},{4,6},{5,7},{6,0},{7,1},{8,10},{9,11},{10,... | collective-permute-start | bytes 1769480 | tf_op jit(solution)/shard_map/ppermute | solution.py:66
  100.5 1.6 %old.1 = (f32[1152,1024]{1,0:T(8,128)S(1)}, f32[1152,1024]{1,0:T(8,128)S(1)}) custom-call(s32[4,1152]{1,0:T(4,128)S(1)} %bitcast.6, s32[4,1152]{1,0:T(4,128)S(1)} %bitcast.7, bf16[1152,1024]{1,0:T(8,128)(2,1)S(1)} %copy-done.1, bf16[1152,1024]{1,0:T(8,128)(2,1)S(1)} %copy-done.2), custom_call_target="tpu_custom_call" | custom-call | flops 4718592 | bytes 14680064 | tf_op jit(solution)/shard_map/old/pallas_call | solution.py:284
  102.1 4.4 %near.1 = (f32[384,1024]{1,0:T(8,128)S(1)}, f32[384,1]{1,0:T(8,128)S(1)}, f32[384,2304]{1,0:T(8,128)S(1)}) custom-call(s32[1]{0:T(128)} %bitcast.where, bf16[384,2304]{1,0:T(8,128)(2,1)S(1)} %get-tuple-element.40.mine, bf16[384,2304]{1,0:T(8,128)(2,1)S(1)} %get-tuple-element.41.theirs, bf16[384,4608]{1,0:T(8,128)(2,1)S(1)} %get-tuple-element.37.x, ...), custom_call_target="tpu_custom_call" | custom-call | flops 3623878656 | bytes 18874368 | tf_op jit(solution)/shard_map/near/pallas_call | solution.py:451
  106.5 2.5 %adam_own.1 = (f32[1152,1024]{1,0:T(8,128)}, bf16[1152,1024]{1,0:T(8,128)(2,1)}, bf16[1152,1024]{1,0:T(8,128)(2,1)}, f32[1152,128]{1,0:T(8,128)S(1)}) custom-call(s32[1]{0:T(128)} %bitcast.where, bf16[4,2,144,256]{3,2,1,0:T(8,128)(2,1)S(1)} %join.1.g_ref, f32[1152,1024]{1,0:T(8,128)S(1)} %get-tuple-element.56.m_old.refs_3_, ...), custom_call_target="tpu_custom_call" | custom-call | flops 5898240 | bytes 4194304 | tf_op jit(solution)/shard_map/adam_own/pallas_call | solution.py:334
  109.0 5.7 %collective-permute-done.18.refs_1_ = bf16[4,2,144,256]{3,2,1,0:T(8,128)(2,1)S(1)} collective-permute-done((bf16[4,2,144,256]{3,2,1,0:T(8,128)(2,1)S(1)}, bf16[4,2,144,256]{3,2,1,0:T(8,128)(2,1)S(1)}, u32[]{:S(2)}, u32[]{:S(2)}) %collective-permute-start.18) | collective-permute-done | bytes 589856 | tf_op jit(solution)/shard_map/ppermute | solution.py:66
  114.7 7.4 %adam_more.1 = (f32[1152,1024]{1,0:T(8,128)}, bf16[1152,1024]{1,0:T(8,128)(2,1)}, bf16[1152,1024]{1,0:T(8,128)(2,1)}, f32[4,1152]{1,0:T(4,128)}, f32[4,1152]{1,0:T(4,128)}) custom-call(s32[1]{0:T(128)} %bitcast.where, bf16[4,2,144,256]{3,2,1,0:T(8,128)(2,1)S(1)} %collective-permute-done.17.refs_0_, ...), custom_call_target="tpu_custom_call", output_to_operand_aliasing={{0}: (7, {}), {1}: (8, {}), {2}: (9, {})} | custom-call | flops 17694720 | bytes 12582912 | tf_op jit(solution)/shard_map/adam_more/pallas_call | solution.py:398
  122.1 3.1 %keys.1 = bf16[384,1024]{1,0:T(8,128)(2,1)} custom-call(s32[1]{0:T(128)} %bitcast.where, bf16[384,2304]{1,0:T(8,128)(2,1)S(1)} %get-tuple-element.40.mine, bf16[384,2304]{1,0:T(8,128)(2,1)S(1)} %get-tuple-element.41.theirs, f32[384,1024]{1,0:T(8,128)S(1)} %get-tuple-element.42.near, bf16[1152,1024]{1,0:T(8,128)(2,1)S(1)} %collective-permute-done.1.far, ...), custom_call_target="tpu_custom_call" | custom-call | flops 1811939328 | bytes 10485760 | tf_op jit(solution)/shard_map/keys/pallas_call | solution.py:473
  125.3 5.6 %back.1 = bf16[384,4608]{1,0:T(8,128)(2,1)} custom-call(s32[1]{0:T(128)} %bitcast.where, bf16[384,4608]{1,0:T(8,128)(2,1)S(1)} %get-tuple-element.37.x, bf16[384,1024]{1,0:T(8,128)(2,1)S(1)} %copy-done, f32[384,1]{1,0:T(8,128)S(1)} %get-tuple-element.38.inv.inv_ref, f32[36,128]{1,0:T(8,128)S(1)} %get-tuple-element.39.gain, ...), custom_call_target="tpu_custom_call" | custom-call | flops 1811939328 | bytes 16777216 | tf_op jit(solution)/shard_map/back/pallas_call | solution.py:502
  (35 shorter events, 6.3 us)
Async XLA Ops:
  0.6 6.1 %copy-start = (bf16[384,1024]{1,0:T(8,128)(2,1)S(1)}, bf16[384,1024]{1,0:T(8,128)(2,1)}, u32[]{:S(2)}) copy-start(bf16[384,1024]{1,0:T(8,128)(2,1)} %refs_2_.3) | copy-start | bytes 2359300
  0.6 53.5 %collective-permute-start.1 = (bf16[1152,1024]{1,0:T(8,128)(2,1)}, bf16[1152,1024]{1,0:T(8,128)(2,1)S(1)}, u32[]{:S(2)}, u32[]{:S(2)}) collective-permute-start(bf16[1152,1024]{1,0:T(8,128)(2,1)} %own.1), channel_id=1, source_target_pairs={{0,65},{1,64},{2,67},{3,66},{4,69},{5,68},{6,71},{7,70},{8,73},{9,... | collective-permute-start | bytes 7077896 | tf_op jit(solution)/shard_map/ppermute | solution.py:66
  2.6 4.6 %copy-start.5 = (bf16[1152,1024]{1,0:T(8,128)(2,1)S(1)}, bf16[1152,1024]{1,0:T(8,128)(2,1)}, u32[]{:S(2)}) copy-start(bf16[1152,1024]{1,0:T(8,128)(2,1)} %own.1) | copy-start | bytes 7077892
  6.6 4.9 %collective-permute-start.3 = (bf16[384,2304]{1,0:T(8,128)(2,1)S(1)}, bf16[384,2304]{1,0:T(8,128)(2,1)S(1)}, u32[]{:S(2)}, u32[]{:S(2)}) collective-permute-start(bf16[384,2304]{1,0:T(8,128)(2,1)S(1)} %get-tuple-element.41.theirs), channel_id=1, source_target_pairs={{0,32},{1,33},{2,34},{3,35},{4,36},{5,37},{6,38},{7,39},{8,40},{9,... | collective-permute-start | bytes 5308424 | tf_op jit(solution)/shard_map/ppermute | solution.py:66
  6.7 4.8 %collective-permute-start.4 = (bf16[384,1024]{1,0:T(8,128)(2,1)S(1)}, bf16[384,1024]{1,0:T(8,128)(2,1)S(1)}, u32[]{:S(2)}, u32[]{:S(2)}) collective-permute-start(bf16[384,1024]{1,0:T(8,128)(2,1)S(1)} %copy-done), channel_id=1, source_target_pairs={{0,32},{1,33},{2,34},{3,35},{4,36},{5,37},{6,38},{7,39},{8,40},{9,... | collective-permute-start | bytes 2359304 | tf_op jit(solution)/shard_map/ppermute | solution.py:66
  7.2 94.9 %collective-permute-start = (bf16[1152,1024]{1,0:T(8,128)(2,1)S(1)}, bf16[1152,1024]{1,0:T(8,128)(2,1)S(1)}, u32[]{:S(2)}, u32[]{:S(2)}) collective-permute-start(bf16[1152,1024]{1,0:T(8,128)(2,1)S(1)} %copy-done.5), channel_id=1, source_target_pairs={{0,32},{1,33},{2,34},{3,35},{4,36},{5,37},{6,38},{7,39},{8,40},{9,... | collective-permute-start | bytes 7077896 | tf_op jit(solution)/shard_map/ppermute | solution.py:66
  13.0 42.5 %collective-permute-start.7 = (bf16[4,2,2,144,256]{4,3,2,1,0:T(8,128)(2,1)S(1)}, bf16[4,2,2,144,256]{4,3,2,1,0:T(8,128)(2,1)S(1)}, u32[]{:S(2)}, u32[]{:S(2)}) collective-permute-start(bf16[4,2,2,144,256]{4,3,2,1,0:T(8,128)(2,1)S(1)} %get-tuple-element.49), channel_id=1, source_target_pairs={{0,4},{1,5},{2,6},{3,7},{4,0},{5,1},{6,2},{7,3},{8,12},{9,13},{10,... | collective-permute-start | bytes 3538952 | tf_op jit(solution)/shard_map/ppermute | solution.py:66
  16.2 39.3 %collective-permute-start.5 = (bf16[4,2,2,144,256]{4,3,2,1,0:T(8,128)(2,1)S(1)}, bf16[4,2,2,144,256]{4,3,2,1,0:T(8,128)(2,1)S(1)}, u32[]{:S(2)}, u32[]{:S(2)}) collective-permute-start(bf16[4,2,2,144,256]{4,3,2,1,0:T(8,128)(2,1)S(1)} %get-tuple-element.47), channel_id=1, source_target_pairs={{0,2},{1,3},{2,4},{3,5},{4,6},{5,7},{6,0},{7,1},{8,10},{9,11},{10,... | collective-permute-start | bytes 3538952 | tf_op jit(solution)/shard_map/ppermute | solution.py:66
  18.3 37.2 %collective-permute-start.6 = (bf16[4,2,2,144,256]{4,3,2,1,0:T(8,128)(2,1)S(1)}, bf16[4,2,2,144,256]{4,3,2,1,0:T(8,128)(2,1)S(1)}, u32[]{:S(2)}, u32[]{:S(2)}) collective-permute-start(bf16[4,2,2,144,256]{4,3,2,1,0:T(8,128)(2,1)S(1)} %get-tuple-element.48), channel_id=1, source_target_pairs={{0,6},{1,7},{2,0},{3,1},{4,2},{5,3},{6,4},{7,5},{8,14},{9,15},{10,... | collective-permute-start | bytes 3538952 | tf_op jit(solution)/shard_map/ppermute | solution.py:66
  54.1 68.1 %collective-permute-start.2 = (bf16[1152,1024]{1,0:T(8,128)(2,1)S(1)}, bf16[1152,1024]{1,0:T(8,128)(2,1)S(1)}, u32[]{:S(2)}, u32[]{:S(2)}) collective-permute-start(bf16[1152,1024]{1,0:T(8,128)(2,1)S(1)} %collective-permute-done.1.far), channel_id=1, source_target_pairs={{0,32},{1,33},{2,34},{3,35},{4,36},{5,37},{6,38},{7,39},{8,40},{9,... | collective-permute-start | bytes 7077896 | tf_op jit(solution)/shard_map/ppermute | solution.py:66
  55.5 45.0 %copy-start.2 = (bf16[1152,1024]{1,0:T(8,128)(2,1)S(1)}, bf16[1152,1024]{1,0:T(8,128)(2,1)}, u32[]{:S(2)}) copy-start(bf16[1152,1024]{1,0:T(8,128)(2,1)} %vc_ref.1) | copy-start | bytes 7077892
  56.0 44.5 %copy-start.1 = (bf16[1152,1024]{1,0:T(8,128)(2,1)S(1)}, bf16[1152,1024]{1,0:T(8,128)(2,1)}, u32[]{:S(2)}) copy-start(bf16[1152,1024]{1,0:T(8,128)(2,1)} %mc_ref.1) | copy-start | bytes 7077892
  56.0 44.4 %copy-start.3 = (s32[1152,4]{0,1:T(4,128)S(1)}, s32[1152,4]{0,1:T(4,128)}, u32[]{:S(2)}) copy-start(s32[1152,4]{0,1:T(4,128)} %param.13) | copy-start | bytes 55300
  56.1 44.4 %copy-start.4 = (s32[1152,4]{0,1:T(4,128)S(1)}, s32[1152,4]{0,1:T(4,128)}, u32[]{:S(2)}) copy-start(s32[1152,4]{0,1:T(4,128)} %param.15) | copy-start | bytes 55300
  56.1 8.0 %collective-permute-start.8 = (bf16[2,2,144,256]{3,2,1,0:T(8,128)(2,1)S(1)}, bf16[2,2,144,256]{3,2,1,0:T(8,128)(2,1)S(1)}, u32[]{:S(2)}, u32[]{:S(2)}) collective-permute-start(bf16[2,2,144,256]{3,2,1,0:T(8,128)(2,1)S(1)} %get-tuple-element.51), channel_id=1, source_target_pairs={{0,8},{1,9},{2,10},{3,11},{4,12},{5,13},{6,14},{7,15},{8,16},{9,17... | collective-permute-start | bytes 884744 | tf_op jit(solution)/shard_map/ppermute | solution.py:66
  57.7 6.7 %collective-permute-start.9 = (bf16[2,2,144,256]{3,2,1,0:T(8,128)(2,1)S(1)}, bf16[2,2,144,256]{3,2,1,0:T(8,128)(2,1)S(1)}, u32[]{:S(2)}, u32[]{:S(2)}) collective-permute-start(bf16[2,2,144,256]{3,2,1,0:T(8,128)(2,1)S(1)} %get-tuple-element.52), channel_id=1, source_target_pairs={{0,24},{1,25},{2,26},{3,27},{4,28},{5,29},{6,30},{7,31},{8,0},{9,1... | collective-permute-start | bytes 884744 | tf_op jit(solution)/shard_map/ppermute | solution.py:66
  59.4 9.1 %collective-permute-start.10 = (bf16[2,2,144,256]{3,2,1,0:T(8,128)(2,1)S(1)}, bf16[2,2,144,256]{3,2,1,0:T(8,128)(2,1)S(1)}, u32[]{:S(2)}, u32[]{:S(2)}) collective-permute-start(bf16[2,2,144,256]{3,2,1,0:T(8,128)(2,1)S(1)} %get-tuple-element.53), channel_id=1, source_target_pairs={{0,16},{1,17},{2,18},{3,19},{4,20},{5,21},{6,22},{7,23},{8,24},{9,... | collective-permute-start | bytes 884744 | tf_op jit(solution)/shard_map/ppermute | solution.py:66
  68.6 6.7 %collective-permute-start.11 = (bf16[2,144,256]{2,1,0:T(8,128)(2,1)S(1)}, bf16[2,144,256]{2,1,0:T(8,128)(2,1)S(1)}, u32[]{:S(2)}, u32[]{:S(2)}) collective-permute-start(bf16[2,144,256]{2,1,0:T(8,128)(2,1)S(1)} %get-tuple-element.54.own), channel_id=1, source_target_pairs={{0,1},{1,0},{2,3},{3,2},{4,5},{5,4},{6,7},{7,6},{8,9},{9,8},{10,11... | collective-permute-start | bytes 442376 | tf_op jit(solution)/shard_map/ppermute | solution.py:66
  70.9 6.7 %collective-permute-start.13 = (bf16[2,144,256]{2,1,0:T(8,128)(2,1)S(1)}, bf16[2,144,256]{2,1,0:T(8,128)(2,1)S(1)}, u32[]{:S(2)}, u32[]{:S(2)}) collective-permute-start(bf16[2,144,256]{2,1,0:T(8,128)(2,1)S(1)} %get-tuple-element.55), channel_id=1, source_target_pairs={{0,64},{1,65},{2,66},{3,67},{4,68},{5,69},{6,70},{7,71},{8,72},{9,... | collective-permute-start | bytes 442376 | tf_op jit(solution)/shard_map/ppermute | solution.py:66
  73.0 6.2 %collective-permute-start.12 = (bf16[2,144,256]{2,1,0:T(8,128)(2,1)S(1)}, bf16[2,144,256]{2,1,0:T(8,128)(2,1)S(1)}, u32[]{:S(2)}, u32[]{:S(2)}) collective-permute-start(bf16[2,144,256]{2,1,0:T(8,128)(2,1)S(1)} %get-tuple-element.55), channel_id=1, source_target_pairs={{0,65},{1,64},{2,67},{3,66},{4,69},{5,68},{6,71},{7,70},{8,73},{9,... | collective-permute-start | bytes 442376 | tf_op jit(solution)/shard_map/ppermute | solution.py:66
  79.3 6.7 %collective-permute-start.16 = (bf16[2,144,256]{2,1,0:T(8,128)(2,1)S(1)}, bf16[2,144,256]{2,1,0:T(8,128)(2,1)S(1)}, u32[]{:S(2)}, u32[]{:S(2)}) collective-permute-start(bf16[2,144,256]{2,1,0:T(8,128)(2,1)S(1)} %total.1.refs_0_), channel_id=1, source_target_pairs={{0,16},{1,17},{2,18},{3,19},{4,20},{5,21},{6,22},{7,23},{8,24},{9,... | collective-permute-start | bytes 442376 | tf_op jit(solution)/shard_map/ppermute | solution.py:66
  82.2 5.2 %collective-permute-start.15 = (bf16[2,144,256]{2,1,0:T(8,128)(2,1)S(1)}, bf16[2,144,256]{2,1,0:T(8,128)(2,1)S(1)}, u32[]{:S(2)}, u32[]{:S(2)}) collective-permute-start(bf16[2,144,256]{2,1,0:T(8,128)(2,1)S(1)} %total.1.refs_0_), channel_id=1, source_target_pairs={{0,24},{1,25},{2,26},{3,27},{4,28},{5,29},{6,30},{7,31},{8,0},{9,1... | collective-permute-start | bytes 442376 | tf_op jit(solution)/shard_map/ppermute | solution.py:66
  83.4 6.4 %collective-permute-start.14 = (bf16[2,144,256]{2,1,0:T(8,128)(2,1)S(1)}, bf16[2,144,256]{2,1,0:T(8,128)(2,1)S(1)}, u32[]{:S(2)}, u32[]{:S(2)}) collective-permute-start(bf16[2,144,256]{2,1,0:T(8,128)(2,1)S(1)} %total.1.refs_0_), channel_id=1, source_target_pairs={{0,8},{1,9},{2,10},{3,11},{4,12},{5,13},{6,14},{7,15},{8,16},{9,17... | collective-permute-start | bytes 442376 | tf_op jit(solution)/shard_map/ppermute | solution.py:66
  89.8 19.1 %collective-permute-start.19 = (bf16[4,2,144,256]{3,2,1,0:T(8,128)(2,1)S(1)}, bf16[4,2,144,256]{3,2,1,0:T(8,128)(2,1)S(1)}, u32[]{:S(2)}, u32[]{:S(2)}) collective-permute-start(bf16[4,2,144,256]{3,2,1,0:T(8,128)(2,1)S(1)} %join.1.g_ref), channel_id=1, source_target_pairs={{0,4},{1,5},{2,6},{3,7},{4,0},{5,1},{6,2},{7,3},{8,12},{9,13},{10,... | collective-permute-start | bytes 1769480 | tf_op jit(solution)/shard_map/ppermute | solution.py:66
  92.1 22.6 %collective-permute-start.18 = (bf16[4,2,144,256]{3,2,1,0:T(8,128)(2,1)S(1)}, bf16[4,2,144,256]{3,2,1,0:T(8,128)(2,1)S(1)}, u32[]{:S(2)}, u32[]{:S(2)}) collective-permute-start(bf16[4,2,144,256]{3,2,1,0:T(8,128)(2,1)S(1)} %join.1.g_ref), channel_id=1, source_target_pairs={{0,6},{1,7},{2,0},{3,1},{4,2},{5,3},{6,4},{7,5},{8,14},{9,15},{10,... | collective-permute-start | bytes 1769480 | tf_op jit(solution)/shard_map/ppermute | solution.py:66
  98.5 16.2 %collective-permute-start.17 = (bf16[4,2,144,256]{3,2,1,0:T(8,128)(2,1)S(1)}, bf16[4,2,144,256]{3,2,1,0:T(8,128)(2,1)S(1)}, u32[]{:S(2)}, u32[]{:S(2)}) collective-permute-start(bf16[4,2,144,256]{3,2,1,0:T(8,128)(2,1)S(1)} %join.1.g_ref), channel_id=1, source_target_pairs={{0,2},{1,3},{2,4},{3,5},{4,6},{5,7},{6,0},{7,1},{8,10},{9,11},{10,... | collective-permute-start | bytes 1769480 | tf_op jit(solution)/shard_map/ppermute | solution.py:66
